TPU v7x, 32 devices: a whole 2x2x4 slice. The times are simulated.
32 devices in a mesh: node: 8 (over z, x), local: 4 (over y, core).
Axes of the slice: x: 2, y: 2, z: 4, core: 2. Of those that a mesh axis runs over, the one named last changes fastest.
Arguments:
- tokens: bfloat16 [2048, 2048], P('node'), may hold values from -6 to 6
- expert_ids: int32 [2048, 8], P('node'), may hold values from 0 to 31, as said below
- gate_scores: float32 [2048, 8], P('node'), may hold values from 0.02 to 0.5
- expert_gate: bfloat16 [32, 2048, 768], P(('node', 'local')), may hold values from -0.125 to 0.125
- expert_up: bfloat16 [32, 2048, 768], P(('node', 'local')), may hold values from -0.125 to 0.125
- expert_down: bfloat16 [32, 768, 2048], P(('node', 'local')), may hold values from -0.21875 to 0.21875
- shared_gate: bfloat16 [2048, 2048], P(None, 'local'), may hold values from -0.125 to 0.125
- shared_up: bfloat16 [2048, 2048], P(None, 'local'), may hold values from -0.125 to 0.125
- shared_down: bfloat16 [2048, 2048], P('local'), may hold values from -0.125 to 0.125
Outputs:
- moe_out: bfloat16 [2048, 2048], P(('node', 'local'))
Inputs may be any that keep to these rules, and one draw needn't show every extreme that they name: `expert_ids`: each token's 8 experts are distinct and lie in exactly 4 groups of 4 consecutive experts (group g is experts g * 4 to g * 4 + 3), two in each. Among the 256 tokens of one index of node, exactly 128 tokens pick experts in each group of 4 consecutive experts, no expert is picked by more than 128 tokens, and one expert is picked by exactly 128 of them in every such block.
All inputs are finite; a program needn't handle non-finite values.
Results may differ from a plain program's by a relative error of at most 0.015.
Values may be sent and summed in bfloat16 or wider, within the bound.
No kernel may reach another device: no remote copies, remote signals or barrier semaphores. Data moves between devices by JAX's collectives and lax.ppermute only.
A program may use at most 64 MiB of HBM per device.

v0:
```python
import functools

import jax
import jax.numpy as jnp
from jax import lax
from jax.experimental import pallas as pl
from jax.experimental.pallas import tpu as pltpu
from jax.sharding import PartitionSpec as P


E_NODE = 4
NEAR = 4
LANES = 128
VMEM_LIMIT = 24 * 1024 * 1024
F32 = jnp.float32
BF16 = jnp.bfloat16


def xor_node(x, k):
    count = lax.axis_size("node")
    return lax.ppermute(x, "node", [(i, i ^ k) for i in range(count)])


def xor_local(x, k):
    count = lax.axis_size("local")
    return lax.ppermute(x, "local", [(i, i ^ k) for i in range(count)])


def params():
    return pltpu.CompilerParams(vmem_limit_bytes=VMEM_LIMIT)


def cost(flops, nbytes, trans=0):
    return pl.CostEstimate(flops=int(flops), bytes_accessed=int(nbytes), transcendentals=int(trans))


SMEM = pl.BlockSpec(memory_space=pltpu.SMEM)
HBM = pl.BlockSpec(memory_space=pltpu.HBM)
VMEM = pl.BlockSpec(memory_space=pltpu.VMEM)


def column_blocks(width, block=512):
    return [(c, min(block, width - c)) for c in range(0, width, block)]


def route_kernel(pieces, node_count, s_ref, ids_hbm, score_hbm, tok_hbm, *refs):
    outs = refs[: len(pieces)]
    oh_ref, hot, rows, ids_ref, score_ref, tok_ref, sems = refs[len(pieces):]
    copies = [
        pltpu.make_async_copy(src, dst, sems.at[i])
        for i, (src, dst) in enumerate(((ids_hbm, ids_ref), (score_hbm, score_ref), (tok_hbm, tok_ref)))
    ]
    for copy in copies:
        copy.start()
    copies[0].wait()
    copies[1].wait()
    tok_rows, width = tok_ref.shape
    picks = ids_ref.shape[0]
    experts = node_count * E_NODE
    node = s_ref[0]
    ids = ids_ref[...]
    group = lax.div(ids, jnp.int32(E_NODE)) ^ node
    score = score_ref[...]
    group_iota = lax.broadcasted_iota(jnp.int32, (node_count, tok_rows), 0)
    expert_iota = lax.broadcasted_iota(jnp.int32, (experts, tok_rows), 0)
    member = jnp.zeros((node_count, tok_rows), F32)
    weight = jnp.zeros((experts, tok_rows), F32)
    for j in range(picks):
        member = jnp.where(group[j : j + 1] == group_iota, 1.0, member)
        weight = weight + jnp.where(ids[j : j + 1] == expert_iota, score[j : j + 1], 0.0)
    row = lax.broadcasted_iota(jnp.int32, (tok_rows, tok_rows), 0)
    col = lax.broadcasted_iota(jnp.int32, (tok_rows, tok_rows), 1)
    upper = jnp.where(row <= col, 1.0, 0.0).astype(BF16)
    position = jnp.dot(member.astype(BF16), upper, preferred_element_type=F32) - 1.0
    position = jnp.where(member > 0.0, position, -1.0).astype(jnp.int32)
    offset = 0
    for k, base, count in pieces:
        first = 0 if base is None else s_ref[base] * count
        slot = lax.broadcasted_iota(jnp.int32, (count, tok_rows), 0) + first
        hot[offset : offset + count, :] = jnp.where(position[k : k + 1] == slot, 1.0, 0.0)
        offset += count
    one_hot = hot[...].astype(BF16)
    oh_ref[...] = one_hot
    high = weight.astype(BF16)
    low = (weight - high.astype(F32)).astype(BF16)
    extra = outs[0].shape[1] - width
    parts = [high, low]
    if extra > 2 * experts:
        parts.append(jnp.zeros((extra - 2 * experts, tok_rows), BF16))
    table = jnp.concatenate(parts, axis=0)
    copies[2].wait()
    for c, w in column_blocks(width) + [(width, extra)]:
        if c < width:
            rows[:, :w] = jnp.dot(one_hot, tok_ref[:, c : c + w], preferred_element_type=F32)
        else:
            rows[:, :w] = lax.dot_general(one_hot, table, (((1,), (1,)), ((), ())), preferred_element_type=F32)
        offset = 0
        for out, (_, _, count) in zip(outs, pieces):
            out[:, c : c + w] = rows[offset : offset + count, :w].astype(BF16)
            offset += count


def route(scalars, ids, scores, tokens, pieces, node_count):
    tok_rows, width = tokens.shape
    experts = node_count * E_NODE
    full = width + -(-2 * experts // LANES) * LANES
    total = sum(p[2] for p in pieces)
    res = pl.pallas_call(
        functools.partial(route_kernel, pieces, node_count),
        out_shape=[jax.ShapeDtypeStruct((p[2], full), BF16) for p in pieces]
        + [jax.ShapeDtypeStruct((total, tok_rows), BF16)],
        in_specs=[SMEM, HBM, HBM, HBM],
        out_specs=[VMEM] * (len(pieces) + 1),
        scratch_shapes=[
            pltpu.VMEM((total, tok_rows), F32),
            pltpu.VMEM((total, 512), F32),
            pltpu.VMEM(ids.shape, ids.dtype),
            pltpu.VMEM(scores.shape, scores.dtype),
            pltpu.VMEM(tokens.shape, tokens.dtype),
            pltpu.SemaphoreType.DMA((3,)),
        ],
        compiler_params=params(),
        cost_estimate=cost(2 * total * tok_rows * full, 2 * (tok_rows * width + total * full)),
        name="route",
    )(scalars, ids, scores, tokens)
    return res[:-1], res[-1]


def hidden_block(hidden):
    for size in (256, 128):
        if hidden % size == 0:
            return size
    return hidden


def ffn_kernel(counts, experts, keep_rows, s_ref, *refs):
    n = len(counts)
    xs = refs[:n]
    wg_ref, wu_ref, wd_ref = refs[n : n + 3]
    outs = refs[n + 3 : -2]
    x, wcol = refs[-2:]
    total, width = x.shape
    expert = s_ref[2]
    extra = xs[0].shape[1] - width
    lane = lax.broadcasted_iota(jnp.int32, (1, extra), 1)
    mask = jnp.where((lane == expert) | (lane == expert + experts), 1.0, 0.0)
    offset = 0
    for ref, count in zip(xs, counts):
        x[offset : offset + count, :] = ref[:, :width].astype(x.dtype)
        wcol[offset : offset + count, :] = jnp.sum(ref[:, width:].astype(F32) * mask, axis=1, keepdims=True)
        offset += count
    rows = x[...].astype(BF16)
    hidden = []
    for c, w in column_blocks(wg_ref.shape[2], 256):
        gate = jnp.dot(rows, wg_ref[0, :, c : c + w], preferred_element_type=F32)
        up = jnp.dot(rows, wu_ref[0, :, c : c + w], preferred_element_type=F32)
        hidden.append((jax.nn.silu(gate) * up).astype(BF16))
    hidden = jnp.concatenate(hidden, axis=1) if len(hidden) > 1 else hidden[0]
    scale = wcol[...]
    for c, w in column_blocks(width):
        part = jnp.dot(hidden, wd_ref[0, :, c : c + w], preferred_element_type=F32) * scale
        outs[0][:, c : c + w] = part[:keep_rows].astype(outs[0].dtype)
        if keep_rows < total:
            outs[1][:, c : c + w] = part[keep_rows:].astype(outs[1].dtype)


def ffn(scalars, xs, w_gate, w_up, w_down, experts, split):
    counts = [x.shape[0] for x in xs]
    total = sum(counts)
    width, hidden = w_gate.shape[1:]
    keep = total // 2 if split else total
    shapes = [jax.ShapeDtypeStruct((keep, width), F32 if split else BF16)]
    if split:
        shapes.append(jax.ShapeDtypeStruct((total - keep, width), BF16))
    packed = all(c % 16 == 0 for c in counts)
    return pl.pallas_call(
        functools.partial(ffn_kernel, counts, experts, keep),
        out_shape=shapes,
        in_specs=[SMEM] + [VMEM] * (len(xs) + 3),
        out_specs=[VMEM] * len(shapes),
        scratch_shapes=[
            pltpu.VMEM((total, width), BF16 if packed else F32),
            pltpu.VMEM((total, 1), F32),
        ],
        compiler_params=params(),
        cost_estimate=cost(6 * total * width * hidden, 6 * width * hidden + 6 * total * width, total * hidden),
    )(scalars, *xs, w_gate, w_up, w_down)


def shared_kernel(x_ref, wg_ref, wu_ref, wd_ref, eg_hbm, eu_hbm, ed_hbm, out_ref, eg_ref, eu_ref, ed_ref, sems):
    step = pl.program_id(0)
    staged = [
        pltpu.make_async_copy(src, dst, sems.at[i])
        for i, (src, dst) in enumerate(((eg_hbm, eg_ref), (eu_hbm, eu_ref), (ed_hbm, ed_ref)))
    ]

    @pl.when(step == 0)
    def _():
        for copy in staged:
            copy.start()

    rows = x_ref[...]
    gate = jnp.dot(rows, wg_ref[...], preferred_element_type=F32)
    up = jnp.dot(rows, wu_ref[...], preferred_element_type=F32)
    hidden = (jax.nn.silu(gate) * up).astype(BF16)
    for c, w in column_blocks(rows.shape[1]):
        part = jnp.dot(hidden, wd_ref[:, c : c + w], preferred_element_type=F32)

        @pl.when(step == 0)
        def _():
            out_ref[:, c : c + w] = part

        @pl.when(step > 0)
        def _():
            out_ref[:, c : c + w] += part

    @pl.when(step == pl.num_programs(0) - 1)
    def _():
        for copy in staged:
            copy.wait()


def shared(tokens, w_gate, w_up, w_down, staged):
    rows, width = tokens.shape
    hidden = w_gate.shape[1]
    block = hidden_block(hidden)
    return pl.pallas_call(
        shared_kernel,
        grid=(hidden // block,),
        out_shape=[jax.ShapeDtypeStruct((rows, width), F32)] + [jax.ShapeDtypeStruct(w.shape, w.dtype) for w in staged],
        in_specs=[
            pl.BlockSpec((rows, width), lambda f: (0, 0)),
            pl.BlockSpec((width, block), lambda f: (0, f)),
            pl.BlockSpec((width, block), lambda f: (0, f)),
            pl.BlockSpec((block, width), lambda f: (f, 0)),
            HBM,
            HBM,
            HBM,
        ],
        out_specs=[pl.BlockSpec((rows, width), lambda f: (0, 0)), VMEM, VMEM, VMEM],
        scratch_shapes=[pltpu.SemaphoreType.DMA((3,))],
        compiler_params=params(),
        cost_estimate=cost(
            6 * rows * width * hidden,
            6 * width * hidden + 6 * rows * width + sum(4 * w.size for w in staged),
            rows * hidden,
        ),
        name="shared",
    )(tokens, w_gate, w_up, w_down, *staged)


def combine_kernel(counts, order, s_ref, oh_ref, shared_ref, *refs):
    n = len(counts)
    parts = refs[:n]
    keep_ref, send_ref, slots, acc = refs[n:]
    tok_rows, width = shared_ref.shape
    offset = 0
    for ref, count in zip(parts, counts):
        slots[offset : offset + count, :] = ref[...].astype(slots.dtype)
        offset += count
    one_hot = oh_ref[...]
    for c, w in column_blocks(width):
        acc[:, c : c + w] = lax.dot_general(
            one_hot, slots[:, c : c + w].astype(BF16), (((0,), (0,)), ((), ())), preferred_element_type=F32
        )
    block = tok_rows // len(order)
    half = len(order) // 2
    for j, rel in enumerate(order):
        start = pl.multiple_of((s_ref[1] ^ rel) * block, block)
        value = acc[pl.ds(start, block), :] + shared_ref[pl.ds(start, block), :]
        if j < half:
            keep_ref[j * block : (j + 1) * block, :] = value
        else:
            send_ref[(j - half) * block : (j - half + 1) * block, :] = value.astype(BF16)


def combine(scalars, one_hot, shared_part, parts, order):
    counts = [p.shape[0] for p in parts]
    tok_rows, width = shared_part.shape
    total = sum(counts)
    packed = all(c % 16 == 0 for c in counts)
    return pl.pallas_call(
        functools.partial(combine_kernel, counts, order),
        out_shape=[
            jax.ShapeDtypeStruct((tok_rows // 2, width), F32),
            jax.ShapeDtypeStruct((tok_rows // 2, width), BF16),
        ],
        in_specs=[SMEM] + [VMEM] * (len(parts) + 2),
        out_specs=[VMEM, VMEM],
        scratch_shapes=[
            pltpu.VMEM((total, width), BF16 if packed else F32),
            pltpu.VMEM((tok_rows, width), F32),
        ],
        compiler_params=params(),
        cost_estimate=cost(2 * total * tok_rows * width, 2 * total * width + 7 * tok_rows * width),
        name="combine",
    )(scalars, one_hot, shared_part, *parts)


def fold(value, bits):
    for bit in bits:
        half = value.shape[0] // 2
        value = value[:half] + xor_local(value[half:].astype(BF16), bit).astype(F32)
    return value


def far_chunks(node_count):
    top = node_count // 2
    chunks = []
    while top >= NEAR:
        chunks.append(list(range(top, 2 * top)))
        top //= 2
    if len(chunks) == 1 and len(chunks[0]) > 1:
        ks = chunks[0]
        chunks = [ks[len(ks) // 2 :], ks[: len(ks) // 2]]
    return chunks


def local(tokens, expert_ids, gate_scores, expert_gate, expert_up, expert_down, shared_gate, shared_up, shared_down):
    node_count = lax.axis_size("node")
    local_count = lax.axis_size("local")
    experts = node_count * E_NODE
    tok_rows, _ = tokens.shape
    capacity = expert_ids.shape[1] * tok_rows // (2 * node_count)
    node = lax.axis_index("node")
    rank = lax.axis_index("local")
    own = node * E_NODE + rank // (local_count // E_NODE)
    scalars = jnp.stack([node, rank, own, rank % 2]).astype(jnp.int32)
    slow_bits = [1 << b for b in range(1, local_count.bit_length() - 1)]
    chunks = far_chunks(node_count)
    near = [k for k in range(1, NEAR)]
    pieces = [(k, 1, capacity // local_count) for ks in chunks for k in ks]
    pieces += [(k, 3, capacity // 2) for k in near] + [(0, None, capacity)]
    sends, one_hot = route(scalars, expert_ids.T, gate_scores.T, tokens, tuple(pieces), node_count)
    weights = (expert_gate, expert_up, expert_down)

    arrived = []
    index = 0
    for ks in chunks:
        got = []
        for k in ks:
            got.append(xor_node(sends[index], k))
            index += 1
        arrived.append(got)
    near_in = []
    for k in near:
        near_in.append(xor_node(sends[index], k))
        index += 1
    own_rows = sends[-1]

    shared_part, *weights = shared(tokens, shared_gate, shared_up, shared_down, weights)
    own_out = ffn(scalars, [own_rows], *weights, experts, False)[0]

    def gather(got):
        rows = [jnp.concatenate(got, axis=0) if len(got) > 1 else got[0]]
        for bit in slow_bits:
            rows = rows + [xor_local(r, bit) for r in rows]
        return rows + [xor_local(r, 1) for r in rows]

    def experts_of(rows):
        keep, send = ffn(scalars, rows, *weights, experts, True)
        return keep + xor_local(send, 1).astype(F32)

    near_rows = near_in + [xor_local(r, 1) for r in near_in]
    near_sum = experts_of(near_rows).astype(BF16)
    count = near_sum.shape[0] // len(near)
    near_back = []
    for i, k in enumerate(near):
        near_back.append(xor_node(near_sum[i * count : (i + 1) * count], k))
    returned = []
    for ks, got in zip(chunks, arrived):
        value = experts_of(gather(got))
        value = fold(value, slow_bits[::-1]).astype(BF16)
        count = value.shape[0] // len(ks)
        for i, k in enumerate(ks):
            returned.append(xor_node(value[i * count : (i + 1) * count], k))

    order = [0]
    for bit in slow_bits:
        order = order + [i ^ bit for i in order]
    order = order + [i ^ 1 for i in order]
    keep, send = combine(scalars, one_hot, shared_part, returned + near_back + [own_out], tuple(order))
    value = keep + xor_local(send, 1).astype(F32)
    return fold(value, slow_bits[::-1]).astype(BF16)


def solution(mesh):
    return shard(mesh)


def shard(mesh):
    return jax.shard_map(
        local,
        mesh=mesh,
        in_specs=(
            P("node", None),
            P("node", None),
            P("node", None),
            P(("node", "local"), None, None),
            P(("node", "local"), None, None),
            P(("node", "local"), None, None),
            P(None, "local"),
            P(None, "local"),
            P("local", None),
        ),
        out_specs=P(("node", "local"), None),
        check_vma=False,
    )
```

profile of v0, /device:TPU:0, one launch (start us, length us, event | category | flops | bytes accessed | tf_op | source)
XLA Modules:
  0.0 119.2 jit_solution(6085124697510848124)
XLA Ops:
  2.8 1.6 %route.1 = (bf16[32,2176]{1,0:T(8,128)(2,1)S(1)}, bf16[32,2176]{1,0:T(8,128)(2,1)S(1)}, bf16[32,2176]{1,0:T(8,128)(2,1)S(1)}, bf16[32,2176]{1,0:T(8,128)(2,1)S(1...) custom-call(s32[4]{0:T(128)S(1)} %pad_add_fusion.s_ref, ...), custom_call_target="tpu_custom_call" | custom-call | flops 499122176 | bytes 2998272 | tf_op jit(solution)/shard_map/route/pallas_call | solution.py:108
  4.5 5.1 %collective-permute-start = (bf16[32,2176]{1,0:T(8,128)(2,1)S(1)}, bf16[32,2176]{1,0:T(8,128)(2,1)S(1)}, u32[]{:S(2)}, u32[]{:S(2)}) collective-permute-start(bf16[32,2176]{1,0:T(8,128)(2,1)S(1)} %get-tuple-element.28), channel_id=1, source_target_pairs={{0,24},{4,28},{8,16},{12,20},{16,8},{20,12},{24,0},{28,4},{1,25},{... | collective-permute-start | bytes 417800 | tf_op jit(solution)/shard_map/ppermute | solution.py:21
  11.5 2.0 %collective-permute-start.10 = (bf16[32,2176]{1,0:T(8,128)(2,1)S(1)}, bf16[32,2176]{1,0:T(8,128)(2,1)S(1)}, u32[]{:S(2)}, u32[]{:S(2)}) collective-permute-start(bf16[32,2176]{1,0:T(8,128)(2,1)S(1)} %get-tuple-element.36), channel_id=1, source_target_pairs={{0,20},{4,16},{8,28},{12,24},{16,4},{20,0},{24,12},{28,8},{1,21},{... | collective-permute-start | bytes 417800 | tf_op jit(solution)/shard_map/ppermute | solution.py:21
  13.5 1.6 %collective-permute-start.18 = (bf16[64,2176]{1,0:T(8,128)(2,1)S(1)}, bf16[64,2176]{1,0:T(8,128)(2,1)S(1)}, u32[]{:S(2)}, u32[]{:S(2)}) collective-permute-start(bf16[64,2176]{1,0:T(8,128)(2,1)S(1)} %get-tuple-element.39), channel_id=1, source_target_pairs={{0,4},{4,0},{8,12},{12,8},{16,20},{20,16},{24,28},{28,24},{1,5},{5... | collective-permute-start | bytes 835592 | tf_op jit(solution)/shard_map/ppermute | solution.py:21
  15.2 10.7 %collective-permute-start.19 = (bf16[64,2176]{1,0:T(8,128)(2,1)S(1)}, bf16[64,2176]{1,0:T(8,128)(2,1)S(1)}, u32[]{:S(2)}, u32[]{:S(2)}) collective-permute-start(bf16[64,2176]{1,0:T(8,128)(2,1)S(1)} %get-tuple-element.40), channel_id=1, source_target_pairs={{0,8},{4,12},{8,0},{12,4},{16,24},{20,28},{24,16},{28,20},{1,9},{5... | collective-permute-start | bytes 835592 | tf_op jit(solution)/shard_map/ppermute | solution.py:21
  25.9 1.6 %collective-permute-start.2 = (bf16[64,2176]{1,0:T(8,128)(2,1)S(1)}, bf16[64,2176]{1,0:T(8,128)(2,1)S(1)}, u32[]{:S(2)}, u32[]{:S(2)}) collective-permute-start(bf16[64,2176]{1,0:T(8,128)(2,1)S(1)} %constant_dynamic-update-slice_fusion.refs_0_), channel_id=1, source_target_pairs={{0,2},{1,3},{2,0},{3,1},{4,6},{5,7},{6,4},{7,5},{8,10},{9,11},{10,... | collective-permute-start | bytes 835592 | tf_op jit(solution)/shard_map/ppermute | solution.py:26
  27.5 3.9 %collective-permute-done.9 = bf16[32,2176]{1,0:T(8,128)(2,1)S(1)} collective-permute-done((bf16[32,2176]{1,0:T(8,128)(2,1)S(1)}, bf16[32,2176]{1,0:T(8,128)(2,1)S(1)}, u32[]{:S(2)}, u32[]{:S(2)}) %collective-permute-start.9) | collective-permute-done | bytes 139296 | tf_op jit(solution)/shard_map/ppermute | solution.py:21
  31.4 3.0 %collective-permute-done.10 = bf16[32,2176]{1,0:T(8,128)(2,1)S(1)} collective-permute-done((bf16[32,2176]{1,0:T(8,128)(2,1)S(1)}, bf16[32,2176]{1,0:T(8,128)(2,1)S(1)}, u32[]{:S(2)}, u32[]{:S(2)}) %collective-permute-start.10) | collective-permute-done | bytes 139296 | tf_op jit(solution)/shard_map/ppermute | solution.py:21
  34.4 1.6 %collective-permute-start.11 = (bf16[64,2176]{1,0:T(8,128)(2,1)S(1)}, bf16[64,2176]{1,0:T(8,128)(2,1)S(1)}, u32[]{:S(2)}, u32[]{:S(2)}) collective-permute-start(bf16[64,2176]{1,0:T(8,128)(2,1)S(1)} %constant_dynamic-update-slice_fusion.2.refs_0_), channel_id=1, source_target_pairs={{0,2},{1,3},{2,0},{3,1},{4,6},{5,7},{6,4},{7,5},{8,10},{9,11},{10,... | collective-permute-start | bytes 835592 | tf_op jit(solution)/shard_map/ppermute | solution.py:26
  36.6 5.6 %collective-permute-done.11.refs_1_ = bf16[64,2176]{1,0:T(8,128)(2,1)S(1)} collective-permute-done((bf16[64,2176]{1,0:T(8,128)(2,1)S(1)}, bf16[64,2176]{1,0:T(8,128)(2,1)S(1)}, u32[]{:S(2)}, u32[]{:S(2)}) %collective-permute-start.11) | collective-permute-done | bytes 278560 | tf_op jit(solution)/shard_map/ppermute | solution.py:26
  42.1 1.9 %copy-done = bf16[1,2048,768]{2,1,0:T(8,128)(2,1)S(1)} copy-done((bf16[1,2048,768]{2,1,0:T(8,128)(2,1)S(1)}, bf16[1,2048,768]{2,1,0:T(8,128)(2,1)}, u32[]{:S(2)}) %copy-start) | copy-done | bytes 3145752
  44.0 1.9 %copy-done.1 = bf16[1,2048,768]{2,1,0:T(8,128)(2,1)S(1)} copy-done((bf16[1,2048,768]{2,1,0:T(8,128)(2,1)S(1)}, bf16[1,2048,768]{2,1,0:T(8,128)(2,1)}, u32[]{:S(2)}) %copy-start.1) | copy-done | bytes 3145752
  45.9 1.9 %copy-done.2 = bf16[1,768,2048]{2,1,0:T(8,128)(2,1)S(1)} copy-done((bf16[1,768,2048]{2,1,0:T(8,128)(2,1)S(1)}, bf16[1,768,2048]{2,1,0:T(8,128)(2,1)}, u32[]{:S(2)}) %copy-start.2) | copy-done | bytes 3145752
  47.8 1.6 %copy-done.4 = bf16[2048,512]{1,0:T(8,128)(2,1)S(1)} copy-done((bf16[2048,512]{1,0:T(8,128)(2,1)S(1)}, bf16[2048,512]{1,0:T(8,128)(2,1)}, u32[]{:S(2)}) %copy-start.4) | copy-done | bytes 2097176
  49.4 1.6 %copy-done.5 = bf16[512,2048]{1,0:T(8,128)(2,1)S(1)} copy-done((bf16[512,2048]{1,0:T(8,128)(2,1)S(1)}, bf16[512,2048]{1,0:T(8,128)(2,1)}, u32[]{:S(2)}) %copy-start.5) | copy-done | bytes 2097176
  52.2 4.5 %shared.1 = (f32[256,2048]{1,0:T(8,128)S(1)}, bf16[1,2048,768]{2,1,0:T(8,128)(2,1)S(1)}, bf16[1,2048,768]{2,1,0:T(8,128)(2,1)S(1)}, bf16[1,768,2048]{2,1,0:T(8,128)(2,1)S(1)}) custom-call(bf16[256,2048]{1,0:T(8,128)(2,1)S(1)} %copy-done.7, bf16[2048,512]{1,0:T(8,128)(2,1)S(1)} %copy-done.3, bf16[2048,512]{1,0:T(8,128)(2,1)S(1)} %copy-done.4, ...), custom_call_target="tpu_custom_call" | custom-call | flops 1610612736 | bytes 28311552 | tf_op jit(solution)/shard_map/shared/pallas_call | solution.py:227
  57.8 3.2 %shard_map.91 = (f32[128,2048]{1,0:T(8,128)S(1)}, bf16[128,2048]{1,0:T(8,128)(2,1)S(1)}) custom-call(s32[4]{0:T(128)S(1)} %pad_add_fusion.s_ref, bf16[64,2176]{1,0:T(8,128)(2,1)S(1)} %constant_dynamic-update-slice_fusion.refs_0_, bf16[64,2176]{1,0:T(8,128)(2,1)S(1)} %collective-permute-done.2.refs_1_, bf16[64,2176]{1,0:T(8,128)(2,1)S(1)} %collective-permute-done.3.refs_2_, ...), custom_call_target="tpu_custom_call" | custom-call | flops 2415919104 | bytes 12582912 | tf_op jit(solution)/shard_map/pallas_call | solution.py:176
  61.1 3.2 %shard_map.92 = (f32[128,2048]{1,0:T(8,128)S(1)}, bf16[128,2048]{1,0:T(8,128)(2,1)S(1)}) custom-call(s32[4]{0:T(128)S(1)} %pad_add_fusion.s_ref, bf16[64,2176]{1,0:T(8,128)(2,1)S(1)} %constant_dynamic-update-slice_fusion.2.refs_0_, bf16[64,2176]{1,0:T(8,128)(2,1)S(1)} %collective-permute-done.11.refs_1_, ...), custom_call_target="tpu_custom_call" | custom-call | flops 2415919104 | bytes 12582912 | tf_op jit(solution)/shard_map/pallas_call | solution.py:176
  64.8 4.4 %shard_map.93 = (f32[192,2048]{1,0:T(8,128)S(1)}, bf16[192,2048]{1,0:T(8,128)(2,1)S(1)}) custom-call(s32[4]{0:T(128)S(1)} %pad_add_fusion.s_ref, bf16[64,2176]{1,0:T(8,128)(2,1)S(1)} %collective-permute-done.18.refs_0_, bf16[64,2176]{1,0:T(8,128)(2,1)S(1)} %collective-permute-done.19.refs_1_, bf16[64,2176]{1,0:T(8,128)(2,1)S(1)} %collective-permute-done.20.refs_2_, ...), custom_call_target="tpu_custom_call" | custom-call | flops 3623878656 | bytes 14155776 | tf_op jit(solution)/shard_map/pallas_call | solution.py:176
  69.5 1.6 %collective-permute-start.6 = (bf16[64,2048]{1,0:T(8,128)(2,1)S(1)}, bf16[64,2048]{1,0:T(8,128)(2,1)S(1)}, u32[]{:S(2)}, u32[]{:S(2)}) collective-permute-start(bf16[64,2048]{1,0:T(8,128)(2,1)S(1)} %slice.82), channel_id=1, source_target_pairs={{0,2},{1,3},{2,0},{3,1},{4,6},{5,7},{6,4},{7,5},{8,10},{9,11},{10,... | collective-permute-start | bytes 786440 | tf_op jit(solution)/shard_map/ppermute | solution.py:26
  73.3 2.5 %collective-permute-start.27 = (bf16[64,2048]{1,0:T(8,128)(2,1)S(1)}, bf16[64,2048]{1,0:T(8,128)(2,1)S(1)}, u32[]{:S(2)}, u32[]{:S(2)}) collective-permute-start(bf16[64,2048]{1,0:T(8,128)(2,1)S(1)} %get-tuple-element.47), channel_id=1, source_target_pairs={{0,12},{4,8},{8,4},{12,0},{16,28},{20,24},{24,20},{28,16},{1,13},{... | collective-permute-start | bytes 786440 | tf_op jit(solution)/shard_map/ppermute | solution.py:21
  75.7 3.0 %collective-permute-done.6 = bf16[64,2048]{1,0:T(8,128)(2,1)S(1)} collective-permute-done((bf16[64,2048]{1,0:T(8,128)(2,1)S(1)}, bf16[64,2048]{1,0:T(8,128)(2,1)S(1)}, u32[]{:S(2)}, u32[]{:S(2)}) %collective-permute-start.6) | collective-permute-done | bytes 262176 | tf_op jit(solution)/shard_map/ppermute | solution.py:26
  78.9 2.3 %collective-permute-start.7 = (bf16[32,2048]{1,0:T(8,128)(2,1)S(1)}, bf16[32,2048]{1,0:T(8,128)(2,1)S(1)}, u32[]{:S(2)}, u32[]{:S(2)}) collective-permute-start(bf16[32,2048]{1,0:T(8,128)(2,1)S(1)} %get-tuple-element.53), channel_id=1, source_target_pairs={{0,24},{4,28},{8,16},{12,20},{16,8},{20,12},{24,0},{28,4},{1,25},{... | collective-permute-start | bytes 393224 | tf_op jit(solution)/shard_map/ppermute | solution.py:21
  81.2 2.7 %collective-permute-done.15 = bf16[64,2048]{1,0:T(8,128)(2,1)S(1)} collective-permute-done((bf16[64,2048]{1,0:T(8,128)(2,1)S(1)}, bf16[64,2048]{1,0:T(8,128)(2,1)S(1)}, u32[]{:S(2)}, u32[]{:S(2)}) %collective-permute-start.15) | collective-permute-done | bytes 262176 | tf_op jit(solution)/shard_map/ppermute | solution.py:26
  83.9 2.2 %collective-permute-start.8 = (bf16[32,2048]{1,0:T(8,128)(2,1)S(1)}, bf16[32,2048]{1,0:T(8,128)(2,1)S(1)}, u32[]{:S(2)}, u32[]{:S(2)}) collective-permute-start(bf16[32,2048]{1,0:T(8,128)(2,1)S(1)} %get-tuple-element.52), channel_id=1, source_target_pairs={{0,28},{4,24},{8,20},{12,16},{16,12},{20,8},{24,4},{28,0},{1,29},{... | collective-permute-start | bytes 393224 | tf_op jit(solution)/shard_map/ppermute | solution.py:21
  86.3 3.8 %collective-permute-start.17 = (bf16[32,2048]{1,0:T(8,128)(2,1)S(1)}, bf16[32,2048]{1,0:T(8,128)(2,1)S(1)}, u32[]{:S(2)}, u32[]{:S(2)}) collective-permute-start(bf16[32,2048]{1,0:T(8,128)(2,1)S(1)} %get-tuple-element.50), channel_id=1, source_target_pairs={{0,20},{4,16},{8,28},{12,24},{16,4},{20,0},{24,12},{28,8},{1,21},{... | collective-permute-start | bytes 393224 | tf_op jit(solution)/shard_map/ppermute | solution.py:21
  90.1 2.0 %shard_map.94.refs_7_ = bf16[128,2048]{1,0:T(8,128)(2,1)S(1)} custom-call(s32[4]{0:T(128)S(1)} %pad_add_fusion.s_ref, bf16[128,2176]{1,0:T(8,128)(2,1)S(1)} %get-tuple-element.44.refs_0_, bf16[1,2048,768]{2,1,0:T(8,128)(2,1)S(1)} %get-tuple-element.30.refs_4_.refs_6_.refs_1_, bf16[1,2048,768]{2,1,0:T(8,128)(2,1)S(1)} %get-tuple-element.31.refs_5_.refs_7_.refs_2_, ...), custom_call_target="tpu_custom_call" | custom-call | flops 1207959552 | bytes 11010048 | tf_op jit(solution)/shard_map/pallas_call | solution.py:176
  92.1 3.0 %collective-permute-done.8.refs_1_ = bf16[32,2048]{1,0:T(8,128)(2,1)S(1)} collective-permute-done((bf16[32,2048]{1,0:T(8,128)(2,1)S(1)}, bf16[32,2048]{1,0:T(8,128)(2,1)S(1)}, u32[]{:S(2)}, u32[]{:S(2)}) %collective-permute-start.8) | collective-permute-done | bytes 131104 | tf_op jit(solution)/shard_map/ppermute | solution.py:21
  95.1 8.2 %collective-permute-done.16.refs_2_ = bf16[32,2048]{1,0:T(8,128)(2,1)S(1)} collective-permute-done((bf16[32,2048]{1,0:T(8,128)(2,1)S(1)}, bf16[32,2048]{1,0:T(8,128)(2,1)S(1)}, u32[]{:S(2)}, u32[]{:S(2)}) %collective-permute-start.16) | collective-permute-done | bytes 131104 | tf_op jit(solution)/shard_map/ppermute | solution.py:21
  103.4 3.1 %collective-permute-done.17.refs_3_ = bf16[32,2048]{1,0:T(8,128)(2,1)S(1)} collective-permute-done((bf16[32,2048]{1,0:T(8,128)(2,1)S(1)}, bf16[32,2048]{1,0:T(8,128)(2,1)S(1)}, u32[]{:S(2)}, u32[]{:S(2)}) %collective-permute-start.17) | collective-permute-done | bytes 131104 | tf_op jit(solution)/shard_map/ppermute | solution.py:21
  108.0 1.9 %collective-permute-done.28 = bf16[128,2048]{1,0:T(8,128)(2,1)S(1)} collective-permute-done((bf16[128,2048]{1,0:T(8,128)(2,1)S(1)}, bf16[128,2048]{1,0:T(8,128)(2,1)S(1)}, u32[]{:S(2)}, u32[]{:S(2)}) %collective-permute-start.28) | collective-permute-done | bytes 524320 | tf_op jit(solution)/shard_map/ppermute | solution.py:26
  111.6 6.8 %collective-permute-done.29 = bf16[64,2048]{1,0:T(8,128)(2,1)S(1)} collective-permute-done((bf16[64,2048]{1,0:T(8,128)(2,1)S(1)}, bf16[64,2048]{1,0:T(8,128)(2,1)S(1)}, u32[]{:S(2)}, u32[]{:S(2)}) %collective-permute-start.29) | collective-permute-done | bytes 262176 | tf_op jit(solution)/shard_map/ppermute | solution.py:26
  (73 shorter events, 15.1 us)
Async XLA Ops:
  0.0 42.1 %copy-start.3 = (bf16[2048,512]{1,0:T(8,128)(2,1)S(1)}, bf16[2048,512]{1,0:T(8,128)(2,1)}, u32[]{:S(2)}) copy-start(bf16[2048,512]{1,0:T(8,128)(2,1)} %wg_ref.1) | copy-start | bytes 6291460
  4.5 10.7 %collective-permute-start = (bf16[32,2176]{1,0:T(8,128)(2,1)S(1)}, bf16[32,2176]{1,0:T(8,128)(2,1)S(1)}, u32[]{:S(2)}, u32[]{:S(2)}) collective-permute-start(bf16[32,2176]{1,0:T(8,128)(2,1)S(1)} %get-tuple-element.28), channel_id=1, source_target_pairs={{0,24},{4,28},{8,16},{12,20},{16,8},{20,12},{24,0},{28,4},{1,25},{... | collective-permute-start | bytes 417800 | tf_op jit(solution)/shard_map/ppermute | solution.py:21
  9.6 16.3 %collective-permute-start.1 = (bf16[32,2176]{1,0:T(8,128)(2,1)S(1)}, bf16[32,2176]{1,0:T(8,128)(2,1)S(1)}, u32[]{:S(2)}, u32[]{:S(2)}) collective-permute-start(bf16[32,2176]{1,0:T(8,128)(2,1)S(1)} %get-tuple-element.29), channel_id=1, source_target_pairs={{0,28},{4,24},{8,20},{12,16},{16,12},{20,8},{24,4},{28,0},{1,29},{... | collective-permute-start | bytes 417800 | tf_op jit(solution)/shard_map/ppermute | solution.py:21
  10.8 20.6 %collective-permute-start.9 = (bf16[32,2176]{1,0:T(8,128)(2,1)S(1)}, bf16[32,2176]{1,0:T(8,128)(2,1)S(1)}, u32[]{:S(2)}, u32[]{:S(2)}) collective-permute-start(bf16[32,2176]{1,0:T(8,128)(2,1)S(1)} %get-tuple-element.35), channel_id=1, source_target_pairs={{0,16},{4,20},{8,24},{12,28},{16,0},{20,4},{24,8},{28,12},{1,17},{... | collective-permute-start | bytes 417800 | tf_op jit(solution)/shard_map/ppermute | solution.py:21
  11.5 22.8 %collective-permute-start.10 = (bf16[32,2176]{1,0:T(8,128)(2,1)S(1)}, bf16[32,2176]{1,0:T(8,128)(2,1)S(1)}, u32[]{:S(2)}, u32[]{:S(2)}) collective-permute-start(bf16[32,2176]{1,0:T(8,128)(2,1)S(1)} %get-tuple-element.36), channel_id=1, source_target_pairs={{0,20},{4,16},{8,28},{12,24},{16,4},{20,0},{24,12},{28,8},{1,21},{... | collective-permute-start | bytes 417800 | tf_op jit(solution)/shard_map/ppermute | solution.py:21
  13.5 22.5 %collective-permute-start.18 = (bf16[64,2176]{1,0:T(8,128)(2,1)S(1)}, bf16[64,2176]{1,0:T(8,128)(2,1)S(1)}, u32[]{:S(2)}, u32[]{:S(2)}) collective-permute-start(bf16[64,2176]{1,0:T(8,128)(2,1)S(1)} %get-tuple-element.39), channel_id=1, source_target_pairs={{0,4},{4,0},{8,12},{12,8},{16,20},{20,16},{24,28},{28,24},{1,5},{5... | collective-permute-start | bytes 835592 | tf_op jit(solution)/shard_map/ppermute | solution.py:21
  15.2 21.3 %collective-permute-start.19 = (bf16[64,2176]{1,0:T(8,128)(2,1)S(1)}, bf16[64,2176]{1,0:T(8,128)(2,1)S(1)}, u32[]{:S(2)}, u32[]{:S(2)}) collective-permute-start(bf16[64,2176]{1,0:T(8,128)(2,1)S(1)} %get-tuple-element.40), channel_id=1, source_target_pairs={{0,8},{4,12},{8,0},{12,4},{16,24},{20,28},{24,16},{28,20},{1,9},{5... | collective-permute-start | bytes 835592 | tf_op jit(solution)/shard_map/ppermute | solution.py:21
  25.9 10.1 %collective-permute-start.2 = (bf16[64,2176]{1,0:T(8,128)(2,1)S(1)}, bf16[64,2176]{1,0:T(8,128)(2,1)S(1)}, u32[]{:S(2)}, u32[]{:S(2)}) collective-permute-start(bf16[64,2176]{1,0:T(8,128)(2,1)S(1)} %constant_dynamic-update-slice_fusion.refs_0_), channel_id=1, source_target_pairs={{0,2},{1,3},{2,0},{3,1},{4,6},{5,7},{6,4},{7,5},{8,10},{9,11},{10,... | collective-permute-start | bytes 835592 | tf_op jit(solution)/shard_map/ppermute | solution.py:26
  34.4 7.7 %collective-permute-start.11 = (bf16[64,2176]{1,0:T(8,128)(2,1)S(1)}, bf16[64,2176]{1,0:T(8,128)(2,1)S(1)}, u32[]{:S(2)}, u32[]{:S(2)}) collective-permute-start(bf16[64,2176]{1,0:T(8,128)(2,1)S(1)} %constant_dynamic-update-slice_fusion.2.refs_0_), channel_id=1, source_target_pairs={{0,2},{1,3},{2,0},{3,1},{4,6},{5,7},{6,4},{7,5},{8,10},{9,11},{10,... | collective-permute-start | bytes 835592 | tf_op jit(solution)/shard_map/ppermute | solution.py:26
  36.0 20.8 %collective-permute-start.20 = (bf16[64,2176]{1,0:T(8,128)(2,1)S(1)}, bf16[64,2176]{1,0:T(8,128)(2,1)S(1)}, u32[]{:S(2)}, u32[]{:S(2)}) collective-permute-start(bf16[64,2176]{1,0:T(8,128)(2,1)S(1)} %get-tuple-element.41), channel_id=1, source_target_pairs={{0,12},{4,8},{8,4},{12,0},{16,28},{20,24},{24,20},{28,16},{1,13},{... | collective-permute-start | bytes 835592 | tf_op jit(solution)/shard_map/ppermute | solution.py:21
  36.0 21.3 %collective-permute-start.3 = (bf16[64,2176]{1,0:T(8,128)(2,1)S(1)}, bf16[64,2176]{1,0:T(8,128)(2,1)S(1)}, u32[]{:S(2)}, u32[]{:S(2)}) collective-permute-start(bf16[64,2176]{1,0:T(8,128)(2,1)S(1)} %constant_dynamic-update-slice_fusion.refs_0_), channel_id=1, source_target_pairs={{0,1},{1,0},{2,3},{3,2},{4,5},{5,4},{6,7},{7,6},{8,9},{9,8},{10,11... | collective-permute-start | bytes 835592 | tf_op jit(solution)/shard_map/ppermute | solution.py:26
  36.0 21.4 %collective-permute-start.4 = (bf16[64,2176]{1,0:T(8,128)(2,1)S(1)}, bf16[64,2176]{1,0:T(8,128)(2,1)S(1)}, u32[]{:S(2)}, u32[]{:S(2)}) collective-permute-start(bf16[64,2176]{1,0:T(8,128)(2,1)S(1)} %collective-permute-done.2.refs_1_), channel_id=1, source_target_pairs={{0,1},{1,0},{2,3},{3,2},{4,5},{5,4},{6,7},{7,6},{8,9},{9,8},{10,11... | collective-permute-start | bytes 835592 | tf_op jit(solution)/shard_map/ppermute | solution.py:26
  36.5 24.5 %collective-permute-start.12 = (bf16[64,2176]{1,0:T(8,128)(2,1)S(1)}, bf16[64,2176]{1,0:T(8,128)(2,1)S(1)}, u32[]{:S(2)}, u32[]{:S(2)}) collective-permute-start(bf16[64,2176]{1,0:T(8,128)(2,1)S(1)} %constant_dynamic-update-slice_fusion.2.refs_0_), channel_id=1, source_target_pairs={{0,1},{1,0},{2,3},{3,2},{4,5},{5,4},{6,7},{7,6},{8,9},{9,8},{10,11... | collective-permute-start | bytes 835592 | tf_op jit(solution)/shard_map/ppermute | solution.py:26
  42.1 19.0 %collective-permute-start.13 = (bf16[64,2176]{1,0:T(8,128)(2,1)S(1)}, bf16[64,2176]{1,0:T(8,128)(2,1)S(1)}, u32[]{:S(2)}, u32[]{:S(2)}) collective-permute-start(bf16[64,2176]{1,0:T(8,128)(2,1)S(1)} %collective-permute-done.11.refs_1_), channel_id=1, source_target_pairs={{0,1},{1,0},{2,3},{3,2},{4,5},{5,4},{6,7},{7,6},{8,9},{9,8},{10,11... | collective-permute-start | bytes 835592 | tf_op jit(solution)/shard_map/ppermute | solution.py:26
  42.1 1.9 %copy-start = (bf16[1,2048,768]{2,1,0:T(8,128)(2,1)S(1)}, bf16[1,2048,768]{2,1,0:T(8,128)(2,1)}, u32[]{:S(2)}) copy-start(bf16[1,2048,768]{2,1,0:T(8,128)(2,1)} %eg_hbm.1) | copy-start | bytes 9437188
  56.7 8.1 %collective-permute-start.21 = (bf16[64,2176]{1,0:T(8,128)(2,1)S(1)}, bf16[64,2176]{1,0:T(8,128)(2,1)S(1)}, u32[]{:S(2)}, u32[]{:S(2)}) collective-permute-start(bf16[64,2176]{1,0:T(8,128)(2,1)S(1)} %collective-permute-done.18.refs_0_), channel_id=1, source_target_pairs={{0,1},{1,0},{2,3},{3,2},{4,5},{5,4},{6,7},{7,6},{8,9},{9,8},{10,11... | collective-permute-start | bytes 835592 | tf_op jit(solution)/shard_map/ppermute | solution.py:26
  57.3 7.5 %collective-permute-start.22 = (bf16[64,2176]{1,0:T(8,128)(2,1)S(1)}, bf16[64,2176]{1,0:T(8,128)(2,1)S(1)}, u32[]{:S(2)}, u32[]{:S(2)}) collective-permute-start(bf16[64,2176]{1,0:T(8,128)(2,1)S(1)} %collective-permute-done.19.refs_1_), channel_id=1, source_target_pairs={{0,1},{1,0},{2,3},{3,2},{4,5},{5,4},{6,7},{7,6},{8,9},{9,8},{10,11... | collective-permute-start | bytes 835592 | tf_op jit(solution)/shard_map/ppermute | solution.py:26
  57.4 7.4 %collective-permute-start.23 = (bf16[64,2176]{1,0:T(8,128)(2,1)S(1)}, bf16[64,2176]{1,0:T(8,128)(2,1)S(1)}, u32[]{:S(2)}, u32[]{:S(2)}) collective-permute-start(bf16[64,2176]{1,0:T(8,128)(2,1)S(1)} %collective-permute-done.20.refs_2_), channel_id=1, source_target_pairs={{0,1},{1,0},{2,3},{3,2},{4,5},{5,4},{6,7},{7,6},{8,9},{9,8},{10,11... | collective-permute-start | bytes 835592 | tf_op jit(solution)/shard_map/ppermute | solution.py:26
  61.0 8.4 %collective-permute-start.5 = (bf16[128,2048]{1,0:T(8,128)(2,1)S(1)}, bf16[128,2048]{1,0:T(8,128)(2,1)S(1)}, u32[]{:S(2)}, u32[]{:S(2)}) collective-permute-start(bf16[128,2048]{1,0:T(8,128)(2,1)S(1)} %get-tuple-element.34), channel_id=1, source_target_pairs={{0,1},{1,0},{2,3},{3,2},{4,5},{5,4},{6,7},{7,6},{8,9},{9,8},{10,11... | collective-permute-start | bytes 1572872 | tf_op jit(solution)/shard_map/ppermute | solution.py:26
  64.3 6.8 %collective-permute-start.14 = (bf16[128,2048]{1,0:T(8,128)(2,1)S(1)}, bf16[128,2048]{1,0:T(8,128)(2,1)S(1)}, u32[]{:S(2)}, u32[]{:S(2)}) collective-permute-start(bf16[128,2048]{1,0:T(8,128)(2,1)S(1)} %get-tuple-element.38), channel_id=1, source_target_pairs={{0,1},{1,0},{2,3},{3,2},{4,5},{5,4},{6,7},{7,6},{8,9},{9,8},{10,11... | collective-permute-start | bytes 1572872 | tf_op jit(solution)/shard_map/ppermute | solution.py:26
  69.2 2.6 %collective-permute-start.24 = (bf16[192,2048]{1,0:T(8,128)(2,1)S(1)}, bf16[192,2048]{1,0:T(8,128)(2,1)S(1)}, u32[]{:S(2)}, u32[]{:S(2)}) collective-permute-start(bf16[192,2048]{1,0:T(8,128)(2,1)S(1)} %get-tuple-element.43), channel_id=1, source_target_pairs={{0,1},{1,0},{2,3},{3,2},{4,5},{5,4},{6,7},{7,6},{8,9},{9,8},{10,11... | collective-permute-start | bytes 2359304 | tf_op jit(solution)/shard_map/ppermute | solution.py:26
  69.5 9.2 %collective-permute-start.6 = (bf16[64,2048]{1,0:T(8,128)(2,1)S(1)}, bf16[64,2048]{1,0:T(8,128)(2,1)S(1)}, u32[]{:S(2)}, u32[]{:S(2)}) collective-permute-start(bf16[64,2048]{1,0:T(8,128)(2,1)S(1)} %slice.82), channel_id=1, source_target_pairs={{0,2},{1,3},{2,0},{3,1},{4,6},{5,7},{6,4},{7,5},{8,10},{9,11},{10,... | collective-permute-start | bytes 786440 | tf_op jit(solution)/shard_map/ppermute | solution.py:26
  71.3 12.6 %collective-permute-start.15 = (bf16[64,2048]{1,0:T(8,128)(2,1)S(1)}, bf16[64,2048]{1,0:T(8,128)(2,1)S(1)}, u32[]{:S(2)}, u32[]{:S(2)}) collective-permute-start(bf16[64,2048]{1,0:T(8,128)(2,1)S(1)} %slice.81), channel_id=1, source_target_pairs={{0,2},{1,3},{2,0},{3,1},{4,6},{5,7},{6,4},{7,5},{8,10},{9,11},{10,... | collective-permute-start | bytes 786440 | tf_op jit(solution)/shard_map/ppermute | solution.py:26
  72.2 14.0 %collective-permute-start.25 = (bf16[64,2048]{1,0:T(8,128)(2,1)S(1)}, bf16[64,2048]{1,0:T(8,128)(2,1)S(1)}, u32[]{:S(2)}, u32[]{:S(2)}) collective-permute-start(bf16[64,2048]{1,0:T(8,128)(2,1)S(1)} %get-tuple-element.49), channel_id=1, source_target_pairs={{0,4},{4,0},{8,12},{12,8},{16,20},{20,16},{24,28},{28,24},{1,5},{5... | collective-permute-start | bytes 786440 | tf_op jit(solution)/shard_map/ppermute | solution.py:21
  72.8 13.5 %collective-permute-start.26 = (bf16[64,2048]{1,0:T(8,128)(2,1)S(1)}, bf16[64,2048]{1,0:T(8,128)(2,1)S(1)}, u32[]{:S(2)}, u32[]{:S(2)}) collective-permute-start(bf16[64,2048]{1,0:T(8,128)(2,1)S(1)} %get-tuple-element.48), channel_id=1, source_target_pairs={{0,8},{4,12},{8,0},{12,4},{16,24},{20,28},{24,16},{28,20},{1,9},{5... | collective-permute-start | bytes 786440 | tf_op jit(solution)/shard_map/ppermute | solution.py:21
  73.3 18.8 %collective-permute-start.27 = (bf16[64,2048]{1,0:T(8,128)(2,1)S(1)}, bf16[64,2048]{1,0:T(8,128)(2,1)S(1)}, u32[]{:S(2)}, u32[]{:S(2)}) collective-permute-start(bf16[64,2048]{1,0:T(8,128)(2,1)S(1)} %get-tuple-element.47), channel_id=1, source_target_pairs={{0,12},{4,8},{8,4},{12,0},{16,28},{20,24},{24,20},{28,16},{1,13},{... | collective-permute-start | bytes 786440 | tf_op jit(solution)/shard_map/ppermute | solution.py:21
  78.9 13.3 %collective-permute-start.7 = (bf16[32,2048]{1,0:T(8,128)(2,1)S(1)}, bf16[32,2048]{1,0:T(8,128)(2,1)S(1)}, u32[]{:S(2)}, u32[]{:S(2)}) collective-permute-start(bf16[32,2048]{1,0:T(8,128)(2,1)S(1)} %get-tuple-element.53), channel_id=1, source_target_pairs={{0,24},{4,28},{8,16},{12,20},{16,8},{20,12},{24,0},{28,4},{1,25},{... | collective-permute-start | bytes 393224 | tf_op jit(solution)/shard_map/ppermute | solution.py:21
  83.9 11.3 %collective-permute-start.8 = (bf16[32,2048]{1,0:T(8,128)(2,1)S(1)}, bf16[32,2048]{1,0:T(8,128)(2,1)S(1)}, u32[]{:S(2)}, u32[]{:S(2)}) collective-permute-start(bf16[32,2048]{1,0:T(8,128)(2,1)S(1)} %get-tuple-element.52), channel_id=1, source_target_pairs={{0,28},{4,24},{8,20},{12,16},{16,12},{20,8},{24,4},{28,0},{1,29},{... | collective-permute-start | bytes 393224 | tf_op jit(solution)/shard_map/ppermute | solution.py:21
  86.2 17.2 %collective-permute-start.16 = (bf16[32,2048]{1,0:T(8,128)(2,1)S(1)}, bf16[32,2048]{1,0:T(8,128)(2,1)S(1)}, u32[]{:S(2)}, u32[]{:S(2)}) collective-permute-start(bf16[32,2048]{1,0:T(8,128)(2,1)S(1)} %get-tuple-element.51), channel_id=1, source_target_pairs={{0,16},{4,20},{8,24},{12,28},{16,0},{20,4},{24,8},{28,12},{1,17},{... | collective-permute-start | bytes 393224 | tf_op jit(solution)/shard_map/ppermute | solution.py:21
  86.3 20.1 %collective-permute-start.17 = (bf16[32,2048]{1,0:T(8,128)(2,1)S(1)}, bf16[32,2048]{1,0:T(8,128)(2,1)S(1)}, u32[]{:S(2)}, u32[]{:S(2)}) collective-permute-start(bf16[32,2048]{1,0:T(8,128)(2,1)S(1)} %get-tuple-element.50), channel_id=1, source_target_pairs={{0,20},{4,16},{8,28},{12,24},{16,4},{20,0},{24,12},{28,8},{1,21},{... | collective-permute-start | bytes 393224 | tf_op jit(solution)/shard_map/ppermute | solution.py:21
  107.9 2.0 %collective-permute-start.28 = (bf16[128,2048]{1,0:T(8,128)(2,1)S(1)}, bf16[128,2048]{1,0:T(8,128)(2,1)S(1)}, u32[]{:S(2)}, u32[]{:S(2)}) collective-permute-start(bf16[128,2048]{1,0:T(8,128)(2,1)S(1)} %get-tuple-element.46), channel_id=1, source_target_pairs={{0,1},{1,0},{2,3},{3,2},{4,5},{5,4},{6,7},{7,6},{8,9},{9,8},{10,11... | collective-permute-start | bytes 1572872 | tf_op jit(solution)/shard_map/ppermute | solution.py:26
  110.1 8.4 %collective-permute-start.29 = (bf16[64,2048]{1,0:T(8,128)(2,1)S(1)}, bf16[64,2048]{1,0:T(8,128)(2,1)S(1)}, u32[]{:S(2)}, u32[]{:S(2)}) collective-permute-start(bf16[64,2048]{1,0:T(8,128)(2,1)S(1)} %slice.80), channel_id=1, source_target_pairs={{0,2},{1,3},{2,0},{3,1},{4,6},{5,7},{6,4},{7,5},{8,10},{9,11},{10,... | collective-permute-start | bytes 786440 | tf_op jit(solution)/shard_map/ppermute | solution.py:26
  (8 other events, 10.9 us)
where the time goes:
time: 120 us; the launch traced here: 119 us
  starting transfers between devices  42.9 us (36%)
  waiting for transfers between devices  41.1 us (34%)
  Pallas kernels  20.3 us (17%)
  local copies, waits for them, and re-layouts  13.1 us (11%)
  other arithmetic  1.53 us (1%)
    ppermute x14, starting transfers between devices, xor_node(): return lax.ppermute(x, 'node', [(i, i ^ k) for i in range(count)])  33.5 us
    ppermute x14, waiting for transfers between devices, xor_node(): return lax.ppermute(x, 'node', [(i, i ^ k) for i in range(count)])  21.1 us
    ppermute x16, waiting for transfers between devices, xor_local(): return lax.ppermute(x, 'local', [(i, i ^ k) for i in range(count)])  20 us
    unnamed x22, local copies, waits for them, and re-layouts  12.8 us
    pallas_call x4, Pallas kernels, ffn(): pl.pallas_call(functools.partial(ffn_kernel, counts, experts, keep), out_...  12.7 us
    ppermute x16, starting transfers between devices, xor_local(): return lax.ppermute(x, 'local', [(i, i ^ k) for i in range(count)])  9.41 us
    pallas_call x1, Pallas kernels, shared(): pl.pallas_call(shared_kernel, grid=(hidden // block,), out_shape=[jax.Sha...  4.5 us
  transfers between devices with their start and end apart: 30, of which 10 were waited for; matrix products, arithmetic and copies ran while one was open for 1% of the time, Pallas kernels for 14%

commit v1 on v0

--- a/solution.py
+++ b/solution.py
@@ -331,8 +331,14 @@
     near = [k for k in range(1, NEAR)]
     pieces = [(k, 1, capacity // local_count) for ks in chunks for k in ks]
     pieces += [(k, 3, capacity // 2) for k in near] + [(0, None, capacity)]
-    sends, one_hot = route(scalars, expert_ids.T, gate_scores.T, tokens, tuple(pieces), node_count)
-    weights = (expert_gate, expert_up, expert_down)
+    in_hbm = functools.partial(pltpu.with_memory_space_constraint, memory_space=pltpu.HBM)
+    sends, one_hot = route(
+        scalars, in_hbm(expert_ids.T), in_hbm(gate_scores.T), in_hbm(tokens), tuple(pieces), node_count
+    )
+    weights = [pltpu.with_memory_space_constraint(w, pltpu.HBM) for w in (expert_gate, expert_up, expert_down)]
+    shared_gate, shared_up, shared_down = [
+        pltpu.with_memory_space_constraint(w, pltpu.HBM) for w in (shared_gate, shared_up, shared_down)
+    ]
 
     arrived = []
     index = 0

time: 120 us -> 109 us (0.908)
  local copies, waits for them, and re-layouts: 13.1 us -> 0.26 us
  Pallas kernels: 20.3 us -> 22.6 us
    unnamed x22 -> x4, local copies, waits for them, and re-layouts: 12.8 us -> 0.02 us
    pallas_call x1, Pallas kernels: 4.5 us -> 5.78 us  [shared(): pl.pallas_call(shared_kernel, grid=(hidden // block,), out_shape=[jax.Sha...]
  transfers between devices with their start and end apart: 30 -> 30, of which waited for: 10 -> 10; matrix products, arithmetic and copies ran while one was open for 1% -> 1% of each run, Pallas kernels for 14% -> 17%
where the time goes in v1:
time: 109 us
  starting transfers between devices  42.9 us (39%)
  waiting for transfers between devices  41 us (38%)
  Pallas kernels  22.6 us (21%)
  other arithmetic  1.53 us (1%)
    ppermute x14, starting transfers between devices, xor_node(): return lax.ppermute(x, 'node', [(i, i ^ k) for i in range(count)])  33.5 us
    ppermute x14, waiting for transfers between devices, xor_node(): return lax.ppermute(x, 'node', [(i, i ^ k) for i in range(count)])  21.1 us
    ppermute x16, waiting for transfers between devices, xor_local(): return lax.ppermute(x, 'local', [(i, i ^ k) for i in range(count)])  20 us
    pallas_call x4, Pallas kernels, ffn(): pl.pallas_call(functools.partial(ffn_kernel, counts, experts, keep), out_...  12.8 us
    ppermute x16, starting transfers between devices, xor_local(): return lax.ppermute(x, 'local', [(i, i ^ k) for i in range(count)])  9.43 us
    pallas_call x1, Pallas kernels, shared(): pl.pallas_call(shared_kernel, grid=(hidden // block,), out_shape=[jax.Sha...  5.78 us
    pallas_call x1, Pallas kernels, route(): pl.pallas_call(functools.partial(route_kernel, pieces, node_count), out_s...  2.55 us
  transfers between devices with their start and end apart: 30, of which 10 were waited for; matrix products, arithmetic and copies ran while one was open for 1% of the time, Pallas kernels for 17%

profile of v1, /device:TPU:0, one launch (start us, length us, event | category | flops | bytes accessed | tf_op | source)
XLA Modules:
  0.0 108.6 jit_solution(4516879017348357943)
XLA Ops:
  0.1 2.6 %route.1 = (bf16[32,2176]{1,0:T(8,128)(2,1)S(1)}, bf16[32,2176]{1,0:T(8,128)(2,1)S(1)}, bf16[32,2176]{1,0:T(8,128)(2,1)S(1)}, bf16[32,2176]{1,0:T(8,128)(2,1)S(1...) custom-call(s32[4]{0:T(128)S(1)} %pad_add_fusion.s_ref, ...), custom_call_target="tpu_custom_call" | custom-call | flops 499122176 | bytes 2998272 | tf_op jit(solution)/shard_map/route/pallas_call | solution.py:108
  2.6 5.1 %collective-permute-start = (bf16[32,2176]{1,0:T(8,128)(2,1)S(1)}, bf16[32,2176]{1,0:T(8,128)(2,1)S(1)}, u32[]{:S(2)}, u32[]{:S(2)}) collective-permute-start(bf16[32,2176]{1,0:T(8,128)(2,1)S(1)} %get-tuple-element.28), channel_id=1, source_target_pairs={{0,24},{4,28},{8,16},{12,20},{16,8},{20,12},{24,0},{28,4},{1,25},{... | collective-permute-start | bytes 417800 | tf_op jit(solution)/shard_map/ppermute | solution.py:21
  7.8 1.1 %collective-permute-start.1 = (bf16[32,2176]{1,0:T(8,128)(2,1)S(1)}, bf16[32,2176]{1,0:T(8,128)(2,1)S(1)}, u32[]{:S(2)}, u32[]{:S(2)}) collective-permute-start(bf16[32,2176]{1,0:T(8,128)(2,1)S(1)} %get-tuple-element.29), channel_id=1, source_target_pairs={{0,28},{4,24},{8,20},{12,16},{16,12},{20,8},{24,4},{28,0},{1,29},{... | collective-permute-start | bytes 417800 | tf_op jit(solution)/shard_map/ppermute | solution.py:21
  8.9 0.8 collective-permute-start.9
  9.7 2.0 %collective-permute-start.10 = (bf16[32,2176]{1,0:T(8,128)(2,1)S(1)}, bf16[32,2176]{1,0:T(8,128)(2,1)S(1)}, u32[]{:S(2)}, u32[]{:S(2)}) collective-permute-start(bf16[32,2176]{1,0:T(8,128)(2,1)S(1)} %get-tuple-element.36), channel_id=1, source_target_pairs={{0,20},{4,16},{8,28},{12,24},{16,4},{20,0},{24,12},{28,8},{1,21},{... | collective-permute-start | bytes 417800 | tf_op jit(solution)/shard_map/ppermute | solution.py:21
  11.7 1.6 %collective-permute-start.18 = (bf16[64,2176]{1,0:T(8,128)(2,1)S(1)}, bf16[64,2176]{1,0:T(8,128)(2,1)S(1)}, u32[]{:S(2)}, u32[]{:S(2)}) collective-permute-start(bf16[64,2176]{1,0:T(8,128)(2,1)S(1)} %get-tuple-element.39), channel_id=1, source_target_pairs={{0,4},{4,0},{8,12},{12,8},{16,20},{20,16},{24,28},{28,24},{1,5},{5... | collective-permute-start | bytes 835592 | tf_op jit(solution)/shard_map/ppermute | solution.py:21
  13.3 10.7 %collective-permute-start.19 = (bf16[64,2176]{1,0:T(8,128)(2,1)S(1)}, bf16[64,2176]{1,0:T(8,128)(2,1)S(1)}, u32[]{:S(2)}, u32[]{:S(2)}) collective-permute-start(bf16[64,2176]{1,0:T(8,128)(2,1)S(1)} %get-tuple-element.40), channel_id=1, source_target_pairs={{0,8},{4,12},{8,0},{12,4},{16,24},{20,28},{24,16},{28,20},{1,9},{5... | collective-permute-start | bytes 835592 | tf_op jit(solution)/shard_map/ppermute | solution.py:21
  24.1 1.6 %collective-permute-start.2 = (bf16[64,2176]{1,0:T(8,128)(2,1)S(1)}, bf16[64,2176]{1,0:T(8,128)(2,1)S(1)}, u32[]{:S(2)}, u32[]{:S(2)}) collective-permute-start(bf16[64,2176]{1,0:T(8,128)(2,1)S(1)} %constant_dynamic-update-slice_fusion.refs_0_), channel_id=1, source_target_pairs={{0,2},{1,3},{2,0},{3,1},{4,6},{5,7},{6,4},{7,5},{8,10},{9,11},{10,... | collective-permute-start | bytes 835592 | tf_op jit(solution)/shard_map/ppermute | solution.py:26
  25.7 3.9 %collective-permute-done.9 = bf16[32,2176]{1,0:T(8,128)(2,1)S(1)} collective-permute-done((bf16[32,2176]{1,0:T(8,128)(2,1)S(1)}, bf16[32,2176]{1,0:T(8,128)(2,1)S(1)}, u32[]{:S(2)}, u32[]{:S(2)}) %collective-permute-start.9) | collective-permute-done | bytes 139296 | tf_op jit(solution)/shard_map/ppermute | solution.py:21
  29.6 2.9 %collective-permute-done.10 = bf16[32,2176]{1,0:T(8,128)(2,1)S(1)} collective-permute-done((bf16[32,2176]{1,0:T(8,128)(2,1)S(1)}, bf16[32,2176]{1,0:T(8,128)(2,1)S(1)}, u32[]{:S(2)}, u32[]{:S(2)}) %collective-permute-start.10) | collective-permute-done | bytes 139296 | tf_op jit(solution)/shard_map/ppermute | solution.py:21
  32.5 1.6 %collective-permute-start.11 = (bf16[64,2176]{1,0:T(8,128)(2,1)S(1)}, bf16[64,2176]{1,0:T(8,128)(2,1)S(1)}, u32[]{:S(2)}, u32[]{:S(2)}) collective-permute-start(bf16[64,2176]{1,0:T(8,128)(2,1)S(1)} %constant_dynamic-update-slice_fusion.2.refs_0_), channel_id=1, source_target_pairs={{0,2},{1,3},{2,0},{3,1},{4,6},{5,7},{6,4},{7,5},{8,10},{9,11},{10,... | collective-permute-start | bytes 835592 | tf_op jit(solution)/shard_map/ppermute | solution.py:26
  34.7 5.5 %collective-permute-done.11.refs_1_ = bf16[64,2176]{1,0:T(8,128)(2,1)S(1)} collective-permute-done((bf16[64,2176]{1,0:T(8,128)(2,1)S(1)}, bf16[64,2176]{1,0:T(8,128)(2,1)S(1)}, u32[]{:S(2)}, u32[]{:S(2)}) %collective-permute-start.11) | collective-permute-done | bytes 278560 | tf_op jit(solution)/shard_map/ppermute | solution.py:26
  40.3 5.8 %shared.1 = (f32[256,2048]{1,0:T(8,128)S(1)}, bf16[1,2048,768]{2,1,0:T(8,128)(2,1)S(1)}, bf16[1,2048,768]{2,1,0:T(8,128)(2,1)S(1)}, bf16[1,768,2048]{2,1,0:T(8,128)(2,1)S(1)}) custom-call(bf16[256,2048]{1,0:T(8,128)(2,1)S(1)} %copy-done, bf16[2048,512]{1,0:T(8,128)(2,1)} %wg_ref.1, bf16[2048,512]{1,0:T(8,128)(2,1)} %wu_ref.1, bf16[512,2048]{1,0:T(8,128)(2,1)} %wd_ref.1, ...), custom_call_target="tpu_custom_call" | custom-call | flops 1610612736 | bytes 28311552 | tf_op jit(solution)/shard_map/shared/pallas_call | solution.py:227
  47.2 3.2 %shard_map.91 = (f32[128,2048]{1,0:T(8,128)S(1)}, bf16[128,2048]{1,0:T(8,128)(2,1)S(1)}) custom-call(s32[4]{0:T(128)S(1)} %pad_add_fusion.s_ref, bf16[64,2176]{1,0:T(8,128)(2,1)S(1)} %constant_dynamic-update-slice_fusion.refs_0_, bf16[64,2176]{1,0:T(8,128)(2,1)S(1)} %collective-permute-done.2.refs_1_, bf16[64,2176]{1,0:T(8,128)(2,1)S(1)} %collective-permute-done.3.refs_2_, ...), custom_call_target="tpu_custom_call" | custom-call | flops 2415919104 | bytes 12582912 | tf_op jit(solution)/shard_map/pallas_call | solution.py:176
  50.5 3.2 %shard_map.92 = (f32[128,2048]{1,0:T(8,128)S(1)}, bf16[128,2048]{1,0:T(8,128)(2,1)S(1)}) custom-call(s32[4]{0:T(128)S(1)} %pad_add_fusion.s_ref, bf16[64,2176]{1,0:T(8,128)(2,1)S(1)} %constant_dynamic-update-slice_fusion.2.refs_0_, bf16[64,2176]{1,0:T(8,128)(2,1)S(1)} %collective-permute-done.11.refs_1_, ...), custom_call_target="tpu_custom_call" | custom-call | flops 2415919104 | bytes 12582912 | tf_op jit(solution)/shard_map/pallas_call | solution.py:176
  54.2 4.4 %shard_map.93 = (f32[192,2048]{1,0:T(8,128)S(1)}, bf16[192,2048]{1,0:T(8,128)(2,1)S(1)}) custom-call(s32[4]{0:T(128)S(1)} %pad_add_fusion.s_ref, bf16[64,2176]{1,0:T(8,128)(2,1)S(1)} %collective-permute-done.18.refs_0_, bf16[64,2176]{1,0:T(8,128)(2,1)S(1)} %collective-permute-done.19.refs_1_, bf16[64,2176]{1,0:T(8,128)(2,1)S(1)} %collective-permute-done.20.refs_2_, ...), custom_call_target="tpu_custom_call" | custom-call | flops 3623878656 | bytes 14155776 | tf_op jit(solution)/shard_map/pallas_call | solution.py:176
  59.0 1.6 %collective-permute-start.6 = (bf16[64,2048]{1,0:T(8,128)(2,1)S(1)}, bf16[64,2048]{1,0:T(8,128)(2,1)S(1)}, u32[]{:S(2)}, u32[]{:S(2)}) collective-permute-start(bf16[64,2048]{1,0:T(8,128)(2,1)S(1)} %slice.82), channel_id=1, source_target_pairs={{0,2},{1,3},{2,0},{3,1},{4,6},{5,7},{6,4},{7,5},{8,10},{9,11},{10,... | collective-permute-start | bytes 786440 | tf_op jit(solution)/shard_map/ppermute | solution.py:26
  62.7 2.4 %collective-permute-start.27 = (bf16[64,2048]{1,0:T(8,128)(2,1)S(1)}, bf16[64,2048]{1,0:T(8,128)(2,1)S(1)}, u32[]{:S(2)}, u32[]{:S(2)}) collective-permute-start(bf16[64,2048]{1,0:T(8,128)(2,1)S(1)} %get-tuple-element.47), channel_id=1, source_target_pairs={{0,12},{4,8},{8,4},{12,0},{16,28},{20,24},{24,20},{28,16},{1,13},{... | collective-permute-start | bytes 786440 | tf_op jit(solution)/shard_map/ppermute | solution.py:21
  65.2 3.1 %collective-permute-done.6 = bf16[64,2048]{1,0:T(8,128)(2,1)S(1)} collective-permute-done((bf16[64,2048]{1,0:T(8,128)(2,1)S(1)}, bf16[64,2048]{1,0:T(8,128)(2,1)S(1)}, u32[]{:S(2)}, u32[]{:S(2)}) %collective-permute-start.6) | collective-permute-done | bytes 262176 | tf_op jit(solution)/shard_map/ppermute | solution.py:26
  68.3 2.4 %collective-permute-start.7 = (bf16[32,2048]{1,0:T(8,128)(2,1)S(1)}, bf16[32,2048]{1,0:T(8,128)(2,1)S(1)}, u32[]{:S(2)}, u32[]{:S(2)}) collective-permute-start(bf16[32,2048]{1,0:T(8,128)(2,1)S(1)} %get-tuple-element.53), channel_id=1, source_target_pairs={{0,24},{4,28},{8,16},{12,20},{16,8},{20,12},{24,0},{28,4},{1,25},{... | collective-permute-start | bytes 393224 | tf_op jit(solution)/shard_map/ppermute | solution.py:21
  70.7 2.6 %collective-permute-done.15 = bf16[64,2048]{1,0:T(8,128)(2,1)S(1)} collective-permute-done((bf16[64,2048]{1,0:T(8,128)(2,1)S(1)}, bf16[64,2048]{1,0:T(8,128)(2,1)S(1)}, u32[]{:S(2)}, u32[]{:S(2)}) %collective-permute-start.15) | collective-permute-done | bytes 262176 | tf_op jit(solution)/shard_map/ppermute | solution.py:26
  73.3 2.3 %collective-permute-start.8 = (bf16[32,2048]{1,0:T(8,128)(2,1)S(1)}, bf16[32,2048]{1,0:T(8,128)(2,1)S(1)}, u32[]{:S(2)}, u32[]{:S(2)}) collective-permute-start(bf16[32,2048]{1,0:T(8,128)(2,1)S(1)} %get-tuple-element.52), channel_id=1, source_target_pairs={{0,28},{4,24},{8,20},{12,16},{16,12},{20,8},{24,4},{28,0},{1,29},{... | collective-permute-start | bytes 393224 | tf_op jit(solution)/shard_map/ppermute | solution.py:21
  75.8 3.8 %collective-permute-start.17 = (bf16[32,2048]{1,0:T(8,128)(2,1)S(1)}, bf16[32,2048]{1,0:T(8,128)(2,1)S(1)}, u32[]{:S(2)}, u32[]{:S(2)}) collective-permute-start(bf16[32,2048]{1,0:T(8,128)(2,1)S(1)} %get-tuple-element.50), channel_id=1, source_target_pairs={{0,20},{4,16},{8,28},{12,24},{16,4},{20,0},{24,12},{28,8},{1,21},{... | collective-permute-start | bytes 393224 | tf_op jit(solution)/shard_map/ppermute | solution.py:21
  79.6 2.0 %shard_map.94.refs_7_ = bf16[128,2048]{1,0:T(8,128)(2,1)S(1)} custom-call(s32[4]{0:T(128)S(1)} %pad_add_fusion.s_ref, bf16[128,2176]{1,0:T(8,128)(2,1)S(1)} %get-tuple-element.44.refs_0_, bf16[1,2048,768]{2,1,0:T(8,128)(2,1)S(1)} %get-tuple-element.30.refs_4_.refs_6_.refs_1_, bf16[1,2048,768]{2,1,0:T(8,128)(2,1)S(1)} %get-tuple-element.31.refs_5_.refs_7_.refs_2_, ...), custom_call_target="tpu_custom_call" | custom-call | flops 1207959552 | bytes 11010048 | tf_op jit(solution)/shard_map/pallas_call | solution.py:176
  81.6 2.9 %collective-permute-done.8.refs_1_ = bf16[32,2048]{1,0:T(8,128)(2,1)S(1)} collective-permute-done((bf16[32,2048]{1,0:T(8,128)(2,1)S(1)}, bf16[32,2048]{1,0:T(8,128)(2,1)S(1)}, u32[]{:S(2)}, u32[]{:S(2)}) %collective-permute-start.8) | collective-permute-done | bytes 131104 | tf_op jit(solution)/shard_map/ppermute | solution.py:21
  84.6 8.3 %collective-permute-done.16.refs_2_ = bf16[32,2048]{1,0:T(8,128)(2,1)S(1)} collective-permute-done((bf16[32,2048]{1,0:T(8,128)(2,1)S(1)}, bf16[32,2048]{1,0:T(8,128)(2,1)S(1)}, u32[]{:S(2)}, u32[]{:S(2)}) %collective-permute-start.16) | collective-permute-done | bytes 131104 | tf_op jit(solution)/shard_map/ppermute | solution.py:21
  92.8 3.0 %collective-permute-done.17.refs_3_ = bf16[32,2048]{1,0:T(8,128)(2,1)S(1)} collective-permute-done((bf16[32,2048]{1,0:T(8,128)(2,1)S(1)}, bf16[32,2048]{1,0:T(8,128)(2,1)S(1)}, u32[]{:S(2)}, u32[]{:S(2)}) %collective-permute-start.17) | collective-permute-done | bytes 131104 | tf_op jit(solution)/shard_map/ppermute | solution.py:21
  95.9 1.5 %combine.1 = (f32[128,2048]{1,0:T(8,128)S(1)}, bf16[128,2048]{1,0:T(8,128)(2,1)S(1)}) custom-call(s32[4]{0:T(128)S(1)} %pad_add_fusion.s_ref, bf16[448,256]{1,0:T(8,128)(2,1)S(1)} %get-tuple-element.26.oh_ref, f32[256,2048]{1,0:T(8,128)S(1)} %get-tuple-element.27.shared_ref, bf16[32,2048]{1,0:T(8,128)(2,1)S(1)} %collective-permute-done.7.refs_0_, ...), custom_call_target="tpu_custom_call" | custom-call | flops 469762048 | bytes 5505024 | tf_op jit(solution)/shard_map/combine/pallas_call | solution.py:282
  97.4 1.9 %collective-permute-done.28 = bf16[128,2048]{1,0:T(8,128)(2,1)S(1)} collective-permute-done((bf16[128,2048]{1,0:T(8,128)(2,1)S(1)}, bf16[128,2048]{1,0:T(8,128)(2,1)S(1)}, u32[]{:S(2)}, u32[]{:S(2)}) %collective-permute-start.28) | collective-permute-done | bytes 524320 | tf_op jit(solution)/shard_map/ppermute | solution.py:26
  99.5 1.6 %collective-permute-start.29 = (bf16[64,2048]{1,0:T(8,128)(2,1)S(1)}, bf16[64,2048]{1,0:T(8,128)(2,1)S(1)}, u32[]{:S(2)}, u32[]{:S(2)}) collective-permute-start(bf16[64,2048]{1,0:T(8,128)(2,1)S(1)} %slice.80), channel_id=1, source_target_pairs={{0,2},{1,3},{2,0},{3,1},{4,6},{5,7},{6,4},{7,5},{8,10},{9,11},{10,... | collective-permute-start | bytes 786440 | tf_op jit(solution)/shard_map/ppermute | solution.py:26
  101.0 6.8 %collective-permute-done.29 = bf16[64,2048]{1,0:T(8,128)(2,1)S(1)} collective-permute-done((bf16[64,2048]{1,0:T(8,128)(2,1)S(1)}, bf16[64,2048]{1,0:T(8,128)(2,1)S(1)}, u32[]{:S(2)}, u32[]{:S(2)}) %collective-permute-start.29) | collective-permute-done | bytes 262176 | tf_op jit(solution)/shard_map/ppermute | solution.py:26
  107.9 0.8 fusion
  (55 shorter events, 5.4 us)
Async XLA Ops:
  0.0 40.3 %copy-start = (bf16[256,2048]{1,0:T(8,128)(2,1)S(1)}, bf16[256,2048]{1,0:T(8,128)(2,1)}, u32[]{:S(2)}) copy-start(bf16[256,2048]{1,0:T(8,128)(2,1)} %x_ref.1) | copy-start | bytes 3145732
  2.6 10.7 %collective-permute-start = (bf16[32,2176]{1,0:T(8,128)(2,1)S(1)}, bf16[32,2176]{1,0:T(8,128)(2,1)S(1)}, u32[]{:S(2)}, u32[]{:S(2)}) collective-permute-start(bf16[32,2176]{1,0:T(8,128)(2,1)S(1)} %get-tuple-element.28), channel_id=1, source_target_pairs={{0,24},{4,28},{8,16},{12,20},{16,8},{20,12},{24,0},{28,4},{1,25},{... | collective-permute-start | bytes 417800 | tf_op jit(solution)/shard_map/ppermute | solution.py:21
  7.8 16.3 %collective-permute-start.1 = (bf16[32,2176]{1,0:T(8,128)(2,1)S(1)}, bf16[32,2176]{1,0:T(8,128)(2,1)S(1)}, u32[]{:S(2)}, u32[]{:S(2)}) collective-permute-start(bf16[32,2176]{1,0:T(8,128)(2,1)S(1)} %get-tuple-element.29), channel_id=1, source_target_pairs={{0,28},{4,24},{8,20},{12,16},{16,12},{20,8},{24,4},{28,0},{1,29},{... | collective-permute-start | bytes 417800 | tf_op jit(solution)/shard_map/ppermute | solution.py:21
  8.9 20.6 %collective-permute-start.9 = (bf16[32,2176]{1,0:T(8,128)(2,1)S(1)}, bf16[32,2176]{1,0:T(8,128)(2,1)S(1)}, u32[]{:S(2)}, u32[]{:S(2)}) collective-permute-start(bf16[32,2176]{1,0:T(8,128)(2,1)S(1)} %get-tuple-element.35), channel_id=1, source_target_pairs={{0,16},{4,20},{8,24},{12,28},{16,0},{20,4},{24,8},{28,12},{1,17},{... | collective-permute-start | bytes 417800 | tf_op jit(solution)/shard_map/ppermute | solution.py:21
  9.7 22.8 %collective-permute-start.10 = (bf16[32,2176]{1,0:T(8,128)(2,1)S(1)}, bf16[32,2176]{1,0:T(8,128)(2,1)S(1)}, u32[]{:S(2)}, u32[]{:S(2)}) collective-permute-start(bf16[32,2176]{1,0:T(8,128)(2,1)S(1)} %get-tuple-element.36), channel_id=1, source_target_pairs={{0,20},{4,16},{8,28},{12,24},{16,4},{20,0},{24,12},{28,8},{1,21},{... | collective-permute-start | bytes 417800 | tf_op jit(solution)/shard_map/ppermute | solution.py:21
  11.7 22.4 %collective-permute-start.18 = (bf16[64,2176]{1,0:T(8,128)(2,1)S(1)}, bf16[64,2176]{1,0:T(8,128)(2,1)S(1)}, u32[]{:S(2)}, u32[]{:S(2)}) collective-permute-start(bf16[64,2176]{1,0:T(8,128)(2,1)S(1)} %get-tuple-element.39), channel_id=1, source_target_pairs={{0,4},{4,0},{8,12},{12,8},{16,20},{20,16},{24,28},{28,24},{1,5},{5... | collective-permute-start | bytes 835592 | tf_op jit(solution)/shard_map/ppermute | solution.py:21
  13.3 21.3 %collective-permute-start.19 = (bf16[64,2176]{1,0:T(8,128)(2,1)S(1)}, bf16[64,2176]{1,0:T(8,128)(2,1)S(1)}, u32[]{:S(2)}, u32[]{:S(2)}) collective-permute-start(bf16[64,2176]{1,0:T(8,128)(2,1)S(1)} %get-tuple-element.40), channel_id=1, source_target_pairs={{0,8},{4,12},{8,0},{12,4},{16,24},{20,28},{24,16},{28,20},{1,9},{5... | collective-permute-start | bytes 835592 | tf_op jit(solution)/shard_map/ppermute | solution.py:21
  24.1 10.0 %collective-permute-start.2 = (bf16[64,2176]{1,0:T(8,128)(2,1)S(1)}, bf16[64,2176]{1,0:T(8,128)(2,1)S(1)}, u32[]{:S(2)}, u32[]{:S(2)}) collective-permute-start(bf16[64,2176]{1,0:T(8,128)(2,1)S(1)} %constant_dynamic-update-slice_fusion.refs_0_), channel_id=1, source_target_pairs={{0,2},{1,3},{2,0},{3,1},{4,6},{5,7},{6,4},{7,5},{8,10},{9,11},{10,... | collective-permute-start | bytes 835592 | tf_op jit(solution)/shard_map/ppermute | solution.py:26
  32.5 7.7 %collective-permute-start.11 = (bf16[64,2176]{1,0:T(8,128)(2,1)S(1)}, bf16[64,2176]{1,0:T(8,128)(2,1)S(1)}, u32[]{:S(2)}, u32[]{:S(2)}) collective-permute-start(bf16[64,2176]{1,0:T(8,128)(2,1)S(1)} %constant_dynamic-update-slice_fusion.2.refs_0_), channel_id=1, source_target_pairs={{0,2},{1,3},{2,0},{3,1},{4,6},{5,7},{6,4},{7,5},{8,10},{9,11},{10,... | collective-permute-start | bytes 835592 | tf_op jit(solution)/shard_map/ppermute | solution.py:26
  34.1 11.9 %collective-permute-start.20 = (bf16[64,2176]{1,0:T(8,128)(2,1)S(1)}, bf16[64,2176]{1,0:T(8,128)(2,1)S(1)}, u32[]{:S(2)}, u32[]{:S(2)}) collective-permute-start(bf16[64,2176]{1,0:T(8,128)(2,1)S(1)} %get-tuple-element.41), channel_id=1, source_target_pairs={{0,12},{4,8},{8,4},{12,0},{16,28},{20,24},{24,20},{28,16},{1,13},{... | collective-permute-start | bytes 835592 | tf_op jit(solution)/shard_map/ppermute | solution.py:21
  34.1 12.5 %collective-permute-start.3 = (bf16[64,2176]{1,0:T(8,128)(2,1)S(1)}, bf16[64,2176]{1,0:T(8,128)(2,1)S(1)}, u32[]{:S(2)}, u32[]{:S(2)}) collective-permute-start(bf16[64,2176]{1,0:T(8,128)(2,1)S(1)} %constant_dynamic-update-slice_fusion.refs_0_), channel_id=1, source_target_pairs={{0,1},{1,0},{2,3},{3,2},{4,5},{5,4},{6,7},{7,6},{8,9},{9,8},{10,11... | collective-permute-start | bytes 835592 | tf_op jit(solution)/shard_map/ppermute | solution.py:26
  34.2 12.6 %collective-permute-start.4 = (bf16[64,2176]{1,0:T(8,128)(2,1)S(1)}, bf16[64,2176]{1,0:T(8,128)(2,1)S(1)}, u32[]{:S(2)}, u32[]{:S(2)}) collective-permute-start(bf16[64,2176]{1,0:T(8,128)(2,1)S(1)} %collective-permute-done.2.refs_1_), channel_id=1, source_target_pairs={{0,1},{1,0},{2,3},{3,2},{4,5},{5,4},{6,7},{7,6},{8,9},{9,8},{10,11... | collective-permute-start | bytes 835592 | tf_op jit(solution)/shard_map/ppermute | solution.py:26
  34.7 15.7 %collective-permute-start.12 = (bf16[64,2176]{1,0:T(8,128)(2,1)S(1)}, bf16[64,2176]{1,0:T(8,128)(2,1)S(1)}, u32[]{:S(2)}, u32[]{:S(2)}) collective-permute-start(bf16[64,2176]{1,0:T(8,128)(2,1)S(1)} %constant_dynamic-update-slice_fusion.2.refs_0_), channel_id=1, source_target_pairs={{0,1},{1,0},{2,3},{3,2},{4,5},{5,4},{6,7},{7,6},{8,9},{9,8},{10,11... | collective-permute-start | bytes 835592 | tf_op jit(solution)/shard_map/ppermute | solution.py:26
  40.3 10.2 %collective-permute-start.13 = (bf16[64,2176]{1,0:T(8,128)(2,1)S(1)}, bf16[64,2176]{1,0:T(8,128)(2,1)S(1)}, u32[]{:S(2)}, u32[]{:S(2)}) collective-permute-start(bf16[64,2176]{1,0:T(8,128)(2,1)S(1)} %collective-permute-done.11.refs_1_), channel_id=1, source_target_pairs={{0,1},{1,0},{2,3},{3,2},{4,5},{5,4},{6,7},{7,6},{8,9},{9,8},{10,11... | collective-permute-start | bytes 835592 | tf_op jit(solution)/shard_map/ppermute | solution.py:26
  46.1 8.1 %collective-permute-start.21 = (bf16[64,2176]{1,0:T(8,128)(2,1)S(1)}, bf16[64,2176]{1,0:T(8,128)(2,1)S(1)}, u32[]{:S(2)}, u32[]{:S(2)}) collective-permute-start(bf16[64,2176]{1,0:T(8,128)(2,1)S(1)} %collective-permute-done.18.refs_0_), channel_id=1, source_target_pairs={{0,1},{1,0},{2,3},{3,2},{4,5},{5,4},{6,7},{7,6},{8,9},{9,8},{10,11... | collective-permute-start | bytes 835592 | tf_op jit(solution)/shard_map/ppermute | solution.py:26
  46.6 7.5 %collective-permute-start.22 = (bf16[64,2176]{1,0:T(8,128)(2,1)S(1)}, bf16[64,2176]{1,0:T(8,128)(2,1)S(1)}, u32[]{:S(2)}, u32[]{:S(2)}) collective-permute-start(bf16[64,2176]{1,0:T(8,128)(2,1)S(1)} %collective-permute-done.19.refs_1_), channel_id=1, source_target_pairs={{0,1},{1,0},{2,3},{3,2},{4,5},{5,4},{6,7},{7,6},{8,9},{9,8},{10,11... | collective-permute-start | bytes 835592 | tf_op jit(solution)/shard_map/ppermute | solution.py:26
  46.7 7.5 %collective-permute-start.23 = (bf16[64,2176]{1,0:T(8,128)(2,1)S(1)}, bf16[64,2176]{1,0:T(8,128)(2,1)S(1)}, u32[]{:S(2)}, u32[]{:S(2)}) collective-permute-start(bf16[64,2176]{1,0:T(8,128)(2,1)S(1)} %collective-permute-done.20.refs_2_), channel_id=1, source_target_pairs={{0,1},{1,0},{2,3},{3,2},{4,5},{5,4},{6,7},{7,6},{8,9},{9,8},{10,11... | collective-permute-start | bytes 835592 | tf_op jit(solution)/shard_map/ppermute | solution.py:26
  50.4 8.4 %collective-permute-start.5 = (bf16[128,2048]{1,0:T(8,128)(2,1)S(1)}, bf16[128,2048]{1,0:T(8,128)(2,1)S(1)}, u32[]{:S(2)}, u32[]{:S(2)}) collective-permute-start(bf16[128,2048]{1,0:T(8,128)(2,1)S(1)} %get-tuple-element.34), channel_id=1, source_target_pairs={{0,1},{1,0},{2,3},{3,2},{4,5},{5,4},{6,7},{7,6},{8,9},{9,8},{10,11... | collective-permute-start | bytes 1572872 | tf_op jit(solution)/shard_map/ppermute | solution.py:26
  53.7 6.9 %collective-permute-start.14 = (bf16[128,2048]{1,0:T(8,128)(2,1)S(1)}, bf16[128,2048]{1,0:T(8,128)(2,1)S(1)}, u32[]{:S(2)}, u32[]{:S(2)}) collective-permute-start(bf16[128,2048]{1,0:T(8,128)(2,1)S(1)} %get-tuple-element.38), channel_id=1, source_target_pairs={{0,1},{1,0},{2,3},{3,2},{4,5},{5,4},{6,7},{7,6},{8,9},{9,8},{10,11... | collective-permute-start | bytes 1572872 | tf_op jit(solution)/shard_map/ppermute | solution.py:26
  58.6 2.7 %collective-permute-start.24 = (bf16[192,2048]{1,0:T(8,128)(2,1)S(1)}, bf16[192,2048]{1,0:T(8,128)(2,1)S(1)}, u32[]{:S(2)}, u32[]{:S(2)}) collective-permute-start(bf16[192,2048]{1,0:T(8,128)(2,1)S(1)} %get-tuple-element.43), channel_id=1, source_target_pairs={{0,1},{1,0},{2,3},{3,2},{4,5},{5,4},{6,7},{7,6},{8,9},{9,8},{10,11... | collective-permute-start | bytes 2359304 | tf_op jit(solution)/shard_map/ppermute | solution.py:26
  59.0 9.2 %collective-permute-start.6 = (bf16[64,2048]{1,0:T(8,128)(2,1)S(1)}, bf16[64,2048]{1,0:T(8,128)(2,1)S(1)}, u32[]{:S(2)}, u32[]{:S(2)}) collective-permute-start(bf16[64,2048]{1,0:T(8,128)(2,1)S(1)} %slice.82), channel_id=1, source_target_pairs={{0,2},{1,3},{2,0},{3,1},{4,6},{5,7},{6,4},{7,5},{8,10},{9,11},{10,... | collective-permute-start | bytes 786440 | tf_op jit(solution)/shard_map/ppermute | solution.py:26
  60.7 12.5 %collective-permute-start.15 = (bf16[64,2048]{1,0:T(8,128)(2,1)S(1)}, bf16[64,2048]{1,0:T(8,128)(2,1)S(1)}, u32[]{:S(2)}, u32[]{:S(2)}) collective-permute-start(bf16[64,2048]{1,0:T(8,128)(2,1)S(1)} %slice.81), channel_id=1, source_target_pairs={{0,2},{1,3},{2,0},{3,1},{4,6},{5,7},{6,4},{7,5},{8,10},{9,11},{10,... | collective-permute-start | bytes 786440 | tf_op jit(solution)/shard_map/ppermute | solution.py:26
  61.6 14.1 %collective-permute-start.25 = (bf16[64,2048]{1,0:T(8,128)(2,1)S(1)}, bf16[64,2048]{1,0:T(8,128)(2,1)S(1)}, u32[]{:S(2)}, u32[]{:S(2)}) collective-permute-start(bf16[64,2048]{1,0:T(8,128)(2,1)S(1)} %get-tuple-element.49), channel_id=1, source_target_pairs={{0,4},{4,0},{8,12},{12,8},{16,20},{20,16},{24,28},{28,24},{1,5},{5... | collective-permute-start | bytes 786440 | tf_op jit(solution)/shard_map/ppermute | solution.py:21
  62.2 13.5 %collective-permute-start.26 = (bf16[64,2048]{1,0:T(8,128)(2,1)S(1)}, bf16[64,2048]{1,0:T(8,128)(2,1)S(1)}, u32[]{:S(2)}, u32[]{:S(2)}) collective-permute-start(bf16[64,2048]{1,0:T(8,128)(2,1)S(1)} %get-tuple-element.48), channel_id=1, source_target_pairs={{0,8},{4,12},{8,0},{12,4},{16,24},{20,28},{24,16},{28,20},{1,9},{5... | collective-permute-start | bytes 786440 | tf_op jit(solution)/shard_map/ppermute | solution.py:21
  62.7 18.9 %collective-permute-start.27 = (bf16[64,2048]{1,0:T(8,128)(2,1)S(1)}, bf16[64,2048]{1,0:T(8,128)(2,1)S(1)}, u32[]{:S(2)}, u32[]{:S(2)}) collective-permute-start(bf16[64,2048]{1,0:T(8,128)(2,1)S(1)} %get-tuple-element.47), channel_id=1, source_target_pairs={{0,12},{4,8},{8,4},{12,0},{16,28},{20,24},{24,20},{28,16},{1,13},{... | collective-permute-start | bytes 786440 | tf_op jit(solution)/shard_map/ppermute | solution.py:21
  68.3 13.3 %collective-permute-start.7 = (bf16[32,2048]{1,0:T(8,128)(2,1)S(1)}, bf16[32,2048]{1,0:T(8,128)(2,1)S(1)}, u32[]{:S(2)}, u32[]{:S(2)}) collective-permute-start(bf16[32,2048]{1,0:T(8,128)(2,1)S(1)} %get-tuple-element.53), channel_id=1, source_target_pairs={{0,24},{4,28},{8,16},{12,20},{16,8},{20,12},{24,0},{28,4},{1,25},{... | collective-permute-start | bytes 393224 | tf_op jit(solution)/shard_map/ppermute | solution.py:21
  73.3 11.3 %collective-permute-start.8 = (bf16[32,2048]{1,0:T(8,128)(2,1)S(1)}, bf16[32,2048]{1,0:T(8,128)(2,1)S(1)}, u32[]{:S(2)}, u32[]{:S(2)}) collective-permute-start(bf16[32,2048]{1,0:T(8,128)(2,1)S(1)} %get-tuple-element.52), channel_id=1, source_target_pairs={{0,28},{4,24},{8,20},{12,16},{16,12},{20,8},{24,4},{28,0},{1,29},{... | collective-permute-start | bytes 393224 | tf_op jit(solution)/shard_map/ppermute | solution.py:21
  75.7 17.1 %collective-permute-start.16 = (bf16[32,2048]{1,0:T(8,128)(2,1)S(1)}, bf16[32,2048]{1,0:T(8,128)(2,1)S(1)}, u32[]{:S(2)}, u32[]{:S(2)}) collective-permute-start(bf16[32,2048]{1,0:T(8,128)(2,1)S(1)} %get-tuple-element.51), channel_id=1, source_target_pairs={{0,16},{4,20},{8,24},{12,28},{16,0},{20,4},{24,8},{28,12},{1,17},{... | collective-permute-start | bytes 393224 | tf_op jit(solution)/shard_map/ppermute | solution.py:21
  75.8 20.1 %collective-permute-start.17 = (bf16[32,2048]{1,0:T(8,128)(2,1)S(1)}, bf16[32,2048]{1,0:T(8,128)(2,1)S(1)}, u32[]{:S(2)}, u32[]{:S(2)}) collective-permute-start(bf16[32,2048]{1,0:T(8,128)(2,1)S(1)} %get-tuple-element.50), channel_id=1, source_target_pairs={{0,20},{4,16},{8,28},{12,24},{16,4},{20,0},{24,12},{28,8},{1,21},{... | collective-permute-start | bytes 393224 | tf_op jit(solution)/shard_map/ppermute | solution.py:21
  97.3 2.0 %collective-permute-start.28 = (bf16[128,2048]{1,0:T(8,128)(2,1)S(1)}, bf16[128,2048]{1,0:T(8,128)(2,1)S(1)}, u32[]{:S(2)}, u32[]{:S(2)}) collective-permute-start(bf16[128,2048]{1,0:T(8,128)(2,1)S(1)} %get-tuple-element.46), channel_id=1, source_target_pairs={{0,1},{1,0},{2,3},{3,2},{4,5},{5,4},{6,7},{7,6},{8,9},{9,8},{10,11... | collective-permute-start | bytes 1572872 | tf_op jit(solution)/shard_map/ppermute | solution.py:26
  99.5 8.4 %collective-permute-start.29 = (bf16[64,2048]{1,0:T(8,128)(2,1)S(1)}, bf16[64,2048]{1,0:T(8,128)(2,1)S(1)}, u32[]{:S(2)}, u32[]{:S(2)}) collective-permute-start(bf16[64,2048]{1,0:T(8,128)(2,1)S(1)} %slice.80), channel_id=1, source_target_pairs={{0,2},{1,3},{2,0},{3,1},{4,6},{5,7},{6,4},{7,5},{8,10},{9,11},{10,... | collective-permute-start | bytes 786440 | tf_op jit(solution)/shard_map/ppermute | solution.py:26

commit v2 on v1

--- a/solution.py
+++ b/solution.py
@@ -45,7 +45,7 @@
 
 def route_kernel(pieces, node_count, s_ref, ids_hbm, score_hbm, tok_hbm, *refs):
     outs = refs[: len(pieces)]
-    oh_ref, hot, rows, ids_ref, score_ref, tok_ref, sems = refs[len(pieces):]
+    late_ref, early_ref, hot, rows, ids_ref, score_ref, tok_ref, sems = refs[len(pieces):]
     copies = [
         pltpu.make_async_copy(src, dst, sems.at[i])
         for i, (src, dst) in enumerate(((ids_hbm, ids_ref), (score_hbm, score_ref), (tok_hbm, tok_ref)))
@@ -80,7 +80,9 @@
         hot[offset : offset + count, :] = jnp.where(position[k : k + 1] == slot, 1.0, 0.0)
         offset += count
     one_hot = hot[...].astype(BF16)
-    oh_ref[...] = one_hot
+    split = late_ref.shape[0]
+    late_ref[...] = hot[:split, :].astype(BF16)
+    early_ref[...] = hot[split:, :].astype(BF16)
     high = weight.astype(BF16)
     low = (weight - high.astype(F32)).astype(BF16)
     extra = outs[0].shape[1] - width
@@ -105,12 +107,13 @@
     experts = node_count * E_NODE
     full = width + -(-2 * experts // LANES) * LANES
     total = sum(p[2] for p in pieces)
+    tail = sum(p[2] for p in pieces[-2:])
     res = pl.pallas_call(
         functools.partial(route_kernel, pieces, node_count),
         out_shape=[jax.ShapeDtypeStruct((p[2], full), BF16) for p in pieces]
-        + [jax.ShapeDtypeStruct((total, tok_rows), BF16)],
+        + [jax.ShapeDtypeStruct((count, tok_rows), BF16) for count in (total - tail, tail)],
         in_specs=[SMEM, HBM, HBM, HBM],
-        out_specs=[VMEM] * (len(pieces) + 1),
+        out_specs=[VMEM] * (len(pieces) + 2),
         scratch_shapes=[
             pltpu.VMEM((total, tok_rows), F32),
             pltpu.VMEM((total, 512), F32),
@@ -123,7 +126,7 @@
         cost_estimate=cost(2 * total * tok_rows * full, 2 * (tok_rows * width + total * full)),
         name="route",
     )(scalars, ids, scores, tokens)
-    return res[:-1], res[-1]
+    return res[:-2], res[-2], res[-1]
 
 
 def hidden_block(hidden):
@@ -133,13 +136,13 @@
     return hidden
 
 
-def ffn_kernel(counts, experts, keep_rows, s_ref, *refs):
+def ffn_kernel(counts, experts, ranges, s_ref, *refs):
     n = len(counts)
     xs = refs[:n]
     wg_ref, wu_ref, wd_ref = refs[n : n + 3]
     outs = refs[n + 3 : -2]
     x, wcol = refs[-2:]
-    total, width = x.shape
+    _, width = x.shape
     expert = s_ref[2]
     extra = xs[0].shape[1] - width
     lane = lax.broadcasted_iota(jnp.int32, (1, extra), 1)
@@ -159,22 +162,23 @@
     scale = wcol[...]
     for c, w in column_blocks(width):
         part = jnp.dot(hidden, wd_ref[0, :, c : c + w], preferred_element_type=F32) * scale
-        outs[0][:, c : c + w] = part[:keep_rows].astype(outs[0].dtype)
-        if keep_rows < total:
-            outs[1][:, c : c + w] = part[keep_rows:].astype(outs[1].dtype)
-
-
-def ffn(scalars, xs, w_gate, w_up, w_down, experts, split):
+        for out, (first, last) in zip(outs, ranges):
+            out[:, c : c + w] = part[first:last].astype(out.dtype)
+
+
+def ffn(scalars, xs, w_gate, w_up, w_down, experts, groups):
     counts = [x.shape[0] for x in xs]
     total = sum(counts)
     width, hidden = w_gate.shape[1:]
-    keep = total // 2 if split else total
-    shapes = [jax.ShapeDtypeStruct((keep, width), F32 if split else BF16)]
-    if split:
-        shapes.append(jax.ShapeDtypeStruct((total - keep, width), BF16))
+    shapes, ranges, done = [], [], 0
+    for number, dtype in groups:
+        first = sum(counts[:done])
+        done += number
+        ranges.append((first, sum(counts[:done])))
+        shapes.append(jax.ShapeDtypeStruct((ranges[-1][1] - first, width), dtype))
     packed = all(c % 16 == 0 for c in counts)
     return pl.pallas_call(
-        functools.partial(ffn_kernel, counts, experts, keep),
+        functools.partial(ffn_kernel, counts, experts, ranges),
         out_shape=shapes,
         in_specs=[SMEM] + [VMEM] * (len(xs) + 3),
         out_specs=[VMEM] * len(shapes),
@@ -187,18 +191,31 @@
     )(scalars, *xs, w_gate, w_up, w_down)
 
 
-def shared_kernel(x_ref, wg_ref, wu_ref, wd_ref, eg_hbm, eu_hbm, ed_hbm, out_ref, eg_ref, eu_ref, ed_ref, sems):
+def stage_kernel(*refs):
+    count = len(refs) // 2
+    sems = refs[-1]
+    copies = [pltpu.make_async_copy(refs[i], refs[count + i], sems.at[i]) for i in range(count)]
+    for copy in copies:
+        copy.start()
+    for copy in copies:
+        copy.wait()
+
+
+def stage(weights):
+    return pl.pallas_call(
+        stage_kernel,
+        out_shape=[jax.ShapeDtypeStruct(w.shape, w.dtype) for w in weights],
+        in_specs=[HBM] * len(weights),
+        out_specs=[VMEM] * len(weights),
+        scratch_shapes=[pltpu.SemaphoreType.DMA((len(weights),))],
+        compiler_params=params(),
+        cost_estimate=cost(0, sum(4 * w.size for w in weights)),
+        name="stage",
+    )(*weights)
+
+
+def shared_kernel(x_ref, wg_ref, wu_ref, wd_ref, out_ref):
     step = pl.program_id(0)
-    staged = [
-        pltpu.make_async_copy(src, dst, sems.at[i])
-        for i, (src, dst) in enumerate(((eg_hbm, eg_ref), (eu_hbm, eu_ref), (ed_hbm, ed_ref)))
-    ]
-
-    @pl.when(step == 0)
-    def _():
-        for copy in staged:
-            copy.start()
-
     rows = x_ref[...]
     gate = jnp.dot(rows, wg_ref[...], preferred_element_type=F32)
     up = jnp.dot(rows, wu_ref[...], preferred_element_type=F32)
@@ -214,87 +231,89 @@
         def _():
             out_ref[:, c : c + w] += part
 
-    @pl.when(step == pl.num_programs(0) - 1)
-    def _():
-        for copy in staged:
-            copy.wait()
-
-
-def shared(tokens, w_gate, w_up, w_down, staged):
+
+def shared(tokens, w_gate, w_up, w_down):
     rows, width = tokens.shape
     hidden = w_gate.shape[1]
     block = hidden_block(hidden)
     return pl.pallas_call(
         shared_kernel,
         grid=(hidden // block,),
-        out_shape=[jax.ShapeDtypeStruct((rows, width), F32)] + [jax.ShapeDtypeStruct(w.shape, w.dtype) for w in staged],
+        out_shape=jax.ShapeDtypeStruct((rows, width), F32),
         in_specs=[
             pl.BlockSpec((rows, width), lambda f: (0, 0)),
             pl.BlockSpec((width, block), lambda f: (0, f)),
             pl.BlockSpec((width, block), lambda f: (0, f)),
             pl.BlockSpec((block, width), lambda f: (f, 0)),
-            HBM,
-            HBM,
-            HBM,
         ],
-        out_specs=[pl.BlockSpec((rows, width), lambda f: (0, 0)), VMEM, VMEM, VMEM],
-        scratch_shapes=[pltpu.SemaphoreType.DMA((3,))],
+        out_specs=pl.BlockSpec((rows, width), lambda f: (0, 0)),
         compiler_params=params(),
-        cost_estimate=cost(
-            6 * rows * width * hidden,
-            6 * width * hidden + 6 * rows * width + sum(4 * w.size for w in staged),
-            rows * hidden,
-        ),
+        cost_estimate=cost(6 * rows * width * hidden, 6 * width * hidden + 6 * rows * width, rows * hidden),
         name="shared",
-    )(tokens, w_gate, w_up, w_down, *staged)
-
-
-def combine_kernel(counts, order, s_ref, oh_ref, shared_ref, *refs):
-    n = len(counts)
-    parts = refs[:n]
-    keep_ref, send_ref, slots, acc = refs[n:]
-    tok_rows, width = shared_ref.shape
+    )(tokens, w_gate, w_up, w_down)
+
+
+def token_blocks(acc, order, s_ref):
+    rows = acc.shape[0] // len(order)
+    for j, rel in enumerate(order):
+        start = pl.multiple_of((s_ref[1] ^ rel) * rows, rows)
+        yield j, j * rows, acc[pl.ds(start, rows), :]
+
+
+def gathered(oh_ref, parts, counts, slots, acc):
     offset = 0
     for ref, count in zip(parts, counts):
         slots[offset : offset + count, :] = ref[...].astype(slots.dtype)
         offset += count
-    one_hot = oh_ref[...]
-    for c, w in column_blocks(width):
+    for c, w in column_blocks(acc.shape[1]):
         acc[:, c : c + w] = lax.dot_general(
-            one_hot, slots[:, c : c + w].astype(BF16), (((0,), (0,)), ((), ())), preferred_element_type=F32
+            oh_ref[...], slots[:, c : c + w].astype(BF16), (((0,), (0,)), ((), ())), preferred_element_type=F32
         )
-    block = tok_rows // len(order)
-    half = len(order) // 2
-    for j, rel in enumerate(order):
-        start = pl.multiple_of((s_ref[1] ^ rel) * block, block)
-        value = acc[pl.ds(start, block), :] + shared_ref[pl.ds(start, block), :]
-        if j < half:
-            keep_ref[j * block : (j + 1) * block, :] = value
+
+
+def early_kernel(counts, order, s_ref, oh_ref, shared_ref, *refs):
+    n = len(counts)
+    out_ref, slots, acc = refs[n:]
+    gathered(oh_ref, refs[:n], counts, slots, acc)
+    acc[...] = acc[...] + shared_ref[...]
+    for j, at, value in token_blocks(acc, order, s_ref):
+        out_ref[at : at + value.shape[0], :] = value
+
+
+def combine_kernel(counts, order, s_ref, oh_ref, base_ref, *refs):
+    n = len(counts)
+    keep_ref, send_ref, slots, acc = refs[n:]
+    gathered(oh_ref, refs[:n], counts, slots, acc)
+    kept = keep_ref.shape[0]
+    for j, at, value in token_blocks(acc, order, s_ref):
+        value = value + base_ref[at : at + value.shape[0], :]
+        if at < kept:
+            keep_ref[at : at + value.shape[0], :] = value
         else:
-            send_ref[(j - half) * block : (j - half + 1) * block, :] = value.astype(BF16)
-
-
-def combine(scalars, one_hot, shared_part, parts, order):
+            send_ref[at - kept : at - kept + value.shape[0], :] = value.astype(BF16)
+
+
+def combine(scalars, one_hot, base, parts, order, final):
     counts = [p.shape[0] for p in parts]
-    tok_rows, width = shared_part.shape
+    tok_rows, width = base.shape
     total = sum(counts)
     packed = all(c % 16 == 0 for c in counts)
+    if final:
+        shapes = [jax.ShapeDtypeStruct((tok_rows // 2, width), t) for t in (F32, BF16)]
+    else:
+        shapes = [jax.ShapeDtypeStruct((tok_rows, width), F32)]
     return pl.pallas_call(
-        functools.partial(combine_kernel, counts, order),
-        out_shape=[
-            jax.ShapeDtypeStruct((tok_rows // 2, width), F32),
-            jax.ShapeDtypeStruct((tok_rows // 2, width), BF16),
-        ],
+        functools.partial(combine_kernel if final else early_kernel, counts, order),
+        out_shape=shapes,
         in_specs=[SMEM] + [VMEM] * (len(parts) + 2),
-        out_specs=[VMEM, VMEM],
+        out_specs=[VMEM] * len(shapes),
         scratch_shapes=[
             pltpu.VMEM((total, width), BF16 if packed else F32),
             pltpu.VMEM((tok_rows, width), F32),
         ],
         compiler_params=params(),
         cost_estimate=cost(2 * total * tok_rows * width, 2 * total * width + 7 * tok_rows * width),
-        name="combine",
-    )(scalars, one_hot, shared_part, *parts)
+    )(scalars, one_hot, base, *parts)
 
 
 def fold(value, bits):
@@ -330,9 +349,9 @@
     chunks = far_chunks(node_count)
     near = [k for k in range(1, NEAR)]
     pieces = [(k, 1, capacity // local_count) for ks in chunks for k in ks]
-    pieces += [(k, 3, capacity // 2) for k in near] + [(0, None, capacity)]
+    pieces += [(k, 3, capacity // 2) for k in near[1:] + near[:1]] + [(0, None, capacity)]
     in_hbm = functools.partial(pltpu.with_memory_space_constraint, memory_space=pltpu.HBM)
-    sends, one_hot = route(
+    sends, late_hot, early_hot = route(
         scalars, in_hbm(expert_ids.T), in_hbm(gate_scores.T), in_hbm(tokens), tuple(pieces), node_count
     )
     weights = [pltpu.with_memory_space_constraint(w, pltpu.HBM) for w in (expert_gate, expert_up, expert_down)]
@@ -349,13 +368,14 @@
             index += 1
         arrived.append(got)
     near_in = []
-    for k in near:
+    for k in near[1:] + near[:1]:
         near_in.append(xor_node(sends[index], k))
         index += 1
+    near_in = near_in[-1:] + near_in[:-1]
     own_rows = sends[-1]
 
-    shared_part, *weights = shared(tokens, shared_gate, shared_up, shared_down, weights)
-    own_out = ffn(scalars, [own_rows], *weights, experts, False)[0]
+    shared_part = shared(in_hbm(tokens), shared_gate, shared_up, shared_down)
+    weights = stage(weights)
 
     def gather(got):
         rows = [jnp.concatenate(got, axis=0) if len(got) > 1 else got[0]]
@@ -363,15 +383,24 @@
             rows = rows + [xor_local(r, bit) for r in rows]
         return rows + [xor_local(r, 1) for r in rows]
 
+    def summed(keep, send):
+        return keep + xor_local(send, 1).astype(F32)
+
     def experts_of(rows):
-        keep, send = ffn(scalars, rows, *weights, experts, True)
-        return keep + xor_local(send, 1).astype(F32)
-
-    near_rows = near_in + [xor_local(r, 1) for r in near_in]
+        half = len(rows) // 2
+        keep, send = ffn(scalars, rows, *weights, experts, ((half, F32), (half, BF16)))
+        return summed(keep, send)
+
+    partner = xor_local(near_in[0], 1)
+    rows = [own_rows, near_in[0], partner]
+    own_out, keep, send = ffn(scalars, rows, *weights, experts, ((1, BF16), (1, F32), (1, BF16)))
+    near_sum = summed(keep, send).astype(BF16)
+    near_back = [xor_node(near_sum, 1)]
+
+    near_rows = near_in[1:] + [xor_local(r, 1) for r in near_in[1:]]
     near_sum = experts_of(near_rows).astype(BF16)
-    count = near_sum.shape[0] // len(near)
-    near_back = []
-    for i, k in enumerate(near):
+    count = near_sum.shape[0] // len(near_in[1:])
+    for i, k in enumerate(near[1:]):
         near_back.append(xor_node(near_sum[i * count : (i + 1) * count], k))
     returned = []
     for ks, got in zip(chunks, arrived):
@@ -385,7 +414,9 @@
     for bit in slow_bits:
         order = order + [i ^ bit for i in order]
     order = order + [i ^ 1 for i in order]
-    keep, send = combine(scalars, one_hot, shared_part, returned + near_back + [own_out], tuple(order))
+    base = combine(scalars, early_hot, shared_part, [near_back[0], own_out], tuple(order), False)[0]
+    parts = returned + near_back[1:]
+    keep, send = combine(scalars, late_hot, base, parts, tuple(order), True)
     value = keep + xor_local(send, 1).astype(F32)
     return fold(value, slow_bits[::-1]).astype(BF16)
 

time: 109 us -> 108 us (level)
  the two profiles are of different devices: /device:TPU:0 before, /device:TPU:16 now
where the time goes in v2:
time: 108 us
  waiting for transfers between devices  50.9 us (47%)
  starting transfers between devices  27.8 us (26%)
  Pallas kernels  27.3 us (25%)
  other arithmetic  1.48 us (1%)
    ppermute x14, waiting for transfers between devices, xor_node(): return lax.ppermute(x, 'node', [(i, i ^ k) for i in range(count)])  29.3 us
    ppermute x17, waiting for transfers between devices, xor_local(): return lax.ppermute(x, 'local', [(i, i ^ k) for i in range(count)])  21.6 us
    ppermute x14, starting transfers between devices, xor_node(): return lax.ppermute(x, 'node', [(i, i ^ k) for i in range(count)])  19 us
    pallas_call x4, Pallas kernels, ffn(): pl.pallas_call(functools.partial(ffn_kernel, counts, experts, ranges), ou...  12.7 us
    ppermute x17, starting transfers between devices, xor_local(): return lax.ppermute(x, 'local', [(i, i ^ k) for i in range(count)])  8.84 us
    pallas_call x1, Pallas kernels, shared(): pl.pallas_call(shared_kernel, grid=(hidden // block,), out_shape=jax.Shap...  5.93 us
    pallas_call x1, Pallas kernels, stage(): pl.pallas_call(stage_kernel, out_shape=[jax.ShapeDtypeStruct(w.shape, w.d...  3.78 us
    pallas_call x1, Pallas kernels, route(): pl.pallas_call(functools.partial(route_kernel, pieces, node_count), out_s...  2.55 us
  transfers between devices with their start and end apart: 31, of which 11 were waited for; matrix products, arithmetic and copies ran while one was open for 1% of the time, Pallas kernels for 22%

profile of v2, /device:TPU:16, one launch (start us, length us, event | category | flops | bytes accessed | tf_op | source)
XLA Modules:
  0.0 108.1 jit_solution(4298718609057278285)
XLA Ops:
  0.1 2.6 %route.1 = (bf16[32,2176]{1,0:T(8,128)(2,1)S(1)}, bf16[32,2176]{1,0:T(8,128)(2,1)S(1)}, bf16[32,2176]{1,0:T(8,128)(2,1)S(1)}, bf16[32,2176]{1,0:T(8,128)(2,1)S(1...) custom-call(s32[4]{0:T(128)S(1)} %pad_add_fusion.s_ref, ...), custom_call_target="tpu_custom_call" | custom-call | flops 499122176 | bytes 2998272 | tf_op jit(solution)/shard_map/route/pallas_call | solution.py:111
  2.7 1.9 %collective-permute-start.22 = (bf16[64,2176]{1,0:T(8,128)(2,1)S(1)}, bf16[64,2176]{1,0:T(8,128)(2,1)S(1)}, u32[]{:S(2)}, u32[]{:S(2)}) collective-permute-start(bf16[64,2176]{1,0:T(8,128)(2,1)S(1)} %get-tuple-element.47), channel_id=1, source_target_pairs={{0,8},{4,12},{8,0},{12,4},{16,24},{20,28},{24,16},{28,20},{1,9},{5... | collective-permute-start | bytes 835592 | tf_op jit(solution)/shard_map/ppermute | solution.py:21
  4.6 1.4 %collective-permute-start.23 = (bf16[64,2176]{1,0:T(8,128)(2,1)S(1)}, bf16[64,2176]{1,0:T(8,128)(2,1)S(1)}, u32[]{:S(2)}, u32[]{:S(2)}) collective-permute-start(bf16[64,2176]{1,0:T(8,128)(2,1)S(1)} %get-tuple-element.48), channel_id=1, source_target_pairs={{0,12},{4,8},{8,4},{12,0},{16,28},{20,24},{24,20},{28,16},{1,13},{... | collective-permute-start | bytes 835592 | tf_op jit(solution)/shard_map/ppermute | solution.py:21
  6.0 2.6 %collective-permute-start.14 = (bf16[32,2176]{1,0:T(8,128)(2,1)S(1)}, bf16[32,2176]{1,0:T(8,128)(2,1)S(1)}, u32[]{:S(2)}, u32[]{:S(2)}) collective-permute-start(bf16[32,2176]{1,0:T(8,128)(2,1)S(1)} %get-tuple-element.44), channel_id=1, source_target_pairs={{0,20},{4,16},{8,28},{12,24},{16,4},{20,0},{24,12},{28,8},{1,21},{... | collective-permute-start | bytes 417800 | tf_op jit(solution)/shard_map/ppermute | solution.py:21
  9.0 1.2 %collective-permute-done.13 = bf16[32,2176]{1,0:T(8,128)(2,1)S(1)} collective-permute-done((bf16[32,2176]{1,0:T(8,128)(2,1)S(1)}, bf16[32,2176]{1,0:T(8,128)(2,1)S(1)}, u32[]{:S(2)}, u32[]{:S(2)}) %collective-permute-start.13) | collective-permute-done | bytes 139296 | tf_op jit(solution)/shard_map/ppermute | solution.py:21
  10.2 2.4 %collective-permute-start.5 = (bf16[32,2176]{1,0:T(8,128)(2,1)S(1)}, bf16[32,2176]{1,0:T(8,128)(2,1)S(1)}, u32[]{:S(2)}, u32[]{:S(2)}) collective-permute-start(bf16[32,2176]{1,0:T(8,128)(2,1)S(1)} %get-tuple-element.40), channel_id=1, source_target_pairs={{0,28},{4,24},{8,20},{12,16},{16,12},{20,8},{24,4},{28,0},{1,29},{... | collective-permute-start | bytes 417800 | tf_op jit(solution)/shard_map/ppermute | solution.py:21
  12.6 15.7 %collective-permute-done.14 = bf16[32,2176]{1,0:T(8,128)(2,1)S(1)} collective-permute-done((bf16[32,2176]{1,0:T(8,128)(2,1)S(1)}, bf16[32,2176]{1,0:T(8,128)(2,1)S(1)}, u32[]{:S(2)}, u32[]{:S(2)}) %collective-permute-start.14) | collective-permute-done | bytes 139296 | tf_op jit(solution)/shard_map/ppermute | solution.py:21
  29.0 1.5 %collective-permute-start.15 = (bf16[64,2176]{1,0:T(8,128)(2,1)S(1)}, bf16[64,2176]{1,0:T(8,128)(2,1)S(1)}, u32[]{:S(2)}, u32[]{:S(2)}) collective-permute-start(bf16[64,2176]{1,0:T(8,128)(2,1)S(1)} %constant_dynamic-update-slice_fusion.2.refs_0_), channel_id=1, source_target_pairs={{0,2},{1,3},{2,0},{3,1},{4,6},{5,7},{6,4},{7,5},{8,10},{9,11},{10,... | collective-permute-start | bytes 835592 | tf_op jit(solution)/shard_map/ppermute | solution.py:26
  31.7 3.2 %collective-permute-done.refs_1_ = bf16[64,2176]{1,0:T(8,128)(2,1)S(1)} collective-permute-done((bf16[64,2176]{1,0:T(8,128)(2,1)S(1)}, bf16[64,2176]{1,0:T(8,128)(2,1)S(1)}, u32[]{:S(2)}, u32[]{:S(2)}) %collective-permute-start) | collective-permute-done | bytes 278560 | tf_op jit(solution)/shard_map/ppermute | solution.py:21
  34.9 3.8 %stage.1 = (bf16[1,2048,768]{2,1,0:T(8,128)(2,1)S(1)}, bf16[1,2048,768]{2,1,0:T(8,128)(2,1)S(1)}, bf16[1,768,2048]{2,1,0:T(8,128)(2,1)S(1)}) custom-call(bf16[1,2048,768]{2,1,0:T(8,128)(2,1)} %refs_0_.1, bf16[1,2048,768]{2,1,0:T(8,128)(2,1)} %refs_1_.1, bf16[1,768,2048]{2,1,0:T(8,128)(2,1)} %refs_2_.1), custom_call_target="tpu_custom_call" | custom-call | bytes 18874368 | tf_op jit(solution)/shard_map/stage/pallas_call | solution.py:205
  39.2 1.9 %collective-permute-done.6.refs_1_ = bf16[64,2176]{1,0:T(8,128)(2,1)S(1)} collective-permute-done((bf16[64,2176]{1,0:T(8,128)(2,1)S(1)}, bf16[64,2176]{1,0:T(8,128)(2,1)S(1)}, u32[]{:S(2)}, u32[]{:S(2)}) %collective-permute-start.6) | collective-permute-done | bytes 278560 | tf_op jit(solution)/shard_map/ppermute | solution.py:26
  41.7 3.2 %shard_map.95 = (f32[128,2048]{1,0:T(8,128)S(1)}, bf16[128,2048]{1,0:T(8,128)(2,1)S(1)}) custom-call(s32[4]{0:T(128)S(1)} %pad_add_fusion.s_ref, bf16[64,2176]{1,0:T(8,128)(2,1)S(1)} %collective-permute-done.22.refs_0_, bf16[64,2176]{1,0:T(8,128)(2,1)S(1)} %collective-permute-done.23.refs_1_, bf16[64,2176]{1,0:T(8,128)(2,1)S(1)} %collective-permute-done.24.refs_2_, ...), custom_call_target="tpu_custom_call" | custom-call | flops 2415919104 | bytes 12582912 | tf_op jit(solution)/shard_map/pallas_call | solution.py:180
  45.4 3.2 %shard_map.91 = (bf16[128,2048]{1,0:T(8,128)(2,1)S(1)}, f32[64,2048]{1,0:T(8,128)S(1)}, bf16[64,2048]{1,0:T(8,128)(2,1)S(1)}) custom-call(s32[4]{0:T(128)S(1)} %pad_add_fusion.s_ref, bf16[128,2176]{1,0:T(8,128)(2,1)S(1)} %get-tuple-element.31.refs_0_, bf16[64,2176]{1,0:T(8,128)(2,1)S(1)} %collective-permute-done.refs_1_, ...), custom_call_target="tpu_custom_call" | custom-call | flops 2415919104 | bytes 12582912 | tf_op jit(solution)/shard_map/pallas_call | solution.py:180
  48.7 3.2 %shard_map.94 = (f32[128,2048]{1,0:T(8,128)S(1)}, bf16[128,2048]{1,0:T(8,128)(2,1)S(1)}) custom-call(s32[4]{0:T(128)S(1)} %pad_add_fusion.s_ref, bf16[64,2176]{1,0:T(8,128)(2,1)S(1)} %constant_dynamic-update-slice_fusion.2.refs_0_, bf16[64,2176]{1,0:T(8,128)(2,1)S(1)} %collective-permute-done.15.refs_1_, ...), custom_call_target="tpu_custom_call" | custom-call | flops 2415919104 | bytes 12582912 | tf_op jit(solution)/shard_map/pallas_call | solution.py:180
  52.4 3.2 %shard_map.93 = (f32[128,2048]{1,0:T(8,128)S(1)}, bf16[128,2048]{1,0:T(8,128)(2,1)S(1)}) custom-call(s32[4]{0:T(128)S(1)} %pad_add_fusion.s_ref, bf16[64,2176]{1,0:T(8,128)(2,1)S(1)} %constant_dynamic-update-slice_fusion.refs_0_, bf16[64,2176]{1,0:T(8,128)(2,1)S(1)} %collective-permute-done.6.refs_1_, bf16[64,2176]{1,0:T(8,128)(2,1)S(1)} %collective-permute-done.7.refs_2_, ...), custom_call_target="tpu_custom_call" | custom-call | flops 2415919104 | bytes 12582912 | tf_op jit(solution)/shard_map/pallas_call | solution.py:180
  55.8 1.5 %collective-permute-start.3 = (bf16[64,2048]{1,0:T(8,128)(2,1)S(1)}, bf16[64,2048]{1,0:T(8,128)(2,1)S(1)}, u32[]{:S(2)}, u32[]{:S(2)}) collective-permute-start(bf16[64,2048]{1,0:T(8,128)(2,1)S(1)} %add_convert_fusion.1), channel_id=1, source_target_pairs={{0,4},{4,0},{8,12},{12,8},{16,20},{20,16},{24,28},{28,24},{1,5},{5... | collective-permute-start | bytes 786440 | tf_op jit(solution)/shard_map/ppermute | solution.py:21
  57.4 3.4 %collective-permute-start.27 = (bf16[64,2048]{1,0:T(8,128)(2,1)S(1)}, bf16[64,2048]{1,0:T(8,128)(2,1)S(1)}, u32[]{:S(2)}, u32[]{:S(2)}) collective-permute-start(bf16[64,2048]{1,0:T(8,128)(2,1)S(1)} %get-tuple-element.54), channel_id=1, source_target_pairs={{0,8},{4,12},{8,0},{12,4},{16,24},{20,28},{24,16},{28,20},{1,9},{5... | collective-permute-start | bytes 786440 | tf_op jit(solution)/shard_map/ppermute | solution.py:21
  61.1 1.5 %collective-permute-start.19 = (bf16[64,2048]{1,0:T(8,128)(2,1)S(1)}, bf16[64,2048]{1,0:T(8,128)(2,1)S(1)}, u32[]{:S(2)}, u32[]{:S(2)}) collective-permute-start(bf16[64,2048]{1,0:T(8,128)(2,1)S(1)} %slice.76), channel_id=1, source_target_pairs={{0,2},{1,3},{2,0},{3,1},{4,6},{5,7},{6,4},{7,5},{8,10},{9,11},{10,... | collective-permute-start | bytes 786440 | tf_op jit(solution)/shard_map/ppermute | solution.py:26
  63.4 6.9 %collective-permute-done.19 = bf16[64,2048]{1,0:T(8,128)(2,1)S(1)} collective-permute-done((bf16[64,2048]{1,0:T(8,128)(2,1)S(1)}, bf16[64,2048]{1,0:T(8,128)(2,1)S(1)}, u32[]{:S(2)}, u32[]{:S(2)}) %collective-permute-start.19) | collective-permute-done | bytes 262176 | tf_op jit(solution)/shard_map/ppermute | solution.py:26
  70.9 4.0 %collective-permute-done.10 = bf16[64,2048]{1,0:T(8,128)(2,1)S(1)} collective-permute-done((bf16[64,2048]{1,0:T(8,128)(2,1)S(1)}, bf16[64,2048]{1,0:T(8,128)(2,1)S(1)}, u32[]{:S(2)}, u32[]{:S(2)}) %collective-permute-start.10) | collective-permute-done | bytes 262176 | tf_op jit(solution)/shard_map/ppermute | solution.py:26
  74.9 1.0 collective-permute-start.21
  76.0 3.1 %collective-permute-start.11 = (bf16[32,2048]{1,0:T(8,128)(2,1)S(1)}, bf16[32,2048]{1,0:T(8,128)(2,1)S(1)}, u32[]{:S(2)}, u32[]{:S(2)}) collective-permute-start(bf16[32,2048]{1,0:T(8,128)(2,1)S(1)} %get-tuple-element.58), channel_id=1, source_target_pairs={{0,24},{4,28},{8,16},{12,20},{16,8},{20,12},{24,0},{28,4},{1,25},{... | collective-permute-start | bytes 393224 | tf_op jit(solution)/shard_map/ppermute | solution.py:21
  79.2 5.9 %shared.1.shared_ref = f32[256,2048]{1,0:T(8,128)S(1)} custom-call(bf16[256,2048]{1,0:T(8,128)(2,1)} %x_ref.1, bf16[2048,512]{1,0:T(8,128)(2,1)} %wg_ref.1, bf16[2048,512]{1,0:T(8,128)(2,1)} %wu_ref.1, bf16[512,2048]{1,0:T(8,128)(2,1)} %wd_ref.1), custom_call_target="tpu_custom_call" | custom-call | flops 1610612736 | bytes 9437184 | tf_op jit(solution)/shard_map/shared/pallas_call | solution.py:239
  85.1 1.1 %shard_map.92.base_ref = f32[256,2048]{1,0:T(8,128)S(1)} custom-call(s32[4]{0:T(128)S(1)} %pad_add_fusion.s_ref, bf16[192,256]{1,0:T(8,128)(2,1)S(1)} %get-tuple-element.30.oh_ref, f32[256,2048]{1,0:T(8,128)S(1)} %shared.1.shared_ref, bf16[64,2048]{1,0:T(8,128)(2,1)S(1)} %collective-permute-done.3.refs_0_, bf16[128,2048]{1,0:T(8,128)(2,1)S(1)} %get-tuple-element.38.refs_1_), custom_call_target="tpu_custom_call" | custom-call | flops 201326592 | bytes 4456448 | tf_op jit(solution)/shard_map/pallas_call | solution.py:305
  86.3 1.9 %collective-permute-done.21.refs_3_ = bf16[32,2048]{1,0:T(8,128)(2,1)S(1)} collective-permute-done((bf16[32,2048]{1,0:T(8,128)(2,1)S(1)}, bf16[32,2048]{1,0:T(8,128)(2,1)S(1)}, u32[]{:S(2)}, u32[]{:S(2)}) %collective-permute-start.21) | collective-permute-done | bytes 131104 | tf_op jit(solution)/shard_map/ppermute | solution.py:21
  88.2 4.2 %collective-permute-done.11.refs_0_ = bf16[32,2048]{1,0:T(8,128)(2,1)S(1)} collective-permute-done((bf16[32,2048]{1,0:T(8,128)(2,1)S(1)}, bf16[32,2048]{1,0:T(8,128)(2,1)S(1)}, u32[]{:S(2)}, u32[]{:S(2)}) %collective-permute-start.11) | collective-permute-done | bytes 131104 | tf_op jit(solution)/shard_map/ppermute | solution.py:21
  92.4 3.1 %collective-permute-done.12.refs_1_ = bf16[32,2048]{1,0:T(8,128)(2,1)S(1)} collective-permute-done((bf16[32,2048]{1,0:T(8,128)(2,1)S(1)}, bf16[32,2048]{1,0:T(8,128)(2,1)S(1)}, u32[]{:S(2)}, u32[]{:S(2)}) %collective-permute-start.12) | collective-permute-done | bytes 131104 | tf_op jit(solution)/shard_map/ppermute | solution.py:21
  95.5 1.2 %shard_map.96 = (f32[128,2048]{1,0:T(8,128)S(1)}, bf16[128,2048]{1,0:T(8,128)(2,1)S(1)}) custom-call(s32[4]{0:T(128)S(1)} %pad_add_fusion.s_ref, bf16[256,256]{1,0:T(8,128)(2,1)S(1)} %get-tuple-element.29.oh_ref, f32[256,2048]{1,0:T(8,128)S(1)} %shard_map.92.base_ref, bf16[32,2048]{1,0:T(8,128)(2,1)S(1)} %collective-permute-done.11.refs_0_, ...), custom_call_target="tpu_custom_call" | custom-call | flops 268435456 | bytes 4718592 | tf_op jit(solution)/shard_map/pallas_call | solution.py:305
  96.8 1.9 %collective-permute-done.29 = bf16[128,2048]{1,0:T(8,128)(2,1)S(1)} collective-permute-done((bf16[128,2048]{1,0:T(8,128)(2,1)S(1)}, bf16[128,2048]{1,0:T(8,128)(2,1)S(1)}, u32[]{:S(2)}, u32[]{:S(2)}) %collective-permute-start.29) | collective-permute-done | bytes 524320 | tf_op jit(solution)/shard_map/ppermute | solution.py:26
  98.9 1.5 %collective-permute-start.30 = (bf16[64,2048]{1,0:T(8,128)(2,1)S(1)}, bf16[64,2048]{1,0:T(8,128)(2,1)S(1)}, u32[]{:S(2)}, u32[]{:S(2)}) collective-permute-start(bf16[64,2048]{1,0:T(8,128)(2,1)S(1)} %slice.75), channel_id=1, source_target_pairs={{0,2},{1,3},{2,0},{3,1},{4,6},{5,7},{6,4},{7,5},{8,10},{9,11},{10,... | collective-permute-start | bytes 786440 | tf_op jit(solution)/shard_map/ppermute | solution.py:26
  100.4 6.9 %collective-permute-done.30 = bf16[64,2048]{1,0:T(8,128)(2,1)S(1)} collective-permute-done((bf16[64,2048]{1,0:T(8,128)(2,1)S(1)}, bf16[64,2048]{1,0:T(8,128)(2,1)S(1)}, u32[]{:S(2)}, u32[]{:S(2)}) %collective-permute-start.30) | collective-permute-done | bytes 262176 | tf_op jit(solution)/shard_map/ppermute | solution.py:26
  107.3 0.8 fusion
  (58 shorter events, 7.2 us)
Async XLA Ops:
  2.6 7.5 %collective-permute-start.13 = (bf16[32,2176]{1,0:T(8,128)(2,1)S(1)}, bf16[32,2176]{1,0:T(8,128)(2,1)S(1)}, u32[]{:S(2)}, u32[]{:S(2)}) collective-permute-start(bf16[32,2176]{1,0:T(8,128)(2,1)S(1)} %get-tuple-element.43), channel_id=1, source_target_pairs={{0,16},{4,20},{8,24},{12,28},{16,0},{20,4},{24,8},{28,12},{1,17},{... | collective-permute-start | bytes 417800 | tf_op jit(solution)/shard_map/ppermute | solution.py:21
  2.7 28.5 %collective-permute-start.22 = (bf16[64,2176]{1,0:T(8,128)(2,1)S(1)}, bf16[64,2176]{1,0:T(8,128)(2,1)S(1)}, u32[]{:S(2)}, u32[]{:S(2)}) collective-permute-start(bf16[64,2176]{1,0:T(8,128)(2,1)S(1)} %get-tuple-element.47), channel_id=1, source_target_pairs={{0,8},{4,12},{8,0},{12,4},{16,24},{20,28},{24,16},{28,20},{1,9},{5... | collective-permute-start | bytes 835592 | tf_op jit(solution)/shard_map/ppermute | solution.py:21
  4.6 26.6 %collective-permute-start.23 = (bf16[64,2176]{1,0:T(8,128)(2,1)S(1)}, bf16[64,2176]{1,0:T(8,128)(2,1)S(1)}, u32[]{:S(2)}, u32[]{:S(2)}) collective-permute-start(bf16[64,2176]{1,0:T(8,128)(2,1)S(1)} %get-tuple-element.48), channel_id=1, source_target_pairs={{0,12},{4,8},{8,4},{12,0},{16,28},{20,24},{24,20},{28,16},{1,13},{... | collective-permute-start | bytes 835592 | tf_op jit(solution)/shard_map/ppermute | solution.py:21
  6.0 22.3 %collective-permute-start.14 = (bf16[32,2176]{1,0:T(8,128)(2,1)S(1)}, bf16[32,2176]{1,0:T(8,128)(2,1)S(1)}, u32[]{:S(2)}, u32[]{:S(2)}) collective-permute-start(bf16[32,2176]{1,0:T(8,128)(2,1)S(1)} %get-tuple-element.44), channel_id=1, source_target_pairs={{0,20},{4,16},{8,28},{12,24},{16,4},{20,0},{24,12},{28,8},{1,21},{... | collective-permute-start | bytes 417800 | tf_op jit(solution)/shard_map/ppermute | solution.py:21
  8.6 20.4 %collective-permute-start.4 = (bf16[32,2176]{1,0:T(8,128)(2,1)S(1)}, bf16[32,2176]{1,0:T(8,128)(2,1)S(1)}, u32[]{:S(2)}, u32[]{:S(2)}) collective-permute-start(bf16[32,2176]{1,0:T(8,128)(2,1)S(1)} %get-tuple-element.39), channel_id=1, source_target_pairs={{0,24},{4,28},{8,16},{12,20},{16,8},{20,12},{24,0},{28,4},{1,25},{... | collective-permute-start | bytes 417800 | tf_op jit(solution)/shard_map/ppermute | solution.py:21
  10.2 20.3 %collective-permute-start.5 = (bf16[32,2176]{1,0:T(8,128)(2,1)S(1)}, bf16[32,2176]{1,0:T(8,128)(2,1)S(1)}, u32[]{:S(2)}, u32[]{:S(2)}) collective-permute-start(bf16[32,2176]{1,0:T(8,128)(2,1)S(1)} %get-tuple-element.40), channel_id=1, source_target_pairs={{0,28},{4,24},{8,20},{12,16},{16,12},{20,8},{24,4},{28,0},{1,29},{... | collective-permute-start | bytes 417800 | tf_op jit(solution)/shard_map/ppermute | solution.py:21
  28.3 6.5 %collective-permute-start = (bf16[64,2176]{1,0:T(8,128)(2,1)S(1)}, bf16[64,2176]{1,0:T(8,128)(2,1)S(1)}, u32[]{:S(2)}, u32[]{:S(2)}) collective-permute-start(bf16[64,2176]{1,0:T(8,128)(2,1)S(1)} %get-tuple-element.32), channel_id=1, source_target_pairs={{0,4},{4,0},{8,12},{12,8},{16,20},{20,16},{24,28},{28,24},{1,5},{5... | collective-permute-start | bytes 835592 | tf_op jit(solution)/shard_map/ppermute | solution.py:21
  29.0 9.7 %collective-permute-start.15 = (bf16[64,2176]{1,0:T(8,128)(2,1)S(1)}, bf16[64,2176]{1,0:T(8,128)(2,1)S(1)}, u32[]{:S(2)}, u32[]{:S(2)}) collective-permute-start(bf16[64,2176]{1,0:T(8,128)(2,1)S(1)} %constant_dynamic-update-slice_fusion.2.refs_0_), channel_id=1, source_target_pairs={{0,2},{1,3},{2,0},{3,1},{4,6},{5,7},{6,4},{7,5},{8,10},{9,11},{10,... | collective-permute-start | bytes 835592 | tf_op jit(solution)/shard_map/ppermute | solution.py:26
  30.5 10.6 %collective-permute-start.6 = (bf16[64,2176]{1,0:T(8,128)(2,1)S(1)}, bf16[64,2176]{1,0:T(8,128)(2,1)S(1)}, u32[]{:S(2)}, u32[]{:S(2)}) collective-permute-start(bf16[64,2176]{1,0:T(8,128)(2,1)S(1)} %constant_dynamic-update-slice_fusion.refs_0_), channel_id=1, source_target_pairs={{0,2},{1,3},{2,0},{3,1},{4,6},{5,7},{6,4},{7,5},{8,10},{9,11},{10,... | collective-permute-start | bytes 835592 | tf_op jit(solution)/shard_map/ppermute | solution.py:26
  31.2 10.0 %collective-permute-start.24 = (bf16[64,2176]{1,0:T(8,128)(2,1)S(1)}, bf16[64,2176]{1,0:T(8,128)(2,1)S(1)}, u32[]{:S(2)}, u32[]{:S(2)}) collective-permute-start(bf16[64,2176]{1,0:T(8,128)(2,1)S(1)} %collective-permute-done.22.refs_0_), channel_id=1, source_target_pairs={{0,1},{1,0},{2,3},{3,2},{4,5},{5,4},{6,7},{7,6},{8,9},{9,8},{10,11... | collective-permute-start | bytes 835592 | tf_op jit(solution)/shard_map/ppermute | solution.py:26
  31.2 10.5 %collective-permute-start.25 = (bf16[64,2176]{1,0:T(8,128)(2,1)S(1)}, bf16[64,2176]{1,0:T(8,128)(2,1)S(1)}, u32[]{:S(2)}, u32[]{:S(2)}) collective-permute-start(bf16[64,2176]{1,0:T(8,128)(2,1)S(1)} %collective-permute-done.23.refs_1_), channel_id=1, source_target_pairs={{0,1},{1,0},{2,3},{3,2},{4,5},{5,4},{6,7},{7,6},{8,9},{9,8},{10,11... | collective-permute-start | bytes 835592 | tf_op jit(solution)/shard_map/ppermute | solution.py:26
  34.9 10.0 %collective-permute-start.1 = (bf16[64,2176]{1,0:T(8,128)(2,1)S(1)}, bf16[64,2176]{1,0:T(8,128)(2,1)S(1)}, u32[]{:S(2)}, u32[]{:S(2)}) collective-permute-start(bf16[64,2176]{1,0:T(8,128)(2,1)S(1)} %collective-permute-done.refs_1_), channel_id=1, source_target_pairs={{0,1},{1,0},{2,3},{3,2},{4,5},{5,4},{6,7},{7,6},{8,9},{9,8},{10,11... | collective-permute-start | bytes 835592 | tf_op jit(solution)/shard_map/ppermute | solution.py:26
  38.7 9.9 %collective-permute-start.16 = (bf16[64,2176]{1,0:T(8,128)(2,1)S(1)}, bf16[64,2176]{1,0:T(8,128)(2,1)S(1)}, u32[]{:S(2)}, u32[]{:S(2)}) collective-permute-start(bf16[64,2176]{1,0:T(8,128)(2,1)S(1)} %constant_dynamic-update-slice_fusion.2.refs_0_), channel_id=1, source_target_pairs={{0,1},{1,0},{2,3},{3,2},{4,5},{5,4},{6,7},{7,6},{8,9},{9,8},{10,11... | collective-permute-start | bytes 835592 | tf_op jit(solution)/shard_map/ppermute | solution.py:26
  41.1 11.3 %collective-permute-start.7 = (bf16[64,2176]{1,0:T(8,128)(2,1)S(1)}, bf16[64,2176]{1,0:T(8,128)(2,1)S(1)}, u32[]{:S(2)}, u32[]{:S(2)}) collective-permute-start(bf16[64,2176]{1,0:T(8,128)(2,1)S(1)} %constant_dynamic-update-slice_fusion.refs_0_), channel_id=1, source_target_pairs={{0,1},{1,0},{2,3},{3,2},{4,5},{5,4},{6,7},{7,6},{8,9},{9,8},{10,11... | collective-permute-start | bytes 835592 | tf_op jit(solution)/shard_map/ppermute | solution.py:26
  41.1 7.6 %collective-permute-start.17 = (bf16[64,2176]{1,0:T(8,128)(2,1)S(1)}, bf16[64,2176]{1,0:T(8,128)(2,1)S(1)}, u32[]{:S(2)}, u32[]{:S(2)}) collective-permute-start(bf16[64,2176]{1,0:T(8,128)(2,1)S(1)} %collective-permute-done.15.refs_1_), channel_id=1, source_target_pairs={{0,1},{1,0},{2,3},{3,2},{4,5},{5,4},{6,7},{7,6},{8,9},{9,8},{10,11... | collective-permute-start | bytes 835592 | tf_op jit(solution)/shard_map/ppermute | solution.py:26
  41.6 10.8 %collective-permute-start.8 = (bf16[64,2176]{1,0:T(8,128)(2,1)S(1)}, bf16[64,2176]{1,0:T(8,128)(2,1)S(1)}, u32[]{:S(2)}, u32[]{:S(2)}) collective-permute-start(bf16[64,2176]{1,0:T(8,128)(2,1)S(1)} %collective-permute-done.6.refs_1_), channel_id=1, source_target_pairs={{0,1},{1,0},{2,3},{3,2},{4,5},{5,4},{6,7},{7,6},{8,9},{9,8},{10,11... | collective-permute-start | bytes 835592 | tf_op jit(solution)/shard_map/ppermute | solution.py:26
  44.9 12.4 %collective-permute-start.26 = (bf16[128,2048]{1,0:T(8,128)(2,1)S(1)}, bf16[128,2048]{1,0:T(8,128)(2,1)S(1)}, u32[]{:S(2)}, u32[]{:S(2)}) collective-permute-start(bf16[128,2048]{1,0:T(8,128)(2,1)S(1)} %get-tuple-element.50), channel_id=1, source_target_pairs={{0,1},{1,0},{2,3},{3,2},{4,5},{5,4},{6,7},{7,6},{8,9},{9,8},{10,11... | collective-permute-start | bytes 1572872 | tf_op jit(solution)/shard_map/ppermute | solution.py:26
  48.6 7.2 %collective-permute-start.2 = (bf16[64,2048]{1,0:T(8,128)(2,1)S(1)}, bf16[64,2048]{1,0:T(8,128)(2,1)S(1)}, u32[]{:S(2)}, u32[]{:S(2)}) collective-permute-start(bf16[64,2048]{1,0:T(8,128)(2,1)S(1)} %get-tuple-element.37), channel_id=1, source_target_pairs={{0,1},{1,0},{2,3},{3,2},{4,5},{5,4},{6,7},{7,6},{8,9},{9,8},{10,11... | collective-permute-start | bytes 786440 | tf_op jit(solution)/shard_map/ppermute | solution.py:26
  51.9 9.0 %collective-permute-start.18 = (bf16[128,2048]{1,0:T(8,128)(2,1)S(1)}, bf16[128,2048]{1,0:T(8,128)(2,1)S(1)}, u32[]{:S(2)}, u32[]{:S(2)}) collective-permute-start(bf16[128,2048]{1,0:T(8,128)(2,1)S(1)} %get-tuple-element.46), channel_id=1, source_target_pairs={{0,1},{1,0},{2,3},{3,2},{4,5},{5,4},{6,7},{7,6},{8,9},{9,8},{10,11... | collective-permute-start | bytes 1572872 | tf_op jit(solution)/shard_map/ppermute | solution.py:26
  55.6 7.0 %collective-permute-start.9 = (bf16[128,2048]{1,0:T(8,128)(2,1)S(1)}, bf16[128,2048]{1,0:T(8,128)(2,1)S(1)}, u32[]{:S(2)}, u32[]{:S(2)}) collective-permute-start(bf16[128,2048]{1,0:T(8,128)(2,1)S(1)} %get-tuple-element.42), channel_id=1, source_target_pairs={{0,1},{1,0},{2,3},{3,2},{4,5},{5,4},{6,7},{7,6},{8,9},{9,8},{10,11... | collective-permute-start | bytes 1572872 | tf_op jit(solution)/shard_map/ppermute | solution.py:26
  55.8 20.2 %collective-permute-start.3 = (bf16[64,2048]{1,0:T(8,128)(2,1)S(1)}, bf16[64,2048]{1,0:T(8,128)(2,1)S(1)}, u32[]{:S(2)}, u32[]{:S(2)}) collective-permute-start(bf16[64,2048]{1,0:T(8,128)(2,1)S(1)} %add_convert_fusion.1), channel_id=1, source_target_pairs={{0,4},{4,0},{8,12},{12,8},{16,20},{20,16},{24,28},{28,24},{1,5},{5... | collective-permute-start | bytes 786440 | tf_op jit(solution)/shard_map/ppermute | solution.py:21
  57.4 21.6 %collective-permute-start.27 = (bf16[64,2048]{1,0:T(8,128)(2,1)S(1)}, bf16[64,2048]{1,0:T(8,128)(2,1)S(1)}, u32[]{:S(2)}, u32[]{:S(2)}) collective-permute-start(bf16[64,2048]{1,0:T(8,128)(2,1)S(1)} %get-tuple-element.54), channel_id=1, source_target_pairs={{0,8},{4,12},{8,0},{12,4},{16,24},{20,28},{24,16},{28,20},{1,9},{5... | collective-permute-start | bytes 786440 | tf_op jit(solution)/shard_map/ppermute | solution.py:21
  60.8 25.5 %collective-permute-start.28 = (bf16[64,2048]{1,0:T(8,128)(2,1)S(1)}, bf16[64,2048]{1,0:T(8,128)(2,1)S(1)}, u32[]{:S(2)}, u32[]{:S(2)}) collective-permute-start(bf16[64,2048]{1,0:T(8,128)(2,1)S(1)} %get-tuple-element.53), channel_id=1, source_target_pairs={{0,12},{4,8},{8,4},{12,0},{16,28},{20,24},{24,20},{28,16},{1,13},{... | collective-permute-start | bytes 786440 | tf_op jit(solution)/shard_map/ppermute | solution.py:21
  61.1 9.2 %collective-permute-start.19 = (bf16[64,2048]{1,0:T(8,128)(2,1)S(1)}, bf16[64,2048]{1,0:T(8,128)(2,1)S(1)}, u32[]{:S(2)}, u32[]{:S(2)}) collective-permute-start(bf16[64,2048]{1,0:T(8,128)(2,1)S(1)} %slice.76), channel_id=1, source_target_pairs={{0,2},{1,3},{2,0},{3,1},{4,6},{5,7},{6,4},{7,5},{8,10},{9,11},{10,... | collective-permute-start | bytes 786440 | tf_op jit(solution)/shard_map/ppermute | solution.py:26
  62.8 12.1 %collective-permute-start.10 = (bf16[64,2048]{1,0:T(8,128)(2,1)S(1)}, bf16[64,2048]{1,0:T(8,128)(2,1)S(1)}, u32[]{:S(2)}, u32[]{:S(2)}) collective-permute-start(bf16[64,2048]{1,0:T(8,128)(2,1)S(1)} %slice.77), channel_id=1, source_target_pairs={{0,2},{1,3},{2,0},{3,1},{4,6},{5,7},{6,4},{7,5},{8,10},{9,11},{10,... | collective-permute-start | bytes 786440 | tf_op jit(solution)/shard_map/ppermute | solution.py:26
  70.5 15.8 %collective-permute-start.20 = (bf16[32,2048]{1,0:T(8,128)(2,1)S(1)}, bf16[32,2048]{1,0:T(8,128)(2,1)S(1)}, u32[]{:S(2)}, u32[]{:S(2)}) collective-permute-start(bf16[32,2048]{1,0:T(8,128)(2,1)S(1)} %get-tuple-element.56), channel_id=1, source_target_pairs={{0,16},{4,20},{8,24},{12,28},{16,0},{20,4},{24,8},{28,12},{1,17},{... | collective-permute-start | bytes 393224 | tf_op jit(solution)/shard_map/ppermute | solution.py:21
  74.9 13.3 %collective-permute-start.21 = (bf16[32,2048]{1,0:T(8,128)(2,1)S(1)}, bf16[32,2048]{1,0:T(8,128)(2,1)S(1)}, u32[]{:S(2)}, u32[]{:S(2)}) collective-permute-start(bf16[32,2048]{1,0:T(8,128)(2,1)S(1)} %get-tuple-element.55), channel_id=1, source_target_pairs={{0,20},{4,16},{8,28},{12,24},{16,4},{20,0},{24,12},{28,8},{1,21},{... | collective-permute-start | bytes 393224 | tf_op jit(solution)/shard_map/ppermute | solution.py:21
  76.0 16.4 %collective-permute-start.11 = (bf16[32,2048]{1,0:T(8,128)(2,1)S(1)}, bf16[32,2048]{1,0:T(8,128)(2,1)S(1)}, u32[]{:S(2)}, u32[]{:S(2)}) collective-permute-start(bf16[32,2048]{1,0:T(8,128)(2,1)S(1)} %get-tuple-element.58), channel_id=1, source_target_pairs={{0,24},{4,28},{8,16},{12,20},{16,8},{20,12},{24,0},{28,4},{1,25},{... | collective-permute-start | bytes 393224 | tf_op jit(solution)/shard_map/ppermute | solution.py:21
  79.1 16.4 %collective-permute-start.12 = (bf16[32,2048]{1,0:T(8,128)(2,1)S(1)}, bf16[32,2048]{1,0:T(8,128)(2,1)S(1)}, u32[]{:S(2)}, u32[]{:S(2)}) collective-permute-start(bf16[32,2048]{1,0:T(8,128)(2,1)S(1)} %get-tuple-element.57), channel_id=1, source_target_pairs={{0,28},{4,24},{8,20},{12,16},{16,12},{20,8},{24,4},{28,0},{1,29},{... | collective-permute-start | bytes 393224 | tf_op jit(solution)/shard_map/ppermute | solution.py:21
  96.7 2.0 %collective-permute-start.29 = (bf16[128,2048]{1,0:T(8,128)(2,1)S(1)}, bf16[128,2048]{1,0:T(8,128)(2,1)S(1)}, u32[]{:S(2)}, u32[]{:S(2)}) collective-permute-start(bf16[128,2048]{1,0:T(8,128)(2,1)S(1)} %get-tuple-element.52), channel_id=1, source_target_pairs={{0,1},{1,0},{2,3},{3,2},{4,5},{5,4},{6,7},{7,6},{8,9},{9,8},{10,11... | collective-permute-start | bytes 1572872 | tf_op jit(solution)/shard_map/ppermute | solution.py:26
  98.9 8.4 %collective-permute-start.30 = (bf16[64,2048]{1,0:T(8,128)(2,1)S(1)}, bf16[64,2048]{1,0:T(8,128)(2,1)S(1)}, u32[]{:S(2)}, u32[]{:S(2)}) collective-permute-start(bf16[64,2048]{1,0:T(8,128)(2,1)S(1)} %slice.75), channel_id=1, source_target_pairs={{0,2},{1,3},{2,0},{3,1},{4,6},{5,7},{6,4},{7,5},{8,10},{9,11},{10,... | collective-permute-start | bytes 786440 | tf_op jit(solution)/shard_map/ppermute | solution.py:26

commit v3 on v2

--- a/solution.py
+++ b/solution.py
@@ -91,14 +91,18 @@
         parts.append(jnp.zeros((extra - 2 * experts, tok_rows), BF16))
     table = jnp.concatenate(parts, axis=0)
     copies[2].wait()
+    aligned = all(count % 16 == 0 for _, _, count in pieces)
     for c, w in column_blocks(width) + [(width, extra)]:
         if c < width:
-            rows[:, :w] = jnp.dot(one_hot, tok_ref[:, c : c + w], preferred_element_type=F32)
+            value = jnp.dot(one_hot, tok_ref[:, c : c + w], preferred_element_type=F32)
         else:
-            rows[:, :w] = lax.dot_general(one_hot, table, (((1,), (1,)), ((), ())), preferred_element_type=F32)
+            value = lax.dot_general(one_hot, table, (((1,), (1,)), ((), ())), preferred_element_type=F32)
+        if not aligned:
+            rows[:, :w] = value
+            value = rows
         offset = 0
         for out, (_, _, count) in zip(outs, pieces):
-            out[:, c : c + w] = rows[offset : offset + count, :w].astype(BF16)
+            out[:, c : c + w] = value[offset : offset + count, :w].astype(BF16)
             offset += count
 
 

time: 108 us -> 108 us (level)
  no operation moved by 1% of the time
where the time goes in v3:
time: 108 us
  waiting for transfers between devices  50.9 us (47%)
  starting transfers between devices  27.8 us (26%)
  Pallas kernels  27.3 us (25%)
  other arithmetic  1.48 us (1%)
    ppermute x14, waiting for transfers between devices, xor_node(): return lax.ppermute(x, 'node', [(i, i ^ k) for i in range(count)])  29.3 us
    ppermute x17, waiting for transfers between devices, xor_local(): return lax.ppermute(x, 'local', [(i, i ^ k) for i in range(count)])  21.6 us
    ppermute x14, starting transfers between devices, xor_node(): return lax.ppermute(x, 'node', [(i, i ^ k) for i in range(count)])  19 us
    pallas_call x4, Pallas kernels, ffn(): pl.pallas_call(functools.partial(ffn_kernel, counts, experts, ranges), ou...  12.7 us
    ppermute x17, starting transfers between devices, xor_local(): return lax.ppermute(x, 'local', [(i, i ^ k) for i in range(count)])  8.84 us
    pallas_call x1, Pallas kernels, shared(): pl.pallas_call(shared_kernel, grid=(hidden // block,), out_shape=jax.Shap...  5.93 us
    pallas_call x1, Pallas kernels, stage(): pl.pallas_call(stage_kernel, out_shape=[jax.ShapeDtypeStruct(w.shape, w.d...  3.78 us
    pallas_call x1, Pallas kernels, route(): pl.pallas_call(functools.partial(route_kernel, pieces, node_count), out_s...  2.55 us
  transfers between devices with their start and end apart: 31, of which 11 were waited for; matrix products, arithmetic and copies ran while one was open for 1% of the time, Pallas kernels for 22%

profile of v3, /device:TPU:16, one launch (start us, length us, event | category | flops | bytes accessed | tf_op | source)
XLA Modules:
  0.0 108.1 jit_solution(4298718609057278285)
XLA Ops:
  0.1 2.6 %route.1 = (bf16[32,2176]{1,0:T(8,128)(2,1)S(1)}, bf16[32,2176]{1,0:T(8,128)(2,1)S(1)}, bf16[32,2176]{1,0:T(8,128)(2,1)S(1)}, bf16[32,2176]{1,0:T(8,128)(2,1)S(1...) custom-call(s32[4]{0:T(128)S(1)} %pad_add_fusion.s_ref, ...), custom_call_target="tpu_custom_call" | custom-call | flops 499122176 | bytes 2998272 | tf_op jit(solution)/shard_map/route/pallas_call | solution.py:115
  2.7 1.9 %collective-permute-start.22 = (bf16[64,2176]{1,0:T(8,128)(2,1)S(1)}, bf16[64,2176]{1,0:T(8,128)(2,1)S(1)}, u32[]{:S(2)}, u32[]{:S(2)}) collective-permute-start(bf16[64,2176]{1,0:T(8,128)(2,1)S(1)} %get-tuple-element.47), channel_id=1, source_target_pairs={{0,8},{4,12},{8,0},{12,4},{16,24},{20,28},{24,16},{28,20},{1,9},{5... | collective-permute-start | bytes 835592 | tf_op jit(solution)/shard_map/ppermute | solution.py:21
  4.6 1.4 %collective-permute-start.23 = (bf16[64,2176]{1,0:T(8,128)(2,1)S(1)}, bf16[64,2176]{1,0:T(8,128)(2,1)S(1)}, u32[]{:S(2)}, u32[]{:S(2)}) collective-permute-start(bf16[64,2176]{1,0:T(8,128)(2,1)S(1)} %get-tuple-element.48), channel_id=1, source_target_pairs={{0,12},{4,8},{8,4},{12,0},{16,28},{20,24},{24,20},{28,16},{1,13},{... | collective-permute-start | bytes 835592 | tf_op jit(solution)/shard_map/ppermute | solution.py:21
  6.0 2.6 %collective-permute-start.14 = (bf16[32,2176]{1,0:T(8,128)(2,1)S(1)}, bf16[32,2176]{1,0:T(8,128)(2,1)S(1)}, u32[]{:S(2)}, u32[]{:S(2)}) collective-permute-start(bf16[32,2176]{1,0:T(8,128)(2,1)S(1)} %get-tuple-element.44), channel_id=1, source_target_pairs={{0,20},{4,16},{8,28},{12,24},{16,4},{20,0},{24,12},{28,8},{1,21},{... | collective-permute-start | bytes 417800 | tf_op jit(solution)/shard_map/ppermute | solution.py:21
  9.0 1.2 %collective-permute-done.13 = bf16[32,2176]{1,0:T(8,128)(2,1)S(1)} collective-permute-done((bf16[32,2176]{1,0:T(8,128)(2,1)S(1)}, bf16[32,2176]{1,0:T(8,128)(2,1)S(1)}, u32[]{:S(2)}, u32[]{:S(2)}) %collective-permute-start.13) | collective-permute-done | bytes 139296 | tf_op jit(solution)/shard_map/ppermute | solution.py:21
  10.2 2.4 %collective-permute-start.5 = (bf16[32,2176]{1,0:T(8,128)(2,1)S(1)}, bf16[32,2176]{1,0:T(8,128)(2,1)S(1)}, u32[]{:S(2)}, u32[]{:S(2)}) collective-permute-start(bf16[32,2176]{1,0:T(8,128)(2,1)S(1)} %get-tuple-element.40), channel_id=1, source_target_pairs={{0,28},{4,24},{8,20},{12,16},{16,12},{20,8},{24,4},{28,0},{1,29},{... | collective-permute-start | bytes 417800 | tf_op jit(solution)/shard_map/ppermute | solution.py:21
  12.6 15.7 %collective-permute-done.14 = bf16[32,2176]{1,0:T(8,128)(2,1)S(1)} collective-permute-done((bf16[32,2176]{1,0:T(8,128)(2,1)S(1)}, bf16[32,2176]{1,0:T(8,128)(2,1)S(1)}, u32[]{:S(2)}, u32[]{:S(2)}) %collective-permute-start.14) | collective-permute-done | bytes 139296 | tf_op jit(solution)/shard_map/ppermute | solution.py:21
  29.0 1.5 %collective-permute-start.15 = (bf16[64,2176]{1,0:T(8,128)(2,1)S(1)}, bf16[64,2176]{1,0:T(8,128)(2,1)S(1)}, u32[]{:S(2)}, u32[]{:S(2)}) collective-permute-start(bf16[64,2176]{1,0:T(8,128)(2,1)S(1)} %constant_dynamic-update-slice_fusion.2.refs_0_), channel_id=1, source_target_pairs={{0,2},{1,3},{2,0},{3,1},{4,6},{5,7},{6,4},{7,5},{8,10},{9,11},{10,... | collective-permute-start | bytes 835592 | tf_op jit(solution)/shard_map/ppermute | solution.py:26
  31.7 3.2 %collective-permute-done.refs_1_ = bf16[64,2176]{1,0:T(8,128)(2,1)S(1)} collective-permute-done((bf16[64,2176]{1,0:T(8,128)(2,1)S(1)}, bf16[64,2176]{1,0:T(8,128)(2,1)S(1)}, u32[]{:S(2)}, u32[]{:S(2)}) %collective-permute-start) | collective-permute-done | bytes 278560 | tf_op jit(solution)/shard_map/ppermute | solution.py:21
  34.9 3.8 %stage.1 = (bf16[1,2048,768]{2,1,0:T(8,128)(2,1)S(1)}, bf16[1,2048,768]{2,1,0:T(8,128)(2,1)S(1)}, bf16[1,768,2048]{2,1,0:T(8,128)(2,1)S(1)}) custom-call(bf16[1,2048,768]{2,1,0:T(8,128)(2,1)} %refs_0_.1, bf16[1,2048,768]{2,1,0:T(8,128)(2,1)} %refs_1_.1, bf16[1,768,2048]{2,1,0:T(8,128)(2,1)} %refs_2_.1), custom_call_target="tpu_custom_call" | custom-call | bytes 18874368 | tf_op jit(solution)/shard_map/stage/pallas_call | solution.py:209
  39.2 1.9 %collective-permute-done.6.refs_1_ = bf16[64,2176]{1,0:T(8,128)(2,1)S(1)} collective-permute-done((bf16[64,2176]{1,0:T(8,128)(2,1)S(1)}, bf16[64,2176]{1,0:T(8,128)(2,1)S(1)}, u32[]{:S(2)}, u32[]{:S(2)}) %collective-permute-start.6) | collective-permute-done | bytes 278560 | tf_op jit(solution)/shard_map/ppermute | solution.py:26
  41.7 3.2 %shard_map.95 = (f32[128,2048]{1,0:T(8,128)S(1)}, bf16[128,2048]{1,0:T(8,128)(2,1)S(1)}) custom-call(s32[4]{0:T(128)S(1)} %pad_add_fusion.s_ref, bf16[64,2176]{1,0:T(8,128)(2,1)S(1)} %collective-permute-done.22.refs_0_, bf16[64,2176]{1,0:T(8,128)(2,1)S(1)} %collective-permute-done.23.refs_1_, bf16[64,2176]{1,0:T(8,128)(2,1)S(1)} %collective-permute-done.24.refs_2_, ...), custom_call_target="tpu_custom_call" | custom-call | flops 2415919104 | bytes 12582912 | tf_op jit(solution)/shard_map/pallas_call | solution.py:184
  45.4 3.2 %shard_map.91 = (bf16[128,2048]{1,0:T(8,128)(2,1)S(1)}, f32[64,2048]{1,0:T(8,128)S(1)}, bf16[64,2048]{1,0:T(8,128)(2,1)S(1)}) custom-call(s32[4]{0:T(128)S(1)} %pad_add_fusion.s_ref, bf16[128,2176]{1,0:T(8,128)(2,1)S(1)} %get-tuple-element.31.refs_0_, bf16[64,2176]{1,0:T(8,128)(2,1)S(1)} %collective-permute-done.refs_1_, ...), custom_call_target="tpu_custom_call" | custom-call | flops 2415919104 | bytes 12582912 | tf_op jit(solution)/shard_map/pallas_call | solution.py:184
  48.7 3.2 %shard_map.94 = (f32[128,2048]{1,0:T(8,128)S(1)}, bf16[128,2048]{1,0:T(8,128)(2,1)S(1)}) custom-call(s32[4]{0:T(128)S(1)} %pad_add_fusion.s_ref, bf16[64,2176]{1,0:T(8,128)(2,1)S(1)} %constant_dynamic-update-slice_fusion.2.refs_0_, bf16[64,2176]{1,0:T(8,128)(2,1)S(1)} %collective-permute-done.15.refs_1_, ...), custom_call_target="tpu_custom_call" | custom-call | flops 2415919104 | bytes 12582912 | tf_op jit(solution)/shard_map/pallas_call | solution.py:184
  52.4 3.2 %shard_map.93 = (f32[128,2048]{1,0:T(8,128)S(1)}, bf16[128,2048]{1,0:T(8,128)(2,1)S(1)}) custom-call(s32[4]{0:T(128)S(1)} %pad_add_fusion.s_ref, bf16[64,2176]{1,0:T(8,128)(2,1)S(1)} %constant_dynamic-update-slice_fusion.refs_0_, bf16[64,2176]{1,0:T(8,128)(2,1)S(1)} %collective-permute-done.6.refs_1_, bf16[64,2176]{1,0:T(8,128)(2,1)S(1)} %collective-permute-done.7.refs_2_, ...), custom_call_target="tpu_custom_call" | custom-call | flops 2415919104 | bytes 12582912 | tf_op jit(solution)/shard_map/pallas_call | solution.py:184
  55.8 1.5 %collective-permute-start.3 = (bf16[64,2048]{1,0:T(8,128)(2,1)S(1)}, bf16[64,2048]{1,0:T(8,128)(2,1)S(1)}, u32[]{:S(2)}, u32[]{:S(2)}) collective-permute-start(bf16[64,2048]{1,0:T(8,128)(2,1)S(1)} %add_convert_fusion.1), channel_id=1, source_target_pairs={{0,4},{4,0},{8,12},{12,8},{16,20},{20,16},{24,28},{28,24},{1,5},{5... | collective-permute-start | bytes 786440 | tf_op jit(solution)/shard_map/ppermute | solution.py:21
  57.4 3.4 %collective-permute-start.27 = (bf16[64,2048]{1,0:T(8,128)(2,1)S(1)}, bf16[64,2048]{1,0:T(8,128)(2,1)S(1)}, u32[]{:S(2)}, u32[]{:S(2)}) collective-permute-start(bf16[64,2048]{1,0:T(8,128)(2,1)S(1)} %get-tuple-element.54), channel_id=1, source_target_pairs={{0,8},{4,12},{8,0},{12,4},{16,24},{20,28},{24,16},{28,20},{1,9},{5... | collective-permute-start | bytes 786440 | tf_op jit(solution)/shard_map/ppermute | solution.py:21
  61.1 1.5 %collective-permute-start.19 = (bf16[64,2048]{1,0:T(8,128)(2,1)S(1)}, bf16[64,2048]{1,0:T(8,128)(2,1)S(1)}, u32[]{:S(2)}, u32[]{:S(2)}) collective-permute-start(bf16[64,2048]{1,0:T(8,128)(2,1)S(1)} %slice.76), channel_id=1, source_target_pairs={{0,2},{1,3},{2,0},{3,1},{4,6},{5,7},{6,4},{7,5},{8,10},{9,11},{10,... | collective-permute-start | bytes 786440 | tf_op jit(solution)/shard_map/ppermute | solution.py:26
  63.4 6.9 %collective-permute-done.19 = bf16[64,2048]{1,0:T(8,128)(2,1)S(1)} collective-permute-done((bf16[64,2048]{1,0:T(8,128)(2,1)S(1)}, bf16[64,2048]{1,0:T(8,128)(2,1)S(1)}, u32[]{:S(2)}, u32[]{:S(2)}) %collective-permute-start.19) | collective-permute-done | bytes 262176 | tf_op jit(solution)/shard_map/ppermute | solution.py:26
  70.9 4.0 %collective-permute-done.10 = bf16[64,2048]{1,0:T(8,128)(2,1)S(1)} collective-permute-done((bf16[64,2048]{1,0:T(8,128)(2,1)S(1)}, bf16[64,2048]{1,0:T(8,128)(2,1)S(1)}, u32[]{:S(2)}, u32[]{:S(2)}) %collective-permute-start.10) | collective-permute-done | bytes 262176 | tf_op jit(solution)/shard_map/ppermute | solution.py:26
  74.9 1.0 collective-permute-start.21
  76.0 3.1 %collective-permute-start.11 = (bf16[32,2048]{1,0:T(8,128)(2,1)S(1)}, bf16[32,2048]{1,0:T(8,128)(2,1)S(1)}, u32[]{:S(2)}, u32[]{:S(2)}) collective-permute-start(bf16[32,2048]{1,0:T(8,128)(2,1)S(1)} %get-tuple-element.58), channel_id=1, source_target_pairs={{0,24},{4,28},{8,16},{12,20},{16,8},{20,12},{24,0},{28,4},{1,25},{... | collective-permute-start | bytes 393224 | tf_op jit(solution)/shard_map/ppermute | solution.py:21
  79.2 5.9 %shared.1.shared_ref = f32[256,2048]{1,0:T(8,128)S(1)} custom-call(bf16[256,2048]{1,0:T(8,128)(2,1)} %x_ref.1, bf16[2048,512]{1,0:T(8,128)(2,1)} %wg_ref.1, bf16[2048,512]{1,0:T(8,128)(2,1)} %wu_ref.1, bf16[512,2048]{1,0:T(8,128)(2,1)} %wd_ref.1), custom_call_target="tpu_custom_call" | custom-call | flops 1610612736 | bytes 9437184 | tf_op jit(solution)/shard_map/shared/pallas_call | solution.py:243
  85.1 1.1 %shard_map.92.base_ref = f32[256,2048]{1,0:T(8,128)S(1)} custom-call(s32[4]{0:T(128)S(1)} %pad_add_fusion.s_ref, bf16[192,256]{1,0:T(8,128)(2,1)S(1)} %get-tuple-element.30.oh_ref, f32[256,2048]{1,0:T(8,128)S(1)} %shared.1.shared_ref, bf16[64,2048]{1,0:T(8,128)(2,1)S(1)} %collective-permute-done.3.refs_0_, bf16[128,2048]{1,0:T(8,128)(2,1)S(1)} %get-tuple-element.38.refs_1_), custom_call_target="tpu_custom_call" | custom-call | flops 201326592 | bytes 4456448 | tf_op jit(solution)/shard_map/pallas_call | solution.py:309
  86.3 1.9 %collective-permute-done.21.refs_3_ = bf16[32,2048]{1,0:T(8,128)(2,1)S(1)} collective-permute-done((bf16[32,2048]{1,0:T(8,128)(2,1)S(1)}, bf16[32,2048]{1,0:T(8,128)(2,1)S(1)}, u32[]{:S(2)}, u32[]{:S(2)}) %collective-permute-start.21) | collective-permute-done | bytes 131104 | tf_op jit(solution)/shard_map/ppermute | solution.py:21
  88.2 4.2 %collective-permute-done.11.refs_0_ = bf16[32,2048]{1,0:T(8,128)(2,1)S(1)} collective-permute-done((bf16[32,2048]{1,0:T(8,128)(2,1)S(1)}, bf16[32,2048]{1,0:T(8,128)(2,1)S(1)}, u32[]{:S(2)}, u32[]{:S(2)}) %collective-permute-start.11) | collective-permute-done | bytes 131104 | tf_op jit(solution)/shard_map/ppermute | solution.py:21
  92.4 3.1 %collective-permute-done.12.refs_1_ = bf16[32,2048]{1,0:T(8,128)(2,1)S(1)} collective-permute-done((bf16[32,2048]{1,0:T(8,128)(2,1)S(1)}, bf16[32,2048]{1,0:T(8,128)(2,1)S(1)}, u32[]{:S(2)}, u32[]{:S(2)}) %collective-permute-start.12) | collective-permute-done | bytes 131104 | tf_op jit(solution)/shard_map/ppermute | solution.py:21
  95.5 1.2 %shard_map.96 = (f32[128,2048]{1,0:T(8,128)S(1)}, bf16[128,2048]{1,0:T(8,128)(2,1)S(1)}) custom-call(s32[4]{0:T(128)S(1)} %pad_add_fusion.s_ref, bf16[256,256]{1,0:T(8,128)(2,1)S(1)} %get-tuple-element.29.oh_ref, f32[256,2048]{1,0:T(8,128)S(1)} %shard_map.92.base_ref, bf16[32,2048]{1,0:T(8,128)(2,1)S(1)} %collective-permute-done.11.refs_0_, ...), custom_call_target="tpu_custom_call" | custom-call | flops 268435456 | bytes 4718592 | tf_op jit(solution)/shard_map/pallas_call | solution.py:309
  96.8 1.9 %collective-permute-done.29 = bf16[128,2048]{1,0:T(8,128)(2,1)S(1)} collective-permute-done((bf16[128,2048]{1,0:T(8,128)(2,1)S(1)}, bf16[128,2048]{1,0:T(8,128)(2,1)S(1)}, u32[]{:S(2)}, u32[]{:S(2)}) %collective-permute-start.29) | collective-permute-done | bytes 524320 | tf_op jit(solution)/shard_map/ppermute | solution.py:26
  98.9 1.5 %collective-permute-start.30 = (bf16[64,2048]{1,0:T(8,128)(2,1)S(1)}, bf16[64,2048]{1,0:T(8,128)(2,1)S(1)}, u32[]{:S(2)}, u32[]{:S(2)}) collective-permute-start(bf16[64,2048]{1,0:T(8,128)(2,1)S(1)} %slice.75), channel_id=1, source_target_pairs={{0,2},{1,3},{2,0},{3,1},{4,6},{5,7},{6,4},{7,5},{8,10},{9,11},{10,... | collective-permute-start | bytes 786440 | tf_op jit(solution)/shard_map/ppermute | solution.py:26
  100.4 6.9 %collective-permute-done.30 = bf16[64,2048]{1,0:T(8,128)(2,1)S(1)} collective-permute-done((bf16[64,2048]{1,0:T(8,128)(2,1)S(1)}, bf16[64,2048]{1,0:T(8,128)(2,1)S(1)}, u32[]{:S(2)}, u32[]{:S(2)}) %collective-permute-start.30) | collective-permute-done | bytes 262176 | tf_op jit(solution)/shard_map/ppermute | solution.py:26
  107.3 0.8 fusion
  (58 shorter events, 7.2 us)
Async XLA Ops:
  2.6 7.5 %collective-permute-start.13 = (bf16[32,2176]{1,0:T(8,128)(2,1)S(1)}, bf16[32,2176]{1,0:T(8,128)(2,1)S(1)}, u32[]{:S(2)}, u32[]{:S(2)}) collective-permute-start(bf16[32,2176]{1,0:T(8,128)(2,1)S(1)} %get-tuple-element.43), channel_id=1, source_target_pairs={{0,16},{4,20},{8,24},{12,28},{16,0},{20,4},{24,8},{28,12},{1,17},{... | collective-permute-start | bytes 417800 | tf_op jit(solution)/shard_map/ppermute | solution.py:21
  2.7 28.5 %collective-permute-start.22 = (bf16[64,2176]{1,0:T(8,128)(2,1)S(1)}, bf16[64,2176]{1,0:T(8,128)(2,1)S(1)}, u32[]{:S(2)}, u32[]{:S(2)}) collective-permute-start(bf16[64,2176]{1,0:T(8,128)(2,1)S(1)} %get-tuple-element.47), channel_id=1, source_target_pairs={{0,8},{4,12},{8,0},{12,4},{16,24},{20,28},{24,16},{28,20},{1,9},{5... | collective-permute-start | bytes 835592 | tf_op jit(solution)/shard_map/ppermute | solution.py:21
  4.6 26.6 %collective-permute-start.23 = (bf16[64,2176]{1,0:T(8,128)(2,1)S(1)}, bf16[64,2176]{1,0:T(8,128)(2,1)S(1)}, u32[]{:S(2)}, u32[]{:S(2)}) collective-permute-start(bf16[64,2176]{1,0:T(8,128)(2,1)S(1)} %get-tuple-element.48), channel_id=1, source_target_pairs={{0,12},{4,8},{8,4},{12,0},{16,28},{20,24},{24,20},{28,16},{1,13},{... | collective-permute-start | bytes 835592 | tf_op jit(solution)/shard_map/ppermute | solution.py:21
  6.0 22.3 %collective-permute-start.14 = (bf16[32,2176]{1,0:T(8,128)(2,1)S(1)}, bf16[32,2176]{1,0:T(8,128)(2,1)S(1)}, u32[]{:S(2)}, u32[]{:S(2)}) collective-permute-start(bf16[32,2176]{1,0:T(8,128)(2,1)S(1)} %get-tuple-element.44), channel_id=1, source_target_pairs={{0,20},{4,16},{8,28},{12,24},{16,4},{20,0},{24,12},{28,8},{1,21},{... | collective-permute-start | bytes 417800 | tf_op jit(solution)/shard_map/ppermute | solution.py:21
  8.6 20.4 %collective-permute-start.4 = (bf16[32,2176]{1,0:T(8,128)(2,1)S(1)}, bf16[32,2176]{1,0:T(8,128)(2,1)S(1)}, u32[]{:S(2)}, u32[]{:S(2)}) collective-permute-start(bf16[32,2176]{1,0:T(8,128)(2,1)S(1)} %get-tuple-element.39), channel_id=1, source_target_pairs={{0,24},{4,28},{8,16},{12,20},{16,8},{20,12},{24,0},{28,4},{1,25},{... | collective-permute-start | bytes 417800 | tf_op jit(solution)/shard_map/ppermute | solution.py:21
  10.2 20.3 %collective-permute-start.5 = (bf16[32,2176]{1,0:T(8,128)(2,1)S(1)}, bf16[32,2176]{1,0:T(8,128)(2,1)S(1)}, u32[]{:S(2)}, u32[]{:S(2)}) collective-permute-start(bf16[32,2176]{1,0:T(8,128)(2,1)S(1)} %get-tuple-element.40), channel_id=1, source_target_pairs={{0,28},{4,24},{8,20},{12,16},{16,12},{20,8},{24,4},{28,0},{1,29},{... | collective-permute-start | bytes 417800 | tf_op jit(solution)/shard_map/ppermute | solution.py:21
  28.3 6.5 %collective-permute-start = (bf16[64,2176]{1,0:T(8,128)(2,1)S(1)}, bf16[64,2176]{1,0:T(8,128)(2,1)S(1)}, u32[]{:S(2)}, u32[]{:S(2)}) collective-permute-start(bf16[64,2176]{1,0:T(8,128)(2,1)S(1)} %get-tuple-element.32), channel_id=1, source_target_pairs={{0,4},{4,0},{8,12},{12,8},{16,20},{20,16},{24,28},{28,24},{1,5},{5... | collective-permute-start | bytes 835592 | tf_op jit(solution)/shard_map/ppermute | solution.py:21
  29.0 9.7 %collective-permute-start.15 = (bf16[64,2176]{1,0:T(8,128)(2,1)S(1)}, bf16[64,2176]{1,0:T(8,128)(2,1)S(1)}, u32[]{:S(2)}, u32[]{:S(2)}) collective-permute-start(bf16[64,2176]{1,0:T(8,128)(2,1)S(1)} %constant_dynamic-update-slice_fusion.2.refs_0_), channel_id=1, source_target_pairs={{0,2},{1,3},{2,0},{3,1},{4,6},{5,7},{6,4},{7,5},{8,10},{9,11},{10,... | collective-permute-start | bytes 835592 | tf_op jit(solution)/shard_map/ppermute | solution.py:26
  30.5 10.6 %collective-permute-start.6 = (bf16[64,2176]{1,0:T(8,128)(2,1)S(1)}, bf16[64,2176]{1,0:T(8,128)(2,1)S(1)}, u32[]{:S(2)}, u32[]{:S(2)}) collective-permute-start(bf16[64,2176]{1,0:T(8,128)(2,1)S(1)} %constant_dynamic-update-slice_fusion.refs_0_), channel_id=1, source_target_pairs={{0,2},{1,3},{2,0},{3,1},{4,6},{5,7},{6,4},{7,5},{8,10},{9,11},{10,... | collective-permute-start | bytes 835592 | tf_op jit(solution)/shard_map/ppermute | solution.py:26
  31.2 10.0 %collective-permute-start.24 = (bf16[64,2176]{1,0:T(8,128)(2,1)S(1)}, bf16[64,2176]{1,0:T(8,128)(2,1)S(1)}, u32[]{:S(2)}, u32[]{:S(2)}) collective-permute-start(bf16[64,2176]{1,0:T(8,128)(2,1)S(1)} %collective-permute-done.22.refs_0_), channel_id=1, source_target_pairs={{0,1},{1,0},{2,3},{3,2},{4,5},{5,4},{6,7},{7,6},{8,9},{9,8},{10,11... | collective-permute-start | bytes 835592 | tf_op jit(solution)/shard_map/ppermute | solution.py:26
  31.2 10.5 %collective-permute-start.25 = (bf16[64,2176]{1,0:T(8,128)(2,1)S(1)}, bf16[64,2176]{1,0:T(8,128)(2,1)S(1)}, u32[]{:S(2)}, u32[]{:S(2)}) collective-permute-start(bf16[64,2176]{1,0:T(8,128)(2,1)S(1)} %collective-permute-done.23.refs_1_), channel_id=1, source_target_pairs={{0,1},{1,0},{2,3},{3,2},{4,5},{5,4},{6,7},{7,6},{8,9},{9,8},{10,11... | collective-permute-start | bytes 835592 | tf_op jit(solution)/shard_map/ppermute | solution.py:26
  34.9 10.0 %collective-permute-start.1 = (bf16[64,2176]{1,0:T(8,128)(2,1)S(1)}, bf16[64,2176]{1,0:T(8,128)(2,1)S(1)}, u32[]{:S(2)}, u32[]{:S(2)}) collective-permute-start(bf16[64,2176]{1,0:T(8,128)(2,1)S(1)} %collective-permute-done.refs_1_), channel_id=1, source_target_pairs={{0,1},{1,0},{2,3},{3,2},{4,5},{5,4},{6,7},{7,6},{8,9},{9,8},{10,11... | collective-permute-start | bytes 835592 | tf_op jit(solution)/shard_map/ppermute | solution.py:26
  38.7 9.9 %collective-permute-start.16 = (bf16[64,2176]{1,0:T(8,128)(2,1)S(1)}, bf16[64,2176]{1,0:T(8,128)(2,1)S(1)}, u32[]{:S(2)}, u32[]{:S(2)}) collective-permute-start(bf16[64,2176]{1,0:T(8,128)(2,1)S(1)} %constant_dynamic-update-slice_fusion.2.refs_0_), channel_id=1, source_target_pairs={{0,1},{1,0},{2,3},{3,2},{4,5},{5,4},{6,7},{7,6},{8,9},{9,8},{10,11... | collective-permute-start | bytes 835592 | tf_op jit(solution)/shard_map/ppermute | solution.py:26
  41.1 11.3 %collective-permute-start.7 = (bf16[64,2176]{1,0:T(8,128)(2,1)S(1)}, bf16[64,2176]{1,0:T(8,128)(2,1)S(1)}, u32[]{:S(2)}, u32[]{:S(2)}) collective-permute-start(bf16[64,2176]{1,0:T(8,128)(2,1)S(1)} %constant_dynamic-update-slice_fusion.refs_0_), channel_id=1, source_target_pairs={{0,1},{1,0},{2,3},{3,2},{4,5},{5,4},{6,7},{7,6},{8,9},{9,8},{10,11... | collective-permute-start | bytes 835592 | tf_op jit(solution)/shard_map/ppermute | solution.py:26
  41.1 7.6 %collective-permute-start.17 = (bf16[64,2176]{1,0:T(8,128)(2,1)S(1)}, bf16[64,2176]{1,0:T(8,128)(2,1)S(1)}, u32[]{:S(2)}, u32[]{:S(2)}) collective-permute-start(bf16[64,2176]{1,0:T(8,128)(2,1)S(1)} %collective-permute-done.15.refs_1_), channel_id=1, source_target_pairs={{0,1},{1,0},{2,3},{3,2},{4,5},{5,4},{6,7},{7,6},{8,9},{9,8},{10,11... | collective-permute-start | bytes 835592 | tf_op jit(solution)/shard_map/ppermute | solution.py:26
  41.6 10.8 %collective-permute-start.8 = (bf16[64,2176]{1,0:T(8,128)(2,1)S(1)}, bf16[64,2176]{1,0:T(8,128)(2,1)S(1)}, u32[]{:S(2)}, u32[]{:S(2)}) collective-permute-start(bf16[64,2176]{1,0:T(8,128)(2,1)S(1)} %collective-permute-done.6.refs_1_), channel_id=1, source_target_pairs={{0,1},{1,0},{2,3},{3,2},{4,5},{5,4},{6,7},{7,6},{8,9},{9,8},{10,11... | collective-permute-start | bytes 835592 | tf_op jit(solution)/shard_map/ppermute | solution.py:26
  44.9 12.4 %collective-permute-start.26 = (bf16[128,2048]{1,0:T(8,128)(2,1)S(1)}, bf16[128,2048]{1,0:T(8,128)(2,1)S(1)}, u32[]{:S(2)}, u32[]{:S(2)}) collective-permute-start(bf16[128,2048]{1,0:T(8,128)(2,1)S(1)} %get-tuple-element.50), channel_id=1, source_target_pairs={{0,1},{1,0},{2,3},{3,2},{4,5},{5,4},{6,7},{7,6},{8,9},{9,8},{10,11... | collective-permute-start | bytes 1572872 | tf_op jit(solution)/shard_map/ppermute | solution.py:26
  48.6 7.2 %collective-permute-start.2 = (bf16[64,2048]{1,0:T(8,128)(2,1)S(1)}, bf16[64,2048]{1,0:T(8,128)(2,1)S(1)}, u32[]{:S(2)}, u32[]{:S(2)}) collective-permute-start(bf16[64,2048]{1,0:T(8,128)(2,1)S(1)} %get-tuple-element.37), channel_id=1, source_target_pairs={{0,1},{1,0},{2,3},{3,2},{4,5},{5,4},{6,7},{7,6},{8,9},{9,8},{10,11... | collective-permute-start | bytes 786440 | tf_op jit(solution)/shard_map/ppermute | solution.py:26
  51.9 9.0 %collective-permute-start.18 = (bf16[128,2048]{1,0:T(8,128)(2,1)S(1)}, bf16[128,2048]{1,0:T(8,128)(2,1)S(1)}, u32[]{:S(2)}, u32[]{:S(2)}) collective-permute-start(bf16[128,2048]{1,0:T(8,128)(2,1)S(1)} %get-tuple-element.46), channel_id=1, source_target_pairs={{0,1},{1,0},{2,3},{3,2},{4,5},{5,4},{6,7},{7,6},{8,9},{9,8},{10,11... | collective-permute-start | bytes 1572872 | tf_op jit(solution)/shard_map/ppermute | solution.py:26
  55.6 7.0 %collective-permute-start.9 = (bf16[128,2048]{1,0:T(8,128)(2,1)S(1)}, bf16[128,2048]{1,0:T(8,128)(2,1)S(1)}, u32[]{:S(2)}, u32[]{:S(2)}) collective-permute-start(bf16[128,2048]{1,0:T(8,128)(2,1)S(1)} %get-tuple-element.42), channel_id=1, source_target_pairs={{0,1},{1,0},{2,3},{3,2},{4,5},{5,4},{6,7},{7,6},{8,9},{9,8},{10,11... | collective-permute-start | bytes 1572872 | tf_op jit(solution)/shard_map/ppermute | solution.py:26
  55.8 20.2 %collective-permute-start.3 = (bf16[64,2048]{1,0:T(8,128)(2,1)S(1)}, bf16[64,2048]{1,0:T(8,128)(2,1)S(1)}, u32[]{:S(2)}, u32[]{:S(2)}) collective-permute-start(bf16[64,2048]{1,0:T(8,128)(2,1)S(1)} %add_convert_fusion.1), channel_id=1, source_target_pairs={{0,4},{4,0},{8,12},{12,8},{16,20},{20,16},{24,28},{28,24},{1,5},{5... | collective-permute-start | bytes 786440 | tf_op jit(solution)/shard_map/ppermute | solution.py:21
  57.4 21.6 %collective-permute-start.27 = (bf16[64,2048]{1,0:T(8,128)(2,1)S(1)}, bf16[64,2048]{1,0:T(8,128)(2,1)S(1)}, u32[]{:S(2)}, u32[]{:S(2)}) collective-permute-start(bf16[64,2048]{1,0:T(8,128)(2,1)S(1)} %get-tuple-element.54), channel_id=1, source_target_pairs={{0,8},{4,12},{8,0},{12,4},{16,24},{20,28},{24,16},{28,20},{1,9},{5... | collective-permute-start | bytes 786440 | tf_op jit(solution)/shard_map/ppermute | solution.py:21
  60.8 25.5 %collective-permute-start.28 = (bf16[64,2048]{1,0:T(8,128)(2,1)S(1)}, bf16[64,2048]{1,0:T(8,128)(2,1)S(1)}, u32[]{:S(2)}, u32[]{:S(2)}) collective-permute-start(bf16[64,2048]{1,0:T(8,128)(2,1)S(1)} %get-tuple-element.53), channel_id=1, source_target_pairs={{0,12},{4,8},{8,4},{12,0},{16,28},{20,24},{24,20},{28,16},{1,13},{... | collective-permute-start | bytes 786440 | tf_op jit(solution)/shard_map/ppermute | solution.py:21
  61.1 9.2 %collective-permute-start.19 = (bf16[64,2048]{1,0:T(8,128)(2,1)S(1)}, bf16[64,2048]{1,0:T(8,128)(2,1)S(1)}, u32[]{:S(2)}, u32[]{:S(2)}) collective-permute-start(bf16[64,2048]{1,0:T(8,128)(2,1)S(1)} %slice.76), channel_id=1, source_target_pairs={{0,2},{1,3},{2,0},{3,1},{4,6},{5,7},{6,4},{7,5},{8,10},{9,11},{10,... | collective-permute-start | bytes 786440 | tf_op jit(solution)/shard_map/ppermute | solution.py:26
  62.8 12.1 %collective-permute-start.10 = (bf16[64,2048]{1,0:T(8,128)(2,1)S(1)}, bf16[64,2048]{1,0:T(8,128)(2,1)S(1)}, u32[]{:S(2)}, u32[]{:S(2)}) collective-permute-start(bf16[64,2048]{1,0:T(8,128)(2,1)S(1)} %slice.77), channel_id=1, source_target_pairs={{0,2},{1,3},{2,0},{3,1},{4,6},{5,7},{6,4},{7,5},{8,10},{9,11},{10,... | collective-permute-start | bytes 786440 | tf_op jit(solution)/shard_map/ppermute | solution.py:26
  70.5 15.8 %collective-permute-start.20 = (bf16[32,2048]{1,0:T(8,128)(2,1)S(1)}, bf16[32,2048]{1,0:T(8,128)(2,1)S(1)}, u32[]{:S(2)}, u32[]{:S(2)}) collective-permute-start(bf16[32,2048]{1,0:T(8,128)(2,1)S(1)} %get-tuple-element.56), channel_id=1, source_target_pairs={{0,16},{4,20},{8,24},{12,28},{16,0},{20,4},{24,8},{28,12},{1,17},{... | collective-permute-start | bytes 393224 | tf_op jit(solution)/shard_map/ppermute | solution.py:21
  74.9 13.3 %collective-permute-start.21 = (bf16[32,2048]{1,0:T(8,128)(2,1)S(1)}, bf16[32,2048]{1,0:T(8,128)(2,1)S(1)}, u32[]{:S(2)}, u32[]{:S(2)}) collective-permute-start(bf16[32,2048]{1,0:T(8,128)(2,1)S(1)} %get-tuple-element.55), channel_id=1, source_target_pairs={{0,20},{4,16},{8,28},{12,24},{16,4},{20,0},{24,12},{28,8},{1,21},{... | collective-permute-start | bytes 393224 | tf_op jit(solution)/shard_map/ppermute | solution.py:21
  76.0 16.4 %collective-permute-start.11 = (bf16[32,2048]{1,0:T(8,128)(2,1)S(1)}, bf16[32,2048]{1,0:T(8,128)(2,1)S(1)}, u32[]{:S(2)}, u32[]{:S(2)}) collective-permute-start(bf16[32,2048]{1,0:T(8,128)(2,1)S(1)} %get-tuple-element.58), channel_id=1, source_target_pairs={{0,24},{4,28},{8,16},{12,20},{16,8},{20,12},{24,0},{28,4},{1,25},{... | collective-permute-start | bytes 393224 | tf_op jit(solution)/shard_map/ppermute | solution.py:21
  79.1 16.4 %collective-permute-start.12 = (bf16[32,2048]{1,0:T(8,128)(2,1)S(1)}, bf16[32,2048]{1,0:T(8,128)(2,1)S(1)}, u32[]{:S(2)}, u32[]{:S(2)}) collective-permute-start(bf16[32,2048]{1,0:T(8,128)(2,1)S(1)} %get-tuple-element.57), channel_id=1, source_target_pairs={{0,28},{4,24},{8,20},{12,16},{16,12},{20,8},{24,4},{28,0},{1,29},{... | collective-permute-start | bytes 393224 | tf_op jit(solution)/shard_map/ppermute | solution.py:21
  96.7 2.0 %collective-permute-start.29 = (bf16[128,2048]{1,0:T(8,128)(2,1)S(1)}, bf16[128,2048]{1,0:T(8,128)(2,1)S(1)}, u32[]{:S(2)}, u32[]{:S(2)}) collective-permute-start(bf16[128,2048]{1,0:T(8,128)(2,1)S(1)} %get-tuple-element.52), channel_id=1, source_target_pairs={{0,1},{1,0},{2,3},{3,2},{4,5},{5,4},{6,7},{7,6},{8,9},{9,8},{10,11... | collective-permute-start | bytes 1572872 | tf_op jit(solution)/shard_map/ppermute | solution.py:26
  98.9 8.4 %collective-permute-start.30 = (bf16[64,2048]{1,0:T(8,128)(2,1)S(1)}, bf16[64,2048]{1,0:T(8,128)(2,1)S(1)}, u32[]{:S(2)}, u32[]{:S(2)}) collective-permute-start(bf16[64,2048]{1,0:T(8,128)(2,1)S(1)} %slice.75), channel_id=1, source_target_pairs={{0,2},{1,3},{2,0},{3,1},{4,6},{5,7},{6,4},{7,5},{8,10},{9,11},{10,... | collective-permute-start | bytes 786440 | tf_op jit(solution)/shard_map/ppermute | solution.py:26

commit v4 on v3

--- a/solution.py
+++ b/solution.py
@@ -44,8 +44,9 @@
 
 
 def route_kernel(pieces, node_count, s_ref, ids_hbm, score_hbm, tok_hbm, *refs):
-    outs = refs[: len(pieces)]
-    late_ref, early_ref, hot, rows, ids_ref, score_ref, tok_ref, sems = refs[len(pieces):]
+    sent = sum(p[4] for p in pieces)
+    outs = refs[:sent]
+    late_ref, early_ref, hot, rows, ids_ref, score_ref, tok_ref, sems = refs[sent:]
     copies = [
         pltpu.make_async_copy(src, dst, sems.at[i])
         for i, (src, dst) in enumerate(((ids_hbm, ids_ref), (score_hbm, score_ref), (tok_hbm, tok_ref)))
@@ -74,8 +75,8 @@
     position = jnp.dot(member.astype(BF16), upper, preferred_element_type=F32) - 1.0
     position = jnp.where(member > 0.0, position, -1.0).astype(jnp.int32)
     offset = 0
-    for k, base, count in pieces:
-        first = 0 if base is None else s_ref[base] * count
+    for k, base, count, rel, _ in pieces:
+        first = 0 if base is None else (s_ref[base] ^ rel) * count
         slot = lax.broadcasted_iota(jnp.int32, (count, tok_rows), 0) + first
         hot[offset : offset + count, :] = jnp.where(position[k : k + 1] == slot, 1.0, 0.0)
         offset += count
@@ -91,7 +92,7 @@
         parts.append(jnp.zeros((extra - 2 * experts, tok_rows), BF16))
     table = jnp.concatenate(parts, axis=0)
     copies[2].wait()
-    aligned = all(count % 16 == 0 for _, _, count in pieces)
+    aligned = all(p[2] % 16 == 0 for p in pieces)
     for c, w in column_blocks(width) + [(width, extra)]:
         if c < width:
             value = jnp.dot(one_hot, tok_ref[:, c : c + w], preferred_element_type=F32)
@@ -100,9 +101,11 @@
         if not aligned:
             rows[:, :w] = value
             value = rows
-        offset = 0
-        for out, (_, _, count) in zip(outs, pieces):
-            out[:, c : c + w] = value[offset : offset + count, :w].astype(BF16)
+        offset, index = 0, 0
+        for _, _, count, _, goes in pieces:
+            if goes:
+                outs[index][:, c : c + w] = value[offset : offset + count, :w].astype(BF16)
+                index += 1
             offset += count
 
 
@@ -114,10 +117,10 @@
     tail = sum(p[2] for p in pieces[-2:])
     res = pl.pallas_call(
         functools.partial(route_kernel, pieces, node_count),
-        out_shape=[jax.ShapeDtypeStruct((p[2], full), BF16) for p in pieces]
+        out_shape=[jax.ShapeDtypeStruct((p[2], full), BF16) for p in pieces if p[4]]
         + [jax.ShapeDtypeStruct((count, tok_rows), BF16) for count in (total - tail, tail)],
         in_specs=[SMEM, HBM, HBM, HBM],
-        out_specs=[VMEM] * (len(pieces) + 2),
+        out_specs=[VMEM] * (sum(p[4] for p in pieces) + 2),
         scratch_shapes=[
             pltpu.VMEM((total, tok_rows), F32),
             pltpu.VMEM((total, 512), F32),
@@ -352,8 +355,15 @@
     slow_bits = [1 << b for b in range(1, local_count.bit_length() - 1)]
     chunks = far_chunks(node_count)
     near = [k for k in range(1, NEAR)]
-    pieces = [(k, 1, capacity // local_count) for ks in chunks for k in ks]
-    pieces += [(k, 3, capacity // 2) for k in near[1:] + near[:1]] + [(0, None, capacity)]
+    whole_k = chunks[0][-1]
+    slow = [0]
+    for bit in slow_bits:
+        slow = slow + [i ^ bit for i in slow]
+    pieces = []
+    for k in (k for ks in chunks for k in ks):
+        rels = slow if k == whole_k else slow[:1]
+        pieces += [(k, 1, capacity // local_count, rel, rel == 0) for rel in rels]
+    pieces += [(k, 3, capacity // 2, 0, True) for k in near[1:] + near[:1]] + [(0, None, capacity, 0, True)]
     in_hbm = functools.partial(pltpu.with_memory_space_constraint, memory_space=pltpu.HBM)
     sends, late_hot, early_hot = route(
         scalars, in_hbm(expert_ids.T), in_hbm(gate_scores.T), in_hbm(tokens), tuple(pieces), node_count
@@ -409,10 +419,19 @@
     returned = []
     for ks, got in zip(chunks, arrived):
         value = experts_of(gather(got))
+        count = capacity // local_count
+        back = {}
+        if whole_k in ks:
+            runs = [value[i : i + len(ks) * count] for i in range(0, value.shape[0], len(ks) * count)]
+            cut = ks.index(whole_k) * count
+            whole = jnp.concatenate([r[cut : cut + count] for r in runs], axis=0).astype(BF16)
+            back[whole_k] = xor_node(whole, whole_k)
+            value = jnp.concatenate([r[:cut] for r in runs], axis=0)
+        rest = [k for k in ks if k != whole_k]
         value = fold(value, slow_bits[::-1]).astype(BF16)
-        count = value.shape[0] // len(ks)
-        for i, k in enumerate(ks):
-            returned.append(xor_node(value[i * count : (i + 1) * count], k))
+        for i, k in enumerate(rest):
+            back[k] = xor_node(value[i * count : (i + 1) * count], k)
+        returned += [back[k] for k in ks]
 
     order = [0]
     for bit in slow_bits:

time: 108 us -> 118 us (1.093)
  the two profiles are of different devices: /device:TPU:16 before, /device:TPU:0 now
where the time goes in v4:
time: 118 us
  waiting for transfers between devices  50.9 us (43%)
  starting transfers between devices  37.4 us (32%)
  Pallas kernels  27.6 us (23%)
  other arithmetic  1.5 us (1%)
    ppermute x14, waiting for transfers between devices, xor_node(): return lax.ppermute(x, 'node', [(i, i ^ k) for i in range(count)])  31.7 us
    ppermute x14, starting transfers between devices, xor_node(): return lax.ppermute(x, 'node', [(i, i ^ k) for i in range(count)])  27.6 us
    ppermute x17, waiting for transfers between devices, xor_local(): return lax.ppermute(x, 'local', [(i, i ^ k) for i in range(count)])  19.2 us
    pallas_call x4, Pallas kernels, ffn(): pl.pallas_call(functools.partial(ffn_kernel, counts, experts, ranges), ou...  12.7 us
    ppermute x17, starting transfers between devices, xor_local(): return lax.ppermute(x, 'local', [(i, i ^ k) for i in range(count)])  9.77 us
    pallas_call x1, Pallas kernels, shared(): pl.pallas_call(shared_kernel, grid=(hidden // block,), out_shape=jax.Shap...  5.86 us
    pallas_call x1, Pallas kernels, stage(): pl.pallas_call(stage_kernel, out_shape=[jax.ShapeDtypeStruct(w.shape, w.d...  3.78 us
    pallas_call x2, Pallas kernels, combine(): pl.pallas_call(functools.partial(combine_kernel if final else early_kerne...  2.65 us
  transfers between devices with their start and end apart: 31, of which 11 were waited for; matrix products, arithmetic and copies ran while one was open for 1% of the time, Pallas kernels for 20%

profile of v4, /device:TPU:0, one launch (start us, length us, event | category | flops | bytes accessed | tf_op | source)
XLA Modules:
  0.0 117.9 jit_solution(18104077041176570193)
XLA Ops:
  0.1 2.6 %route.1 = (bf16[32,2176]{1,0:T(8,128)(2,1)S(1)}, bf16[32,2176]{1,0:T(8,128)(2,1)S(1)}, bf16[32,2176]{1,0:T(8,128)(2,1)S(1)}, bf16[32,2176]{1,0:T(8,128)(2,1)S(1...) custom-call(s32[4]{0:T(128)S(1)} %pad_add_fusion.s_ref, ...), custom_call_target="tpu_custom_call" | custom-call | flops 534773760 | bytes 3137536 | tf_op jit(solution)/shard_map/route/pallas_call | solution.py:118
  2.7 4.1 %collective-permute-start.13 = (bf16[32,2176]{1,0:T(8,128)(2,1)S(1)}, bf16[32,2176]{1,0:T(8,128)(2,1)S(1)}, u32[]{:S(2)}, u32[]{:S(2)}) collective-permute-start(bf16[32,2176]{1,0:T(8,128)(2,1)S(1)} %get-tuple-element.43), channel_id=1, source_target_pairs={{0,16},{4,20},{8,24},{12,28},{16,0},{20,4},{24,8},{28,12},{1,17},{... | collective-permute-start | bytes 417800 | tf_op jit(solution)/shard_map/ppermute | solution.py:21
  6.8 1.6 %collective-permute-start.22 = (bf16[64,2176]{1,0:T(8,128)(2,1)S(1)}, bf16[64,2176]{1,0:T(8,128)(2,1)S(1)}, u32[]{:S(2)}, u32[]{:S(2)}) collective-permute-start(bf16[64,2176]{1,0:T(8,128)(2,1)S(1)} %get-tuple-element.47), channel_id=1, source_target_pairs={{0,8},{4,12},{8,0},{12,4},{16,24},{20,28},{24,16},{28,20},{1,9},{5... | collective-permute-start | bytes 835592 | tf_op jit(solution)/shard_map/ppermute | solution.py:21
  8.4 1.4 %collective-permute-start.23 = (bf16[64,2176]{1,0:T(8,128)(2,1)S(1)}, bf16[64,2176]{1,0:T(8,128)(2,1)S(1)}, u32[]{:S(2)}, u32[]{:S(2)}) collective-permute-start(bf16[64,2176]{1,0:T(8,128)(2,1)S(1)} %get-tuple-element.48), channel_id=1, source_target_pairs={{0,12},{4,8},{8,4},{12,0},{16,28},{20,24},{24,20},{28,16},{1,13},{... | collective-permute-start | bytes 835592 | tf_op jit(solution)/shard_map/ppermute | solution.py:21
  9.8 3.9 %collective-permute-start.4 = (bf16[32,2176]{1,0:T(8,128)(2,1)S(1)}, bf16[32,2176]{1,0:T(8,128)(2,1)S(1)}, u32[]{:S(2)}, u32[]{:S(2)}) collective-permute-start(bf16[32,2176]{1,0:T(8,128)(2,1)S(1)} %get-tuple-element.39), channel_id=1, source_target_pairs={{0,24},{4,28},{8,16},{12,20},{16,8},{20,12},{24,0},{28,4},{1,25},{... | collective-permute-start | bytes 417800 | tf_op jit(solution)/shard_map/ppermute | solution.py:21
  14.4 3.7 %collective-permute-start.5 = (bf16[32,2176]{1,0:T(8,128)(2,1)S(1)}, bf16[32,2176]{1,0:T(8,128)(2,1)S(1)}, u32[]{:S(2)}, u32[]{:S(2)}) collective-permute-start(bf16[32,2176]{1,0:T(8,128)(2,1)S(1)} %get-tuple-element.40), channel_id=1, source_target_pairs={{0,28},{4,24},{8,20},{12,16},{16,12},{20,8},{24,4},{28,0},{1,29},{... | collective-permute-start | bytes 417800 | tf_op jit(solution)/shard_map/ppermute | solution.py:21
  18.1 10.1 %collective-permute-done.14 = bf16[32,2176]{1,0:T(8,128)(2,1)S(1)} collective-permute-done((bf16[32,2176]{1,0:T(8,128)(2,1)S(1)}, bf16[32,2176]{1,0:T(8,128)(2,1)S(1)}, u32[]{:S(2)}, u32[]{:S(2)}) %collective-permute-start.14) | collective-permute-done | bytes 139296 | tf_op jit(solution)/shard_map/ppermute | solution.py:21
  28.2 1.4 %collective-permute-start = (bf16[64,2176]{1,0:T(8,128)(2,1)S(1)}, bf16[64,2176]{1,0:T(8,128)(2,1)S(1)}, u32[]{:S(2)}, u32[]{:S(2)}) collective-permute-start(bf16[64,2176]{1,0:T(8,128)(2,1)S(1)} %get-tuple-element.32), channel_id=1, source_target_pairs={{0,4},{4,0},{8,12},{12,8},{16,20},{20,16},{24,28},{28,24},{1,5},{5... | collective-permute-start | bytes 835592 | tf_op jit(solution)/shard_map/ppermute | solution.py:21
  29.6 1.9 %collective-permute-done.4 = bf16[32,2176]{1,0:T(8,128)(2,1)S(1)} collective-permute-done((bf16[32,2176]{1,0:T(8,128)(2,1)S(1)}, bf16[32,2176]{1,0:T(8,128)(2,1)S(1)}, u32[]{:S(2)}, u32[]{:S(2)}) %collective-permute-start.4) | collective-permute-done | bytes 139296 | tf_op jit(solution)/shard_map/ppermute | solution.py:21
  31.5 1.5 %collective-permute-start.15 = (bf16[64,2176]{1,0:T(8,128)(2,1)S(1)}, bf16[64,2176]{1,0:T(8,128)(2,1)S(1)}, u32[]{:S(2)}, u32[]{:S(2)}) collective-permute-start(bf16[64,2176]{1,0:T(8,128)(2,1)S(1)} %constant_dynamic-update-slice_fusion.2.refs_0_), channel_id=1, source_target_pairs={{0,2},{1,3},{2,0},{3,1},{4,6},{5,7},{6,4},{7,5},{8,10},{9,11},{10,... | collective-permute-start | bytes 835592 | tf_op jit(solution)/shard_map/ppermute | solution.py:26
  33.1 1.4 %collective-permute-done.5 = bf16[32,2176]{1,0:T(8,128)(2,1)S(1)} collective-permute-done((bf16[32,2176]{1,0:T(8,128)(2,1)S(1)}, bf16[32,2176]{1,0:T(8,128)(2,1)S(1)}, u32[]{:S(2)}, u32[]{:S(2)}) %collective-permute-start.5) | collective-permute-done | bytes 139296 | tf_op jit(solution)/shard_map/ppermute | solution.py:21
  34.5 1.6 %collective-permute-start.6 = (bf16[64,2176]{1,0:T(8,128)(2,1)S(1)}, bf16[64,2176]{1,0:T(8,128)(2,1)S(1)}, u32[]{:S(2)}, u32[]{:S(2)}) collective-permute-start(bf16[64,2176]{1,0:T(8,128)(2,1)S(1)} %constant_dynamic-update-slice_fusion.refs_0_), channel_id=1, source_target_pairs={{0,2},{1,3},{2,0},{3,1},{4,6},{5,7},{6,4},{7,5},{8,10},{9,11},{10,... | collective-permute-start | bytes 835592 | tf_op jit(solution)/shard_map/ppermute | solution.py:26
  37.6 3.8 %stage.1 = (bf16[1,2048,768]{2,1,0:T(8,128)(2,1)S(1)}, bf16[1,2048,768]{2,1,0:T(8,128)(2,1)S(1)}, bf16[1,768,2048]{2,1,0:T(8,128)(2,1)S(1)}) custom-call(bf16[1,2048,768]{2,1,0:T(8,128)(2,1)} %refs_0_.1, bf16[1,2048,768]{2,1,0:T(8,128)(2,1)} %refs_1_.1, bf16[1,768,2048]{2,1,0:T(8,128)(2,1)} %refs_2_.1), custom_call_target="tpu_custom_call" | custom-call | bytes 18874368 | tf_op jit(solution)/shard_map/stage/pallas_call | solution.py:212
  42.0 2.1 %collective-permute-done.6.refs_1_ = bf16[64,2176]{1,0:T(8,128)(2,1)S(1)} collective-permute-done((bf16[64,2176]{1,0:T(8,128)(2,1)S(1)}, bf16[64,2176]{1,0:T(8,128)(2,1)S(1)}, u32[]{:S(2)}, u32[]{:S(2)}) %collective-permute-start.6) | collective-permute-done | bytes 278560 | tf_op jit(solution)/shard_map/ppermute | solution.py:26
  44.6 3.2 %shard_map.95 = (f32[128,2048]{1,0:T(8,128)S(1)}, bf16[128,2048]{1,0:T(8,128)(2,1)S(1)}) custom-call(s32[4]{0:T(128)S(1)} %pad_add_fusion.s_ref, bf16[64,2176]{1,0:T(8,128)(2,1)S(1)} %collective-permute-done.22.refs_0_, bf16[64,2176]{1,0:T(8,128)(2,1)S(1)} %collective-permute-done.23.refs_1_, bf16[64,2176]{1,0:T(8,128)(2,1)S(1)} %collective-permute-done.24.refs_2_, ...), custom_call_target="tpu_custom_call" | custom-call | flops 2415919104 | bytes 12582912 | tf_op jit(solution)/shard_map/pallas_call | solution.py:187
  48.3 3.2 %shard_map.91 = (bf16[128,2048]{1,0:T(8,128)(2,1)S(1)}, f32[64,2048]{1,0:T(8,128)S(1)}, bf16[64,2048]{1,0:T(8,128)(2,1)S(1)}) custom-call(s32[4]{0:T(128)S(1)} %pad_add_fusion.s_ref, bf16[128,2176]{1,0:T(8,128)(2,1)S(1)} %get-tuple-element.31.refs_0_, bf16[64,2176]{1,0:T(8,128)(2,1)S(1)} %collective-permute-done.refs_1_, ...), custom_call_target="tpu_custom_call" | custom-call | flops 2415919104 | bytes 12582912 | tf_op jit(solution)/shard_map/pallas_call | solution.py:187
  51.7 3.2 %shard_map.94 = (f32[128,2048]{1,0:T(8,128)S(1)}, bf16[128,2048]{1,0:T(8,128)(2,1)S(1)}) custom-call(s32[4]{0:T(128)S(1)} %pad_add_fusion.s_ref, bf16[64,2176]{1,0:T(8,128)(2,1)S(1)} %constant_dynamic-update-slice_fusion.2.refs_0_, bf16[64,2176]{1,0:T(8,128)(2,1)S(1)} %collective-permute-done.15.refs_1_, ...), custom_call_target="tpu_custom_call" | custom-call | flops 2415919104 | bytes 12582912 | tf_op jit(solution)/shard_map/pallas_call | solution.py:187
  55.3 3.2 %shard_map.93 = (f32[128,2048]{1,0:T(8,128)S(1)}, bf16[128,2048]{1,0:T(8,128)(2,1)S(1)}) custom-call(s32[4]{0:T(128)S(1)} %pad_add_fusion.s_ref, bf16[64,2176]{1,0:T(8,128)(2,1)S(1)} %constant_dynamic-update-slice_fusion.refs_0_, bf16[64,2176]{1,0:T(8,128)(2,1)S(1)} %collective-permute-done.6.refs_1_, bf16[64,2176]{1,0:T(8,128)(2,1)S(1)} %collective-permute-done.7.refs_2_, ...), custom_call_target="tpu_custom_call" | custom-call | flops 2415919104 | bytes 12582912 | tf_op jit(solution)/shard_map/pallas_call | solution.py:187
  58.7 1.5 %collective-permute-start.3 = (bf16[64,2048]{1,0:T(8,128)(2,1)S(1)}, bf16[64,2048]{1,0:T(8,128)(2,1)S(1)}, u32[]{:S(2)}, u32[]{:S(2)}) collective-permute-start(bf16[64,2048]{1,0:T(8,128)(2,1)S(1)} %add_convert_fusion.1), channel_id=1, source_target_pairs={{0,4},{4,0},{8,12},{12,8},{16,20},{20,16},{24,28},{28,24},{1,5},{5... | collective-permute-start | bytes 786440 | tf_op jit(solution)/shard_map/ppermute | solution.py:21
  60.5 2.0 %collective-permute-start.28 = (bf16[64,2048]{1,0:T(8,128)(2,1)S(1)}, bf16[64,2048]{1,0:T(8,128)(2,1)S(1)}, u32[]{:S(2)}, u32[]{:S(2)}) collective-permute-start(bf16[64,2048]{1,0:T(8,128)(2,1)S(1)} %get-tuple-element.55), channel_id=1, source_target_pairs={{0,12},{4,8},{8,4},{12,0},{16,28},{20,24},{24,20},{28,16},{1,13},{... | collective-permute-start | bytes 786440 | tf_op jit(solution)/shard_map/ppermute | solution.py:21
  62.7 1.6 %collective-permute-start.19 = (bf16[64,2048]{1,0:T(8,128)(2,1)S(1)}, bf16[64,2048]{1,0:T(8,128)(2,1)S(1)}, u32[]{:S(2)}, u32[]{:S(2)}) collective-permute-start(bf16[64,2048]{1,0:T(8,128)(2,1)S(1)} %slice.83), channel_id=1, source_target_pairs={{0,2},{1,3},{2,0},{3,1},{4,6},{5,7},{6,4},{7,5},{8,10},{9,11},{10,... | collective-permute-start | bytes 786440 | tf_op jit(solution)/shard_map/ppermute | solution.py:26
  65.1 8.3 %collective-permute-done.10 = bf16[32,2048]{1,0:T(8,128)(2,1)S(1)} collective-permute-done((bf16[32,2048]{1,0:T(8,128)(2,1)S(1)}, bf16[32,2048]{1,0:T(8,128)(2,1)S(1)}, u32[]{:S(2)}, u32[]{:S(2)}) %collective-permute-start.10) | collective-permute-done | bytes 131104 | tf_op jit(solution)/shard_map/ppermute | solution.py:26
  73.4 4.8 %collective-permute-start.12 = (bf16[64,2048]{1,0:T(8,128)(2,1)S(1)}, bf16[64,2048]{1,0:T(8,128)(2,1)S(1)}, u32[]{:S(2)}, u32[]{:S(2)}) collective-permute-start(bf16[64,2048]{1,0:T(8,128)(2,1)S(1)} %pad_maximum_fusion), channel_id=1, source_target_pairs={{0,28},{4,24},{8,20},{12,16},{16,12},{20,8},{24,4},{28,0},{1,29},{... | collective-permute-start | bytes 786440 | tf_op jit(solution)/shard_map/ppermute | solution.py:21
  79.4 2.1 %collective-permute-start.21 = (bf16[32,2048]{1,0:T(8,128)(2,1)S(1)}, bf16[32,2048]{1,0:T(8,128)(2,1)S(1)}, u32[]{:S(2)}, u32[]{:S(2)}) collective-permute-start(bf16[32,2048]{1,0:T(8,128)(2,1)S(1)} %get-tuple-element.60), channel_id=1, source_target_pairs={{0,20},{4,16},{8,28},{12,24},{16,4},{20,0},{24,12},{28,8},{1,21},{... | collective-permute-start | bytes 393224 | tf_op jit(solution)/shard_map/ppermute | solution.py:21
  81.4 5.9 %shared.1.shared_ref = f32[256,2048]{1,0:T(8,128)S(1)} custom-call(bf16[256,2048]{1,0:T(8,128)(2,1)} %x_ref.1, bf16[2048,512]{1,0:T(8,128)(2,1)} %wg_ref.1, bf16[2048,512]{1,0:T(8,128)(2,1)} %wu_ref.1, bf16[512,2048]{1,0:T(8,128)(2,1)} %wd_ref.1), custom_call_target="tpu_custom_call" | custom-call | flops 1610612736 | bytes 9437184 | tf_op jit(solution)/shard_map/shared/pallas_call | solution.py:246
  87.3 1.1 shard_map.92.base_ref
  88.5 14.3 %collective-permute-done.20.refs_2_ = bf16[32,2048]{1,0:T(8,128)(2,1)S(1)} collective-permute-done((bf16[32,2048]{1,0:T(8,128)(2,1)S(1)}, bf16[32,2048]{1,0:T(8,128)(2,1)S(1)}, u32[]{:S(2)}, u32[]{:S(2)}) %collective-permute-start.20) | collective-permute-done | bytes 131104 | tf_op jit(solution)/shard_map/ppermute | solution.py:21
  102.8 2.3 %collective-permute-done.21.refs_3_ = bf16[32,2048]{1,0:T(8,128)(2,1)S(1)} collective-permute-done((bf16[32,2048]{1,0:T(8,128)(2,1)S(1)}, bf16[32,2048]{1,0:T(8,128)(2,1)S(1)}, u32[]{:S(2)}, u32[]{:S(2)}) %collective-permute-start.21) | collective-permute-done | bytes 131104 | tf_op jit(solution)/shard_map/ppermute | solution.py:21
  105.0 1.5 %shard_map.96 = (f32[128,2048]{1,0:T(8,128)S(1)}, bf16[128,2048]{1,0:T(8,128)(2,1)S(1)}) custom-call(s32[4]{0:T(128)S(1)} %pad_add_fusion.s_ref, bf16[288,256]{1,0:T(8,128)(2,1)S(1)} %get-tuple-element.29.oh_ref, f32[256,2048]{1,0:T(8,128)S(1)} %shard_map.92.base_ref, bf16[32,2048]{1,0:T(8,128)(2,1)S(1)} %collective-permute-done.11.refs_0_, ...), custom_call_target="tpu_custom_call" | custom-call | flops 301989888 | bytes 4849664 | tf_op jit(solution)/shard_map/pallas_call | solution.py:312
  106.6 1.9 %collective-permute-done.29 = bf16[128,2048]{1,0:T(8,128)(2,1)S(1)} collective-permute-done((bf16[128,2048]{1,0:T(8,128)(2,1)S(1)}, bf16[128,2048]{1,0:T(8,128)(2,1)S(1)}, u32[]{:S(2)}, u32[]{:S(2)}) %collective-permute-start.29) | collective-permute-done | bytes 524320 | tf_op jit(solution)/shard_map/ppermute | solution.py:26
  108.7 1.5 %collective-permute-start.30 = (bf16[64,2048]{1,0:T(8,128)(2,1)S(1)}, bf16[64,2048]{1,0:T(8,128)(2,1)S(1)}, u32[]{:S(2)}, u32[]{:S(2)}) collective-permute-start(bf16[64,2048]{1,0:T(8,128)(2,1)S(1)} %slice.82), channel_id=1, source_target_pairs={{0,2},{1,3},{2,0},{3,1},{4,6},{5,7},{6,4},{7,5},{8,10},{9,11},{10,... | collective-permute-start | bytes 786440 | tf_op jit(solution)/shard_map/ppermute | solution.py:26
  110.2 6.9 %collective-permute-done.30 = bf16[64,2048]{1,0:T(8,128)(2,1)S(1)} collective-permute-done((bf16[64,2048]{1,0:T(8,128)(2,1)S(1)}, bf16[64,2048]{1,0:T(8,128)(2,1)S(1)}, u32[]{:S(2)}, u32[]{:S(2)}) %collective-permute-start.30) | collective-permute-done | bytes 262176 | tf_op jit(solution)/shard_map/ppermute | solution.py:26
  (58 shorter events, 8.3 us)
Async XLA Ops:
  2.7 11.7 %collective-permute-start.13 = (bf16[32,2176]{1,0:T(8,128)(2,1)S(1)}, bf16[32,2176]{1,0:T(8,128)(2,1)S(1)}, u32[]{:S(2)}, u32[]{:S(2)}) collective-permute-start(bf16[32,2176]{1,0:T(8,128)(2,1)S(1)} %get-tuple-element.43), channel_id=1, source_target_pairs={{0,16},{4,20},{8,24},{12,28},{16,0},{20,4},{24,8},{28,12},{1,17},{... | collective-permute-start | bytes 417800 | tf_op jit(solution)/shard_map/ppermute | solution.py:21
  6.8 29.2 %collective-permute-start.22 = (bf16[64,2176]{1,0:T(8,128)(2,1)S(1)}, bf16[64,2176]{1,0:T(8,128)(2,1)S(1)}, u32[]{:S(2)}, u32[]{:S(2)}) collective-permute-start(bf16[64,2176]{1,0:T(8,128)(2,1)S(1)} %get-tuple-element.47), channel_id=1, source_target_pairs={{0,8},{4,12},{8,0},{12,4},{16,24},{20,28},{24,16},{28,20},{1,9},{5... | collective-permute-start | bytes 835592 | tf_op jit(solution)/shard_map/ppermute | solution.py:21
  8.4 27.7 %collective-permute-start.23 = (bf16[64,2176]{1,0:T(8,128)(2,1)S(1)}, bf16[64,2176]{1,0:T(8,128)(2,1)S(1)}, u32[]{:S(2)}, u32[]{:S(2)}) collective-permute-start(bf16[64,2176]{1,0:T(8,128)(2,1)S(1)} %get-tuple-element.48), channel_id=1, source_target_pairs={{0,12},{4,8},{8,4},{12,0},{16,28},{20,24},{24,20},{28,16},{1,13},{... | collective-permute-start | bytes 835592 | tf_op jit(solution)/shard_map/ppermute | solution.py:21
  9.8 18.4 %collective-permute-start.14 = (bf16[32,2176]{1,0:T(8,128)(2,1)S(1)}, bf16[32,2176]{1,0:T(8,128)(2,1)S(1)}, u32[]{:S(2)}, u32[]{:S(2)}) collective-permute-start(bf16[32,2176]{1,0:T(8,128)(2,1)S(1)} %get-tuple-element.44), channel_id=1, source_target_pairs={{0,20},{4,16},{8,28},{12,24},{16,4},{20,0},{24,12},{28,8},{1,21},{... | collective-permute-start | bytes 417800 | tf_op jit(solution)/shard_map/ppermute | solution.py:21
  9.8 21.7 %collective-permute-start.4 = (bf16[32,2176]{1,0:T(8,128)(2,1)S(1)}, bf16[32,2176]{1,0:T(8,128)(2,1)S(1)}, u32[]{:S(2)}, u32[]{:S(2)}) collective-permute-start(bf16[32,2176]{1,0:T(8,128)(2,1)S(1)} %get-tuple-element.39), channel_id=1, source_target_pairs={{0,24},{4,28},{8,16},{12,20},{16,8},{20,12},{24,0},{28,4},{1,25},{... | collective-permute-start | bytes 417800 | tf_op jit(solution)/shard_map/ppermute | solution.py:21
  14.4 20.0 %collective-permute-start.5 = (bf16[32,2176]{1,0:T(8,128)(2,1)S(1)}, bf16[32,2176]{1,0:T(8,128)(2,1)S(1)}, u32[]{:S(2)}, u32[]{:S(2)}) collective-permute-start(bf16[32,2176]{1,0:T(8,128)(2,1)S(1)} %get-tuple-element.40), channel_id=1, source_target_pairs={{0,28},{4,24},{8,20},{12,16},{16,12},{20,8},{24,4},{28,0},{1,29},{... | collective-permute-start | bytes 417800 | tf_op jit(solution)/shard_map/ppermute | solution.py:21
  28.2 9.4 %collective-permute-start = (bf16[64,2176]{1,0:T(8,128)(2,1)S(1)}, bf16[64,2176]{1,0:T(8,128)(2,1)S(1)}, u32[]{:S(2)}, u32[]{:S(2)}) collective-permute-start(bf16[64,2176]{1,0:T(8,128)(2,1)S(1)} %get-tuple-element.32), channel_id=1, source_target_pairs={{0,4},{4,0},{8,12},{12,8},{16,20},{20,16},{24,28},{28,24},{1,5},{5... | collective-permute-start | bytes 835592 | tf_op jit(solution)/shard_map/ppermute | solution.py:21
  31.5 9.9 %collective-permute-start.15 = (bf16[64,2176]{1,0:T(8,128)(2,1)S(1)}, bf16[64,2176]{1,0:T(8,128)(2,1)S(1)}, u32[]{:S(2)}, u32[]{:S(2)}) collective-permute-start(bf16[64,2176]{1,0:T(8,128)(2,1)S(1)} %constant_dynamic-update-slice_fusion.2.refs_0_), channel_id=1, source_target_pairs={{0,2},{1,3},{2,0},{3,1},{4,6},{5,7},{6,4},{7,5},{8,10},{9,11},{10,... | collective-permute-start | bytes 835592 | tf_op jit(solution)/shard_map/ppermute | solution.py:26
  34.5 9.6 %collective-permute-start.6 = (bf16[64,2176]{1,0:T(8,128)(2,1)S(1)}, bf16[64,2176]{1,0:T(8,128)(2,1)S(1)}, u32[]{:S(2)}, u32[]{:S(2)}) collective-permute-start(bf16[64,2176]{1,0:T(8,128)(2,1)S(1)} %constant_dynamic-update-slice_fusion.refs_0_), channel_id=1, source_target_pairs={{0,2},{1,3},{2,0},{3,1},{4,6},{5,7},{6,4},{7,5},{8,10},{9,11},{10,... | collective-permute-start | bytes 835592 | tf_op jit(solution)/shard_map/ppermute | solution.py:26
  36.0 8.0 %collective-permute-start.24 = (bf16[64,2176]{1,0:T(8,128)(2,1)S(1)}, bf16[64,2176]{1,0:T(8,128)(2,1)S(1)}, u32[]{:S(2)}, u32[]{:S(2)}) collective-permute-start(bf16[64,2176]{1,0:T(8,128)(2,1)S(1)} %collective-permute-done.22.refs_0_), channel_id=1, source_target_pairs={{0,1},{1,0},{2,3},{3,2},{4,5},{5,4},{6,7},{7,6},{8,9},{9,8},{10,11... | collective-permute-start | bytes 835592 | tf_op jit(solution)/shard_map/ppermute | solution.py:26
  36.1 8.5 %collective-permute-start.25 = (bf16[64,2176]{1,0:T(8,128)(2,1)S(1)}, bf16[64,2176]{1,0:T(8,128)(2,1)S(1)}, u32[]{:S(2)}, u32[]{:S(2)}) collective-permute-start(bf16[64,2176]{1,0:T(8,128)(2,1)S(1)} %collective-permute-done.23.refs_1_), channel_id=1, source_target_pairs={{0,1},{1,0},{2,3},{3,2},{4,5},{5,4},{6,7},{7,6},{8,9},{9,8},{10,11... | collective-permute-start | bytes 835592 | tf_op jit(solution)/shard_map/ppermute | solution.py:26
  37.6 10.2 %collective-permute-start.1 = (bf16[64,2176]{1,0:T(8,128)(2,1)S(1)}, bf16[64,2176]{1,0:T(8,128)(2,1)S(1)}, u32[]{:S(2)}, u32[]{:S(2)}) collective-permute-start(bf16[64,2176]{1,0:T(8,128)(2,1)S(1)} %collective-permute-done.refs_1_), channel_id=1, source_target_pairs={{0,1},{1,0},{2,3},{3,2},{4,5},{5,4},{6,7},{7,6},{8,9},{9,8},{10,11... | collective-permute-start | bytes 835592 | tf_op jit(solution)/shard_map/ppermute | solution.py:26
  41.4 10.1 %collective-permute-start.16 = (bf16[64,2176]{1,0:T(8,128)(2,1)S(1)}, bf16[64,2176]{1,0:T(8,128)(2,1)S(1)}, u32[]{:S(2)}, u32[]{:S(2)}) collective-permute-start(bf16[64,2176]{1,0:T(8,128)(2,1)S(1)} %constant_dynamic-update-slice_fusion.2.refs_0_), channel_id=1, source_target_pairs={{0,1},{1,0},{2,3},{3,2},{4,5},{5,4},{6,7},{7,6},{8,9},{9,8},{10,11... | collective-permute-start | bytes 835592 | tf_op jit(solution)/shard_map/ppermute | solution.py:26
  44.0 11.3 %collective-permute-start.7 = (bf16[64,2176]{1,0:T(8,128)(2,1)S(1)}, bf16[64,2176]{1,0:T(8,128)(2,1)S(1)}, u32[]{:S(2)}, u32[]{:S(2)}) collective-permute-start(bf16[64,2176]{1,0:T(8,128)(2,1)S(1)} %constant_dynamic-update-slice_fusion.refs_0_), channel_id=1, source_target_pairs={{0,1},{1,0},{2,3},{3,2},{4,5},{5,4},{6,7},{7,6},{8,9},{9,8},{10,11... | collective-permute-start | bytes 835592 | tf_op jit(solution)/shard_map/ppermute | solution.py:26
  44.0 7.6 %collective-permute-start.17 = (bf16[64,2176]{1,0:T(8,128)(2,1)S(1)}, bf16[64,2176]{1,0:T(8,128)(2,1)S(1)}, u32[]{:S(2)}, u32[]{:S(2)}) collective-permute-start(bf16[64,2176]{1,0:T(8,128)(2,1)S(1)} %collective-permute-done.15.refs_1_), channel_id=1, source_target_pairs={{0,1},{1,0},{2,3},{3,2},{4,5},{5,4},{6,7},{7,6},{8,9},{9,8},{10,11... | collective-permute-start | bytes 835592 | tf_op jit(solution)/shard_map/ppermute | solution.py:26
  44.6 10.8 %collective-permute-start.8 = (bf16[64,2176]{1,0:T(8,128)(2,1)S(1)}, bf16[64,2176]{1,0:T(8,128)(2,1)S(1)}, u32[]{:S(2)}, u32[]{:S(2)}) collective-permute-start(bf16[64,2176]{1,0:T(8,128)(2,1)S(1)} %collective-permute-done.6.refs_1_), channel_id=1, source_target_pairs={{0,1},{1,0},{2,3},{3,2},{4,5},{5,4},{6,7},{7,6},{8,9},{9,8},{10,11... | collective-permute-start | bytes 835592 | tf_op jit(solution)/shard_map/ppermute | solution.py:26
  47.8 12.4 %collective-permute-start.26 = (bf16[128,2048]{1,0:T(8,128)(2,1)S(1)}, bf16[128,2048]{1,0:T(8,128)(2,1)S(1)}, u32[]{:S(2)}, u32[]{:S(2)}) collective-permute-start(bf16[128,2048]{1,0:T(8,128)(2,1)S(1)} %get-tuple-element.50), channel_id=1, source_target_pairs={{0,1},{1,0},{2,3},{3,2},{4,5},{5,4},{6,7},{7,6},{8,9},{9,8},{10,11... | collective-permute-start | bytes 1572872 | tf_op jit(solution)/shard_map/ppermute | solution.py:26
  51.5 7.2 %collective-permute-start.2 = (bf16[64,2048]{1,0:T(8,128)(2,1)S(1)}, bf16[64,2048]{1,0:T(8,128)(2,1)S(1)}, u32[]{:S(2)}, u32[]{:S(2)}) collective-permute-start(bf16[64,2048]{1,0:T(8,128)(2,1)S(1)} %get-tuple-element.37), channel_id=1, source_target_pairs={{0,1},{1,0},{2,3},{3,2},{4,5},{5,4},{6,7},{7,6},{8,9},{9,8},{10,11... | collective-permute-start | bytes 786440 | tf_op jit(solution)/shard_map/ppermute | solution.py:26
  54.8 7.7 %collective-permute-start.18 = (bf16[128,2048]{1,0:T(8,128)(2,1)S(1)}, bf16[128,2048]{1,0:T(8,128)(2,1)S(1)}, u32[]{:S(2)}, u32[]{:S(2)}) collective-permute-start(bf16[128,2048]{1,0:T(8,128)(2,1)S(1)} %get-tuple-element.46), channel_id=1, source_target_pairs={{0,1},{1,0},{2,3},{3,2},{4,5},{5,4},{6,7},{7,6},{8,9},{9,8},{10,11... | collective-permute-start | bytes 1572872 | tf_op jit(solution)/shard_map/ppermute | solution.py:26
  58.5 5.7 %collective-permute-start.9 = (bf16[128,2048]{1,0:T(8,128)(2,1)S(1)}, bf16[128,2048]{1,0:T(8,128)(2,1)S(1)}, u32[]{:S(2)}, u32[]{:S(2)}) collective-permute-start(bf16[128,2048]{1,0:T(8,128)(2,1)S(1)} %get-tuple-element.42), channel_id=1, source_target_pairs={{0,1},{1,0},{2,3},{3,2},{4,5},{5,4},{6,7},{7,6},{8,9},{9,8},{10,11... | collective-permute-start | bytes 1572872 | tf_op jit(solution)/shard_map/ppermute | solution.py:26
  58.7 19.6 %collective-permute-start.3 = (bf16[64,2048]{1,0:T(8,128)(2,1)S(1)}, bf16[64,2048]{1,0:T(8,128)(2,1)S(1)}, u32[]{:S(2)}, u32[]{:S(2)}) collective-permute-start(bf16[64,2048]{1,0:T(8,128)(2,1)S(1)} %add_convert_fusion.1), channel_id=1, source_target_pairs={{0,4},{4,0},{8,12},{12,8},{16,20},{20,16},{24,28},{28,24},{1,5},{5... | collective-permute-start | bytes 786440 | tf_op jit(solution)/shard_map/ppermute | solution.py:21
  60.4 19.0 %collective-permute-start.27 = (bf16[64,2048]{1,0:T(8,128)(2,1)S(1)}, bf16[64,2048]{1,0:T(8,128)(2,1)S(1)}, u32[]{:S(2)}, u32[]{:S(2)}) collective-permute-start(bf16[64,2048]{1,0:T(8,128)(2,1)S(1)} %get-tuple-element.56), channel_id=1, source_target_pairs={{0,8},{4,12},{8,0},{12,4},{16,24},{20,28},{24,16},{28,20},{1,9},{5... | collective-permute-start | bytes 786440 | tf_op jit(solution)/shard_map/ppermute | solution.py:21
  60.5 28.0 %collective-permute-start.28 = (bf16[64,2048]{1,0:T(8,128)(2,1)S(1)}, bf16[64,2048]{1,0:T(8,128)(2,1)S(1)}, u32[]{:S(2)}, u32[]{:S(2)}) collective-permute-start(bf16[64,2048]{1,0:T(8,128)(2,1)S(1)} %get-tuple-element.55), channel_id=1, source_target_pairs={{0,12},{4,8},{8,4},{12,0},{16,28},{20,24},{24,20},{28,16},{1,13},{... | collective-permute-start | bytes 786440 | tf_op jit(solution)/shard_map/ppermute | solution.py:21
  62.7 15.5 %collective-permute-start.19 = (bf16[64,2048]{1,0:T(8,128)(2,1)S(1)}, bf16[64,2048]{1,0:T(8,128)(2,1)S(1)}, u32[]{:S(2)}, u32[]{:S(2)}) collective-permute-start(bf16[64,2048]{1,0:T(8,128)(2,1)S(1)} %slice.83), channel_id=1, source_target_pairs={{0,2},{1,3},{2,0},{3,1},{4,6},{5,7},{6,4},{7,5},{8,10},{9,11},{10,... | collective-permute-start | bytes 786440 | tf_op jit(solution)/shard_map/ppermute | solution.py:26
  64.5 8.9 %collective-permute-start.10 = (bf16[32,2048]{1,0:T(8,128)(2,1)S(1)}, bf16[32,2048]{1,0:T(8,128)(2,1)S(1)}, u32[]{:S(2)}, u32[]{:S(2)}) collective-permute-start(bf16[32,2048]{1,0:T(8,128)(2,1)S(1)} %get-tuple-element.59), channel_id=1, source_target_pairs={{0,2},{1,3},{2,0},{3,1},{4,6},{5,7},{6,4},{7,5},{8,10},{9,11},{10,... | collective-permute-start | bytes 393224 | tf_op jit(solution)/shard_map/ppermute | solution.py:26
  73.4 15.1 %collective-permute-start.12 = (bf16[64,2048]{1,0:T(8,128)(2,1)S(1)}, bf16[64,2048]{1,0:T(8,128)(2,1)S(1)}, u32[]{:S(2)}, u32[]{:S(2)}) collective-permute-start(bf16[64,2048]{1,0:T(8,128)(2,1)S(1)} %pad_maximum_fusion), channel_id=1, source_target_pairs={{0,28},{4,24},{8,20},{12,16},{16,12},{20,8},{24,4},{28,0},{1,29},{... | collective-permute-start | bytes 786440 | tf_op jit(solution)/shard_map/ppermute | solution.py:21
  78.2 10.3 %collective-permute-start.11 = (bf16[32,2048]{1,0:T(8,128)(2,1)S(1)}, bf16[32,2048]{1,0:T(8,128)(2,1)S(1)}, u32[]{:S(2)}, u32[]{:S(2)}) collective-permute-start(bf16[32,2048]{1,0:T(8,128)(2,1)S(1)} %fusion.2), channel_id=1, source_target_pairs={{0,24},{4,28},{8,16},{12,20},{16,8},{20,12},{24,0},{28,4},{1,25},{... | collective-permute-start | bytes 393224 | tf_op jit(solution)/shard_map/ppermute | solution.py:21
  78.4 24.4 %collective-permute-start.20 = (bf16[32,2048]{1,0:T(8,128)(2,1)S(1)}, bf16[32,2048]{1,0:T(8,128)(2,1)S(1)}, u32[]{:S(2)}, u32[]{:S(2)}) collective-permute-start(bf16[32,2048]{1,0:T(8,128)(2,1)S(1)} %get-tuple-element.61), channel_id=1, source_target_pairs={{0,16},{4,20},{8,24},{12,28},{16,0},{20,4},{24,8},{28,12},{1,17},{... | collective-permute-start | bytes 393224 | tf_op jit(solution)/shard_map/ppermute | solution.py:21
  79.4 25.7 %collective-permute-start.21 = (bf16[32,2048]{1,0:T(8,128)(2,1)S(1)}, bf16[32,2048]{1,0:T(8,128)(2,1)S(1)}, u32[]{:S(2)}, u32[]{:S(2)}) collective-permute-start(bf16[32,2048]{1,0:T(8,128)(2,1)S(1)} %get-tuple-element.60), channel_id=1, source_target_pairs={{0,20},{4,16},{8,28},{12,24},{16,4},{20,0},{24,12},{28,8},{1,21},{... | collective-permute-start | bytes 393224 | tf_op jit(solution)/shard_map/ppermute | solution.py:21
  106.5 2.0 %collective-permute-start.29 = (bf16[128,2048]{1,0:T(8,128)(2,1)S(1)}, bf16[128,2048]{1,0:T(8,128)(2,1)S(1)}, u32[]{:S(2)}, u32[]{:S(2)}) collective-permute-start(bf16[128,2048]{1,0:T(8,128)(2,1)S(1)} %get-tuple-element.52), channel_id=1, source_target_pairs={{0,1},{1,0},{2,3},{3,2},{4,5},{5,4},{6,7},{7,6},{8,9},{9,8},{10,11... | collective-permute-start | bytes 1572872 | tf_op jit(solution)/shard_map/ppermute | solution.py:26
  108.7 8.4 %collective-permute-start.30 = (bf16[64,2048]{1,0:T(8,128)(2,1)S(1)}, bf16[64,2048]{1,0:T(8,128)(2,1)S(1)}, u32[]{:S(2)}, u32[]{:S(2)}) collective-permute-start(bf16[64,2048]{1,0:T(8,128)(2,1)S(1)} %slice.82), channel_id=1, source_target_pairs={{0,2},{1,3},{2,0},{3,1},{4,6},{5,7},{6,4},{7,5},{8,10},{9,11},{10,... | collective-permute-start | bytes 786440 | tf_op jit(solution)/shard_map/ppermute | solution.py:26
